TPU v7x, 32 devices: a whole 2x2x4 slice. The times are simulated.
32 devices in a mesh: tm: 4 (over y, core), space: 8 (over z, x).
Axes of the slice: x: 2, y: 2, z: 4, core: 2. Of those that a mesh axis runs over, the one named last changes fastest.
Arguments:
- latent: bfloat16 [32, 32, 64, 256], P('tm', 'space'), may hold values from -6 to 6
- spatial_weight: bfloat16 [3, 3, 256, 256], replicated, may hold values from -0.125 to 0.125
- spatial_bias: float32 [256], replicated, may hold values from -3 to 3
- temporal_weight: bfloat16 [3, 256, 256], replicated, may hold values from -0.21875 to 0.21875
- temporal_bias: float32 [256], replicated, may hold values from -3 to 3
Outputs:
- upsampled: bfloat16 [32, 64, 128, 256], P(('tm', 'space'))
All inputs are finite; a program needn't handle non-finite values.
Results may differ from a plain program's by a relative error of at most 0.0032.
Values may be sent and summed in bfloat16 or wider, within the bound.
No kernel may reach another device: no remote copies, remote signals or barrier semaphores. Data moves between devices by JAX's collectives and lax.ppermute only.
A program may use at most 128 MiB of HBM per device.

v0:
```python
import jax
import jax.numpy as jnp
from jax import lax
from jax.sharding import PartitionSpec as P


def padded(cells, sides, width):
    for axis, dim in sides:
        count = lax.axis_size(axis)
        ends = count - 1
        head = lax.slice_in_dim(cells, 0, width, axis=dim)
        tail = lax.slice_in_dim(cells, cells.shape[dim] - width, cells.shape[dim], axis=dim)
        cells = jnp.concatenate(
            [
                lax.ppermute(tail, axis, [(i, (i + 1) % count) for i in range(ends)]),
                cells,
                lax.ppermute(head, axis, [((i + 1) % count, i) for i in range(ends)]),
            ],
            axis=dim,
        )
    return cells


def from_behind(block, axis, distance):
    devices = range(lax.axis_size(axis))
    route = [(i - distance, i) for i in devices if i - distance in devices]
    return lax.ppermute(block, axis, route)


def temporal_mix(earlier, hidden, latent, temporal_weight, temporal_bias):
    count, rows, cols, chans = hidden.shape
    joined = jnp.concatenate([earlier, hidden], axis=0)
    total = jnp.zeros((count * rows * cols, chans), jnp.float32)
    for k in range(3):
        piece = joined[k : k + count].reshape(count * rows * cols, chans)
        total = total + jnp.dot(piece, temporal_weight[k], preferred_element_type=jnp.float32)
    own = latent.reshape(count * rows * cols, chans).astype(jnp.float32)
    return (own + total + temporal_bias).astype(jnp.bfloat16).reshape(count, rows, cols, chans)


def body(latent, spatial_weight, spatial_bias, temporal_weight, temporal_bias):
    frames, rows, cols, chans = latent.shape
    bordered = padded(latent, (("space", 1),), 1)
    bordered = jnp.pad(bordered, ((0, 0), (0, 0), (1, 1), (0, 0)))
    total = jnp.zeros((frames * rows * cols, chans), jnp.float32)
    for a in range(3):
        for b in range(3):
            tile = bordered[:, a : a + rows, b : b + cols, :].reshape(frames * rows * cols, chans)
            total = total + jnp.dot(tile, spatial_weight[a, b], preferred_element_type=jnp.float32)
    hidden = (
        jax.nn.silu(total + spatial_bias).astype(jnp.bfloat16).reshape(frames, rows, cols, chans)
    )
    earlier = from_behind(hidden[frames - 2 :], "tm", 1)
    local_mixed = temporal_mix(earlier, hidden, latent, temporal_weight, temporal_bias)
    mixed = lax.all_to_all(local_mixed, "space", split_axis=0, concat_axis=1, tiled=True)
    count, height, width, depth = mixed.shape
    grown = jnp.broadcast_to(mixed[:, :, None, :, None, :], (count, height, 2, width, 2, depth))
    return grown.reshape(count, 2 * height, 2 * width, depth)


def solution(mesh):
    in_specs = (P("tm", "space", None, None), P(), P(), P(), P())
    out_specs = P(("tm", "space"), None, None, None)
    return jax.shard_map(body, mesh=mesh, in_specs=in_specs, out_specs=out_specs, check_vma=False)
```

profile of v0, /device:TPU:0, one launch (start us, length us, event | category | flops | bytes accessed | tf_op | source)
XLA Modules:
  0.0 76.4 jit_solution(11071638202679942732)
XLA Ops:
  0.0 1.1 %fusion.40 = (bf16[8,1,64,256]{3,2,1,0:T(8,128)(2,1)S(1)}, bf16[8,1,64,256]{3,2,1,0:T(8,128)(2,1)S(1)}) fusion(bf16[8,4,64,256]{3,2,1,0:T(8,128)(2,1)} %param.5), kind=kLoop, calls=%fused_computation.57 | loop fusion | bytes 1048576 | tf_op jit(solution)/shard_map/slice | solution.py:12
  1.1 4.9 %collective-permute-start = (bf16[8,1,64,256]{3,2,1,0:T(8,128)(2,1)S(1)}, bf16[8,1,64,256]{3,2,1,0:T(8,128)(2,1)S(1)}, u32[]{:S(2)}, u32[]{:S(2)}) collective-permute-start(bf16[8,1,64,256]{3,2,1,0:T(8,128)(2,1)S(1)} %get-tuple-element.15), channel_id=1, source_target_pairs={{0,1},{1,2},{2,3},{3,4},{4,5},{5,6},{6,7},{8,9},{9,10},{10,11},{11... | collective-permute-start | bytes 786440 | tf_op jit(solution)/shard_map/ppermute | solution.py:15
  5.9 1.3 %collective-permute-start.1 = (bf16[8,1,64,256]{3,2,1,0:T(8,128)(2,1)S(1)}, bf16[8,1,64,256]{3,2,1,0:T(8,128)(2,1)S(1)}, u32[]{:S(2)}, u32[]{:S(2)}) collective-permute-start(bf16[8,1,64,256]{3,2,1,0:T(8,128)(2,1)S(1)} %get-tuple-element.16), channel_id=1, source_target_pairs={{1,0},{2,1},{3,2},{4,3},{5,4},{6,5},{7,6},{9,8},{10,9},{11,10},{12... | collective-permute-start | bytes 786440 | tf_op jit(solution)/shard_map/ppermute | solution.py:17
  7.2 9.8 %collective-permute-done = bf16[8,1,64,256]{3,2,1,0:T(8,128)(2,1)S(1)} collective-permute-done((bf16[8,1,64,256]{3,2,1,0:T(8,128)(2,1)S(1)}, bf16[8,1,64,256]{3,2,1,0:T(8,128)(2,1)S(1)}, u32[]{:S(2)}, u32[]{:S(2)}) %collective-permute-start) | collective-permute-done | bytes 262176 | tf_op jit(solution)/shard_map/ppermute | solution.py:15
  17.1 0.0 collective-permute-done.1
  17.1 2.1 %fusion.10 = bf16[8,6,66,256]{3,2,1,0:T(8,128)(2,1)S(1)} fusion(bf16[8,1,64,256]{3,2,1,0:T(8,128)(2,1)S(1)} %collective-permute-done.1, bf16[8,4,64,256]{3,2,1,0:T(8,128)(2,1)} %param.5, bf16[8,1,64,256]{3,2,1,0:T(8,128)(2,1)S(1)} %collective-permute-done), kind=kLoop, calls=%fused_computation.22 | loop fusion | flops 9732096 | bytes 3194880 | tf_op jit(solution)/shard_map/concatenate | solution.py:13
  19.2 0.0 copy-start.1
  19.3 1.2 %fusion.39 = (bf16[8,4,64,256]{3,2,1,0:T(8,128)(2,1)S(1)}, bf16[8,4,64,256]{3,2,1,0:T(8,128)(2,1)S(1)}, bf16[8,4,64,256]{3,2,1,0:T(8,128)(2,1)S(1)}, bf16[8,4,64...) fusion(bf16[8,6,66,256]{3,2,1,0:T(8,128)(2,1)S(1)} %fusion.10), kind=kLoop, calls=%fused_computation.56 | loop fusion | bytes 12582912 | tf_op jit(solution)/shard_map/slice | solution.py:48
  20.5 0.0 copy-done.1
  20.5 0.4 fusion.25
  20.9 0.0 copy-start
  21.0 0.4 fusion.16
  21.4 0.8 %copy-done = bf16[8,4,64,256]{3,2,1,0:T(8,128)(2,1)S(1)} copy-done((bf16[8,4,64,256]{3,2,1,0:T(8,128)(2,1)S(1)}, bf16[8,4,64,256]{3,2,1,0:T(8,128)(2,1)}, u32[]{:S(2)}) %copy-start) | copy-done | bytes 1048600
  22.2 0.2 pad_maximum_fusion.1
  22.3 0.4 convolution_add_fusion.8
  22.8 0.4 convolution_add_fusion.7
  23.2 0.4 convolution_add_fusion.6
  23.7 0.4 convolution_add_fusion.5
  24.1 0.4 convolution_add_fusion.4
  24.5 0.0 copy-start.4
  24.5 0.4 convolution_add_fusion.3
  25.0 0.2 copy-done.4
  25.2 0.8 %multiply_convert_fusion = bf16[2048,256]{1,0:T(8,128)(2,1)S(1)} fusion(f32[2048,256]{1,0:T(8,128)S(1)} %fusion.16, f32[2048,256]{1,0:T(8,128)S(1)} %convolution_add_fusion.3, bf16[2048,256]{1,0:T(8,128)(2,1)S(1)} %bitcast.77, f32[256]{0:T(256)S(1)} %copy-done.4, bf16[3,3,256,256]{3,2,1,0:T(8,128)(2,1)S(1)} %copy-done.1), kind=kOutput, calls=%fused_computation.17 | convolution fusion | flops 272629760 | bytes 6423552 | tf_op jit(solution)/shard_map/dot_general | solution.py:49
  26.0 0.0 copy-start.2
  26.1 1.4 %collective-permute-start.2 = (bf16[2,4,64,256]{3,2,1,0:T(8,128)(2,1)S(1)}, bf16[2,4,64,256]{3,2,1,0:T(8,128)(2,1)S(1)}, u32[]{:S(2)}, u32[]{:S(2)}) collective-permute-start(bf16[2,4,64,256]{3,2,1,0:T(8,128)(2,1)S(1)} %bitcast.78), channel_id=1, source_target_pairs={{0,8},{8,16},{16,24},{1,9},{9,17},{17,25},{2,10},{10,18},{18,26},{... | collective-permute-start | bytes 786440 | tf_op jit(solution)/shard_map/ppermute | solution.py:27
  27.5 1.1 %collective-permute-done.2 = bf16[2,4,64,256]{3,2,1,0:T(8,128)(2,1)S(1)} collective-permute-done((bf16[2,4,64,256]{3,2,1,0:T(8,128)(2,1)S(1)}, bf16[2,4,64,256]{3,2,1,0:T(8,128)(2,1)S(1)}, u32[]{:S(2)}, u32[]{:S(2)}) %collective-permute-start.2) | collective-permute-done | bytes 262176 | tf_op jit(solution)/shard_map/ppermute | solution.py:27
  28.7 0.1 fusion.11
  28.8 0.0 copy-done.2
  28.8 0.4 fusion.13
  29.2 0.0 copy-start.3
  29.2 0.5 convolution_add_fusion.1
  29.7 0.2 copy-done.3
  29.9 0.5 fusion.5
  30.4 32.8 %all_to_all.4 = bf16[8,4,64,256]{3,2,1,0:T(8,128)(2,1)S(1)} all-to-all(bf16[8,4,64,256]{3,2,1,0:T(8,128)(2,1)S(1)} %bitcast.76), channel_id=1, replica_groups=mesh['tm'=4,'space'=8] {'space'}, dimensions={0} | all-to-all | bytes 2097152 | tf_op jit(solution)/shard_map/all_to_all | solution.py:55
  63.2 6.0 %broadcast_in_dim.13 = bf16[32,2,64,2,256]{4,3,2,1,0:T(2,128)(2,1)} broadcast(bf16[32,64,256]{2,1,0:T(8,128)(2,1)S(1)} %bitcast.69), dimensions={0,2,4} | broadcast | bytes 5242880 | tf_op jit(solution)/shard_map/broadcast_in_dim | solution.py:57
  69.2 7.2 %broadcast_in_dim.14 = bf16[1,64,128,256]{3,2,1,0:T(8,128)(2,1)} reshape(bf16[32,2,64,2,256]{4,3,2,1,0:T(2,128)(2,1)} %broadcast_in_dim.13) | data formatting | bytes 8388608 | tf_op jit(solution)/shard_map/broadcast_in_dim | solution.py:57
  (1 shorter events, 0.0 us)
Async XLA Ops:
  1.1 16.0 %collective-permute-start = (bf16[8,1,64,256]{3,2,1,0:T(8,128)(2,1)S(1)}, bf16[8,1,64,256]{3,2,1,0:T(8,128)(2,1)S(1)}, u32[]{:S(2)}, u32[]{:S(2)}) collective-permute-start(bf16[8,1,64,256]{3,2,1,0:T(8,128)(2,1)S(1)} %get-tuple-element.15), channel_id=1, source_target_pairs={{0,1},{1,2},{2,3},{3,4},{4,5},{5,6},{6,7},{8,9},{9,10},{10,11},{11... | collective-permute-start | bytes 786440 | tf_op jit(solution)/shard_map/ppermute | solution.py:15
  5.9 11.2 %collective-permute-start.1 = (bf16[8,1,64,256]{3,2,1,0:T(8,128)(2,1)S(1)}, bf16[8,1,64,256]{3,2,1,0:T(8,128)(2,1)S(1)}, u32[]{:S(2)}, u32[]{:S(2)}) collective-permute-start(bf16[8,1,64,256]{3,2,1,0:T(8,128)(2,1)S(1)} %get-tuple-element.16), channel_id=1, source_target_pairs={{1,0},{2,1},{3,2},{4,3},{5,4},{6,5},{7,6},{9,8},{10,9},{11,10},{12... | collective-permute-start | bytes 786440 | tf_op jit(solution)/shard_map/ppermute | solution.py:17
  19.2 1.3 %copy-start.1 = (bf16[3,3,256,256]{3,2,1,0:T(8,128)(2,1)S(1)}, bf16[3,3,256,256]{3,2,1,0:T(8,128)(2,1)}, u32[]{:S(2)}) copy-start(bf16[3,3,256,256]{3,2,1,0:T(8,128)(2,1)} %param.6) | copy-start | bytes 3538948
  20.9 1.2 %copy-start = (bf16[8,4,64,256]{3,2,1,0:T(8,128)(2,1)S(1)}, bf16[8,4,64,256]{3,2,1,0:T(8,128)(2,1)}, u32[]{:S(2)}) copy-start(bf16[8,4,64,256]{3,2,1,0:T(8,128)(2,1)} %param.5) | copy-start | bytes 3145732
  24.5 0.7 copy-start.4
  26.0 2.8 %copy-start.2 = (bf16[3,256,256]{2,1,0:T(8,128)(2,1)S(1)}, bf16[3,256,256]{2,1,0:T(8,128)(2,1)}, u32[]{:S(2)}) copy-start(bf16[3,256,256]{2,1,0:T(8,128)(2,1)} %param.8) | copy-start | bytes 1179652
  26.1 2.6 %collective-permute-start.2 = (bf16[2,4,64,256]{3,2,1,0:T(8,128)(2,1)S(1)}, bf16[2,4,64,256]{3,2,1,0:T(8,128)(2,1)S(1)}, u32[]{:S(2)}, u32[]{:S(2)}) collective-permute-start(bf16[2,4,64,256]{3,2,1,0:T(8,128)(2,1)S(1)} %bitcast.78), channel_id=1, source_target_pairs={{0,8},{8,16},{16,24},{1,9},{9,17},{17,25},{2,10},{10,18},{18,26},{... | collective-permute-start | bytes 786440 | tf_op jit(solution)/shard_map/ppermute | solution.py:27
  29.2 0.7 copy-start.3
where the time goes:
time: 77.9 us; the launch traced here: 76.4 us
  blocking collectives  32.8 us (42%)
  local copies, waits for them, and re-layouts  16.8 us (22%)
  waiting for transfers between devices  11 us (14%)
  starting transfers between devices  7.59 us (10%)
  matrix products  5.67 us (7%)
  other arithmetic  2.43 us (3%)
    all_to_all x1, blocking collectives, body(): lax.all_to_all(local_mixed, 'space', split_axis=0, concat_axis=1, tiled=T...  32.8 us
    broadcast_in_dim x2, local copies, waits for them, and re-layouts, body(): jnp.broadcast_to(mixed[:, :, None, :, None, :], (count, height, 2, width,...  13.2 us
    ppermute x1, waiting for transfers between devices, padded(): lax.ppermute(tail, axis, [(i, (i + 1) % count) for i in range(ends)])  9.85 us
    ppermute x1, starting transfers between devices, padded(): lax.ppermute(tail, axis, [(i, (i + 1) % count) for i in range(ends)])  4.86 us
    dot_general x9, matrix products, body(): jnp.dot(tile, spatial_weight[a, b], preferred_element_type=jnp.float32)  4.28 us
    concatenate x2, other arithmetic, padded(): jnp.concatenate([lax.ppermute(tail, axis, [(i, (i + 1) % count) for i in...  2.3 us
  transfers between devices with their start and end apart: 3, of which 2 were waited for; matrix products, arithmetic and copies ran while one was open for 0% of the time, Pallas kernels for 0%

commit v1 on v0

v1 whole, which is shorter than its diff:
```python
import jax
import jax.numpy as jnp
from jax import lax
from jax.experimental import pallas as pl
from jax.experimental.pallas import tpu as pltpu
from jax.sharding import PartitionSpec as P

VMEM = pl.BlockSpec(memory_space=pltpu.VMEM)
ANY = pl.BlockSpec(memory_space=pl.ANY)
MIB = 1 << 20


def activate(taps, weight_ref, bias):
    frames, cols, chans = taps[0].shape
    wide = jnp.concatenate([t.reshape(frames * cols, chans) for t in taps], axis=1)

    def tap(b):
        w = weight_ref[:, b].reshape(3 * chans, chans)
        return jnp.dot(wide, w, preferred_element_type=jnp.float32).reshape(frames, cols, chans)

    col = lax.broadcasted_iota(jnp.int32, (1, cols, chans), 1)
    left = jnp.where(col == 0, 0.0, pltpu.roll(tap(0), 1, axis=1))
    right = jnp.where(col == cols - 1, 0.0, pltpu.roll(tap(2), cols - 1, axis=1))
    v = tap(1) + left + right + bias
    half = 0.5 * v
    return (half + half * jnp.tanh(half)).astype(jnp.bfloat16)


def mix(hidden, own, weight_ref, bias):
    frames, cols, chans = own.shape
    wide = jnp.concatenate([hidden[k : k + frames].reshape(frames * cols, chans) for k in range(3)], axis=1)
    total = jnp.dot(wide, weight_ref[...].reshape(3 * chans, chans), preferred_element_type=jnp.float32)
    return (own.astype(jnp.float32) + total.reshape(frames, cols, chans) + bias).astype(jnp.bfloat16)


def finish(rows, latent_ref, sw_ref, sb_ref, tw_ref, tb_ref, outs, mixed_ref):
    frames = latent_ref.shape[0]
    inside = lax.axis_index("tm") > 0
    me = lax.axis_index("space")
    for i, (r, taps) in enumerate(rows):
        hidden = activate(taps, sw_ref, sb_ref[...])
        first = lax.broadcasted_iota(jnp.int32, hidden.shape, 0) < 2
        hidden = jnp.where(jnp.logical_and(first, jnp.logical_not(inside)), jnp.zeros_like(hidden), hidden)
        mixed_ref[:, i] = mix(hidden, latent_ref[:, r], tw_ref, tb_ref[...])
    for k in range(frames):
        outs[k][...] = mixed_ref[lax.rem(me + k, frames)]


def inner_kernel(latent_ref, prev_ref, sw_ref, sb_ref, tw_ref, tb_ref, *rest):
    outs, mixed_ref = rest[:-1], rest[-1]
    rows = latent_ref.shape[1]

    def row(r):
        return jnp.concatenate([prev_ref[:, r], latent_ref[:, r]], axis=0)

    jobs = [(r, [row(r - 1), row(r), row(r + 1)]) for r in range(1, rows - 1)]
    finish(jobs, latent_ref, sw_ref, sb_ref, tw_ref, tb_ref, outs, mixed_ref)


def edge_kernel(latent_ref, prev_ref, up_ref, down_ref, prev_up_ref, prev_down_ref, sw_ref, sb_ref, tw_ref, tb_ref, *rest):
    outs, mixed_ref = rest[:-1], rest[-1]
    rows = latent_ref.shape[1]

    def row(r):
        if r < 0:
            return jnp.concatenate([prev_up_ref[:, 0], up_ref[:, 0]], axis=0)
        if r == rows:
            return jnp.concatenate([prev_down_ref[:, 0], down_ref[:, 0]], axis=0)
        return jnp.concatenate([prev_ref[:, r], latent_ref[:, r]], axis=0)

    jobs = [(r, [row(r - 1), row(r), row(r + 1)]) for r in (0, rows - 1)]
    finish(jobs, latent_ref, sw_ref, sb_ref, tw_ref, tb_ref, outs, mixed_ref)


def conv_call(kernel, count, frames, cols, chans, args, name):
    shape = (count, cols, chans)
    rows = count * frames * cols
    return pl.pallas_call(
        kernel,
        out_shape=[jax.ShapeDtypeStruct(shape, jnp.bfloat16)] * frames,
        in_specs=[VMEM] * len(args),
        out_specs=[VMEM] * frames,
        scratch_shapes=[pltpu.VMEM((frames,) + shape, jnp.bfloat16)],
        compiler_params=pltpu.CompilerParams(vmem_limit_bytes=32 * MIB),
        cost_estimate=pl.CostEstimate(flops=2 * rows * 12 * chans * chans, transcendentals=rows * chans, bytes_accessed=4 * MIB),
        name=name,
    )(*args)


def grow_kernel(groups, *refs):
    pieces, out_ref, grown_ref, sems = refs[:-4], refs[-3], refs[-2], refs[-1]
    n = len(pieces)
    count, cols, chans = pieces[0].shape
    tile = out_ref.shape[1] // n
    me = lax.axis_index("space")
    at = lax.broadcasted_iota(jnp.int32, (2 * cols, cols), 0)
    of = lax.broadcasted_iota(jnp.int32, (2 * cols, cols), 1)
    twice = jnp.where(at // 2 == of, 1.0, 0.0).astype(jnp.bfloat16)
    copies = []
    for k in range(n):
        src = lax.rem(me + n - k, n)
        for i in range(count):
            wide = jnp.dot(twice, pieces[k][i], preferred_element_type=jnp.float32).astype(jnp.bfloat16)
            grown_ref[k, 2 * i] = wide
            grown_ref[k, 2 * i + 1] = wide
        done = 0
        for g, (first, rows) in enumerate(groups):
            copy = pltpu.make_async_copy(
                grown_ref.at[k, pl.ds(2 * done, 2 * rows)],
                out_ref.at[0, pl.ds(src * tile + 2 * first, 2 * rows)],
                sems.at[k, g],
            )
            copy.start()
            copies.append(copy)
            done += rows
    for copy in copies:
        copy.wait()


def grow_call(groups, pieces, out, height, name):
    n = len(pieces)
    count, cols, chans = pieces[0].shape
    shape = jax.ShapeDtypeStruct((1, 2 * height, 2 * cols, chans), jnp.bfloat16)
    extra = [] if out is None else [out]

    def kernel(*refs):
        grow_kernel(groups, *refs[:n], None, *refs[n + len(extra) :])

    return pl.pallas_call(
        kernel,
        out_shape=shape,
        in_specs=[VMEM] * n + [ANY] * len(extra),
        out_specs=ANY,
        input_output_aliases={n: 0} if extra else {},
        scratch_shapes=[
            pltpu.VMEM((n, 2 * count, 2 * cols, chans), jnp.bfloat16),
            pltpu.SemaphoreType.DMA((n, len(groups))),
        ],
        compiler_params=pltpu.CompilerParams(vmem_limit_bytes=32 * MIB),
        cost_estimate=pl.CostEstimate(flops=0, transcendentals=0, bytes_accessed=2 * n * count * 4 * cols * chans),
        name=name,
    )(*pieces, *extra)


def shifted(block, axis, distance):
    n = lax.axis_size(axis)
    return lax.ppermute(block, axis, [(i, i + distance) for i in range(n) if 0 <= i + distance < n])


def corner(block, distance):
    ts, ss = lax.axis_size("tm"), lax.axis_size("space")
    route = [(t * ss + s, (t + 1) * ss + s + distance) for t in range(ts - 1) for s in range(ss) if 0 <= s + distance < ss]
    return lax.ppermute(block, ("tm", "space"), route)


def exchange(pieces):
    n = len(pieces)
    return [pieces[0]] + [lax.ppermute(pieces[k], "space", [(i, (i + k) % n) for i in range(n)]) for k in range(1, n)]


def body(latent, spatial_weight, spatial_bias, temporal_weight, temporal_bias):
    frames, rows, cols, chans = latent.shape
    n = lax.axis_size("space")
    params = [spatial_weight, spatial_bias.reshape(1, chans), temporal_weight, temporal_bias.reshape(1, chans)]
    head, tail = latent[:, :1], latent[:, rows - 1 :]
    prev = shifted(latent[frames - 2 :], "tm", 1)
    up = shifted(tail, "space", 1)
    down = shifted(head, "space", -1)
    prev_up = corner(tail[frames - 2 :], 1)
    prev_down = corner(head[frames - 2 :], -1)
    inner = conv_call(inner_kernel, rows - 2, frames, cols, chans, [latent, prev] + params, "inner")
    inner = exchange(inner)
    edge = conv_call(edge_kernel, 2, frames, cols, chans, [latent, prev, up, down, prev_up, prev_down] + params, "edge")
    edge = exchange(edge)
    out = grow_call(((1, rows - 2),), inner, None, rows * n, "grow_inner")
    return grow_call(((0, 1), (rows - 1, 1)), edge, out, rows * n, "grow_edge")


def solution(mesh):
    in_specs = (P("tm", "space", None, None), P(), P(), P(), P())
    out_specs = P(("tm", "space"), None, None, None)
    return jax.shard_map(body, mesh=mesh, in_specs=in_specs, out_specs=out_specs, check_vma=False)
```

time: 77.9 us -> 58.6 us (0.75); the launches traced: 76.4 us -> 58.2 us
  blocking collectives: 32.8 us -> 0 us
  starting transfers between devices: 7.59 us -> 38.5 us
  Pallas kernels: 0 us -> 9.22 us
  local copies, waits for them, and re-layouts: 16.8 us -> 7.87 us
  waiting for transfers between devices: 11 us -> 2.45 us
  matrix products: 5.67 us -> 0 us
  other arithmetic: 2.43 us -> 0 us
    all_to_all x1 -> x0, blocking collectives: 32.8 us -> none  [body(): lax.all_to_all(local_mixed, 'space', split_axis=0, concat_axis=1, tiled=T...]
    ppermute x3 -> x19, starting transfers between devices: 7.59 us -> 38.5 us  [the longest x14 22.4 us: exchange(): lax.ppermute(pieces[k], 'space', [(i, (i + k) % n) for i in range(n)])]
    broadcast_in_dim x2 -> x0, local copies, waits for them, and re-layouts: 13.2 us -> none  [body(): jnp.broadcast_to(mixed[:, :, None, :, None, :], (count, height, 2, width,...]
    pallas_call x0 -> x4, Pallas kernels: none -> 9.22 us  [the longest x2 6.06 us: conv_call(): pl.pallas_call(kernel, out_shape=[jax.ShapeDtypeStruct(shape, jnp.bfloat1...]
    ppermute x3 -> x19, waiting for transfers between devices: 11 us -> 2.45 us  [the longest x14 2.44 us: exchange(): lax.ppermute(pieces[k], 'space', [(i, (i + k) % n) for i in range(n)])]
    dot_general x12 -> x0, matrix products: 5.67 us -> none  [the longest x9 4.28 us: body(): jnp.dot(tile, spatial_weight[a, b], preferred_element_type=jnp.float32)]
    unnamed x10 -> x12, local copies, waits for them, and re-layouts: 1.26 us -> 4.85 us
    concatenate x3 -> x0, other arithmetic: 2.43 us -> none  [the longest x2 2.3 us: padded(): jnp.concatenate([lax.ppermute(tail, axis, [(i, (i + 1) % count) for i in...]
  transfers between devices with their start and end apart: 3 -> 19, of which waited for: 2 -> 3; matrix products, arithmetic and copies ran while one was open for 0% -> 3% of each run, Pallas kernels for 0% -> 13%
where the time goes in v1:
time: 58.6 us; the launch traced here: 58.2 us
  starting transfers between devices  38.5 us (66%)
  Pallas kernels  9.22 us (16%)
  local copies, waits for them, and re-layouts  7.87 us (13%)
  waiting for transfers between devices  2.45 us (4%)
    ppermute x14, starting transfers between devices, exchange(): lax.ppermute(pieces[k], 'space', [(i, (i + k) % n) for i in range(n)])  22.4 us
    ppermute x3, starting transfers between devices, shifted(): lax.ppermute(block, axis, [(i, i + distance) for i in range(n) if 0 <= i...  8.53 us
    ppermute x2, starting transfers between devices, corner(): return lax.ppermute(block, ('tm', 'space'), route)  7.56 us
    pallas_call x2, Pallas kernels, conv_call(): pl.pallas_call(kernel, out_shape=[jax.ShapeDtypeStruct(shape, jnp.bfloat1...  6.06 us
    unnamed x12, local copies, waits for them, and re-layouts  4.85 us
    pallas_call x2, Pallas kernels, grow_call(): pl.pallas_call(kernel, out_shape=shape, in_specs=[VMEM] * n + [ANY] * len...  3.16 us
    ppermute x14, waiting for transfers between devices, exchange(): lax.ppermute(pieces[k], 'space', [(i, (i + k) % n) for i in range(n)])  2.44 us
  transfers between devices with their start and end apart: 19, of which 3 were waited for; matrix products, arithmetic and copies ran while one was open for 3% of the time, Pallas kernels for 13%

profile of v1, /device:TPU:0, one launch (start us, length us, event | category | flops | bytes accessed | tf_op | source)
XLA Modules:
  0.0 58.2 jit_solution(11765324676280879642)
XLA Ops:
  0.0 1.1 %slice.17 = bf16[2,4,64,256]{3,2,1,0:T(8,128)(2,1)S(1)} slice(bf16[8,4,64,256]{3,2,1,0:T(8,128)(2,1)} %latent_ref.3), slice={[6:8], [0:4], [0:64], [0:256]} | slice | bytes 524288 | tf_op jit(solution)/shard_map/slice | solution.py:166
  1.1 2.4 %collective-permute-start = (bf16[2,4,64,256]{3,2,1,0:T(8,128)(2,1)S(1)}, bf16[2,4,64,256]{3,2,1,0:T(8,128)(2,1)S(1)}, u32[]{:S(2)}, u32[]{:S(2)}) collective-permute-start(bf16[2,4,64,256]{3,2,1,0:T(8,128)(2,1)S(1)} %slice.17), channel_id=1, source_target_pairs={{0,8},{8,16},{16,24},{1,9},{9,17},{17,25},{2,10},{10,18},{18,26},{... | collective-permute-start | bytes 786440 | tf_op jit(solution)/shard_map/ppermute | solution.py:147
  3.5 1.1 %fusion.1 = (bf16[8,1,64,256]{3,2,1,0:T(8,128)(2,1)S(1)}, bf16[8,1,64,256]{3,2,1,0:T(8,128)(2,1)S(1)}) fusion(bf16[8,4,64,256]{3,2,1,0:T(8,128)(2,1)} %latent_ref.3), kind=kLoop, calls=%fused_computation.1 | loop fusion | bytes 1048576 | tf_op jit(solution)/shard_map/slice | solution.py:165
  4.5 1.3 %collective-permute-start.2 = (bf16[8,1,64,256]{3,2,1,0:T(8,128)(2,1)S(1)}, bf16[8,1,64,256]{3,2,1,0:T(8,128)(2,1)S(1)}, u32[]{:S(2)}, u32[]{:S(2)}) collective-permute-start(bf16[8,1,64,256]{3,2,1,0:T(8,128)(2,1)S(1)} %get-tuple-element.39), channel_id=1, source_target_pairs={{1,0},{2,1},{3,2},{4,3},{5,4},{6,5},{7,6},{9,8},{10,9},{11,10},{12... | collective-permute-start | bytes 786440 | tf_op jit(solution)/shard_map/ppermute | solution.py:147
  5.8 4.9 %collective-permute-start.1 = (bf16[8,1,64,256]{3,2,1,0:T(8,128)(2,1)S(1)}, bf16[8,1,64,256]{3,2,1,0:T(8,128)(2,1)S(1)}, u32[]{:S(2)}, u32[]{:S(2)}) collective-permute-start(bf16[8,1,64,256]{3,2,1,0:T(8,128)(2,1)S(1)} %get-tuple-element.40), channel_id=1, source_target_pairs={{0,1},{1,2},{2,3},{3,4},{4,5},{5,6},{6,7},{8,9},{9,10},{10,11},{11... | collective-permute-start | bytes 786440 | tf_op jit(solution)/shard_map/ppermute | solution.py:147
  10.7 0.9 %fusion = (bf16[2,1,64,256]{3,2,1,0:T(8,128)(2,1)S(1)}, bf16[2,1,64,256]{3,2,1,0:T(8,128)(2,1)S(1)}) fusion(bf16[8,4,64,256]{3,2,1,0:T(8,128)(2,1)} %latent_ref.3), kind=kLoop, calls=%fused_computation | loop fusion | bytes 262144 | tf_op jit(solution)/shard_map/slice | solution.py:170
  11.6 0.7 %collective-permute-start.4 = (bf16[2,1,64,256]{3,2,1,0:T(8,128)(2,1)S(1)}, bf16[2,1,64,256]{3,2,1,0:T(8,128)(2,1)S(1)}, u32[]{:S(2)}, u32[]{:S(2)}) collective-permute-start(bf16[2,1,64,256]{3,2,1,0:T(8,128)(2,1)S(1)} %get-tuple-element.37), channel_id=1, source_target_pairs={{1,8},{2,9},{3,10},{4,11},{5,12},{6,13},{7,14},{9,16},{10,17},{11,... | collective-permute-start | bytes 196616 | tf_op jit(solution)/shard_map/ppermute | solution.py:153
  12.3 6.9 %collective-permute-start.3 = (bf16[2,1,64,256]{3,2,1,0:T(8,128)(2,1)S(1)}, bf16[2,1,64,256]{3,2,1,0:T(8,128)(2,1)S(1)}, u32[]{:S(2)}, u32[]{:S(2)}) collective-permute-start(bf16[2,1,64,256]{3,2,1,0:T(8,128)(2,1)S(1)} %get-tuple-element.38), channel_id=1, source_target_pairs={{0,9},{1,10},{2,11},{3,12},{4,13},{5,14},{6,15},{8,17},{9,18},{10,... | collective-permute-start | bytes 196616 | tf_op jit(solution)/shard_map/ppermute | solution.py:153
  19.2 0.0 collective-permute-done.prev_ref
  19.2 0.0 copy-start
  19.2 1.2 %copy-done = bf16[8,4,64,256]{3,2,1,0:T(8,128)(2,1)S(1)} copy-done((bf16[8,4,64,256]{3,2,1,0:T(8,128)(2,1)S(1)}, bf16[8,4,64,256]{3,2,1,0:T(8,128)(2,1)}, u32[]{:S(2)}) %copy-start) | copy-done | bytes 1048600
  20.4 1.3 %copy-done.1 = bf16[3,3,256,256]{3,2,1,0:T(8,128)(2,1)S(1)} copy-done((bf16[3,3,256,256]{3,2,1,0:T(8,128)(2,1)S(1)}, bf16[3,3,256,256]{3,2,1,0:T(8,128)(2,1)}, u32[]{:S(2)}) %copy-start.1) | copy-done | bytes 1179672
  21.7 1.0 %copy-done.3 = bf16[3,256,256]{2,1,0:T(8,128)(2,1)S(1)} copy-done((bf16[3,256,256]{2,1,0:T(8,128)(2,1)S(1)}, bf16[3,256,256]{2,1,0:T(8,128)(2,1)}, u32[]{:S(2)}) %copy-start.3) | copy-done | bytes 393240
  22.7 0.7 %copy-done.4 = f32[256]{0:T(256)S(1)} copy-done((f32[256]{0:T(256)S(1)}, f32[256]{0:T(256)}, u32[]{:S(2)}) %copy-start.4) | copy-done | bytes 1048
  23.4 0.7 %copy-done.5 = f32[256]{0:T(256)S(1)} copy-done((f32[256]{0:T(256)S(1)}, f32[256]{0:T(256)}, u32[]{:S(2)}) %copy-start.5) | copy-done | bytes 1048
  24.0 3.0 %inner.1 = (bf16[2,64,256]{2,1,0:T(8,128)(2,1)S(1)}, bf16[2,64,256]{2,1,0:T(8,128)(2,1)S(1)}, bf16[2,64,256]{2,1,0:T(8,128)(2,1)S(1)}, bf16[2,64,256]{2,1,0:T(8,...) custom-call(bf16[8,4,64,256]{3,2,1,0:T(8,128)(2,1)S(1)} %copy-done, ...), custom_call_target="tpu_custom_call" | custom-call | flops 1610612736 | bytes 4194304 | tf_op jit(solution)/shard_map/inner/pallas_call | solution.py:78
  27.1 3.0 %collective-permute-start.12 = (bf16[2,64,256]{2,1,0:T(8,128)(2,1)S(1)}, bf16[2,64,256]{2,1,0:T(8,128)(2,1)S(1)}, u32[]{:S(2)}, u32[]{:S(2)}) collective-permute-start(bf16[2,64,256]{2,1,0:T(8,128)(2,1)S(1)} %get-tuple-element.30), channel_id=1, source_target_pairs={{0,1},{1,2},{2,3},{3,4},{4,5},{5,6},{6,7},{7,0},{8,9},{9,10},{10,1... | collective-permute-start | bytes 196616 | tf_op jit(solution)/shard_map/ppermute | solution.py:158
  30.0 0.0 collective-permute-done.4.prev_down_ref
  30.1 1.6 %collective-permute-start.13 = (bf16[2,64,256]{2,1,0:T(8,128)(2,1)S(1)}, bf16[2,64,256]{2,1,0:T(8,128)(2,1)S(1)}, u32[]{:S(2)}, u32[]{:S(2)}) collective-permute-start(bf16[2,64,256]{2,1,0:T(8,128)(2,1)S(1)} %get-tuple-element.31), channel_id=1, source_target_pairs={{0,2},{1,3},{2,4},{3,5},{4,6},{5,7},{6,0},{7,1},{8,10},{9,11},{10,... | collective-permute-start | bytes 196616 | tf_op jit(solution)/shard_map/ppermute | solution.py:158
  31.6 0.0 collective-permute-done.3.prev_up_ref
  31.6 1.1 %collective-permute-start.14 = (bf16[2,64,256]{2,1,0:T(8,128)(2,1)S(1)}, bf16[2,64,256]{2,1,0:T(8,128)(2,1)S(1)}, u32[]{:S(2)}, u32[]{:S(2)}) collective-permute-start(bf16[2,64,256]{2,1,0:T(8,128)(2,1)S(1)} %get-tuple-element.32), channel_id=1, source_target_pairs={{0,3},{1,4},{2,5},{3,6},{4,7},{5,0},{6,1},{7,2},{8,11},{9,12},{10,... | collective-permute-start | bytes 196616 | tf_op jit(solution)/shard_map/ppermute | solution.py:158
  32.7 0.0 collective-permute-done.2.down_ref
  32.7 1.3 %collective-permute-start.15 = (bf16[2,64,256]{2,1,0:T(8,128)(2,1)S(1)}, bf16[2,64,256]{2,1,0:T(8,128)(2,1)S(1)}, u32[]{:S(2)}, u32[]{:S(2)}) collective-permute-start(bf16[2,64,256]{2,1,0:T(8,128)(2,1)S(1)} %get-tuple-element.33), channel_id=1, source_target_pairs={{0,4},{1,5},{2,6},{3,7},{4,0},{5,1},{6,2},{7,3},{8,12},{9,13},{10,... | collective-permute-start | bytes 196616 | tf_op jit(solution)/shard_map/ppermute | solution.py:158
  34.0 0.0 collective-permute-done.1.up_ref
  34.0 2.5 %collective-permute-start.16 = (bf16[2,64,256]{2,1,0:T(8,128)(2,1)S(1)}, bf16[2,64,256]{2,1,0:T(8,128)(2,1)S(1)}, u32[]{:S(2)}, u32[]{:S(2)}) collective-permute-start(bf16[2,64,256]{2,1,0:T(8,128)(2,1)S(1)} %get-tuple-element.34), channel_id=1, source_target_pairs={{0,5},{1,6},{2,7},{3,0},{4,1},{5,2},{6,3},{7,4},{8,13},{9,14},{10,... | collective-permute-start | bytes 196616 | tf_op jit(solution)/shard_map/ppermute | solution.py:158
  36.5 3.0 %edge.1 = (bf16[2,64,256]{2,1,0:T(8,128)(2,1)S(1)}, bf16[2,64,256]{2,1,0:T(8,128)(2,1)S(1)}, bf16[2,64,256]{2,1,0:T(8,128)(2,1)S(1)}, bf16[2,64,256]{2,1,0:T(8,1...) custom-call(bf16[8,4,64,256]{3,2,1,0:T(8,128)(2,1)S(1)} %copy-done, ...), custom_call_target="tpu_custom_call" | custom-call | flops 1610612736 | bytes 4194304 | tf_op jit(solution)/shard_map/edge/pallas_call | solution.py:78
  39.6 0.0 collective-permute-done.12.refs_1_
  39.6 2.9 %collective-permute-start.17 = (bf16[2,64,256]{2,1,0:T(8,128)(2,1)S(1)}, bf16[2,64,256]{2,1,0:T(8,128)(2,1)S(1)}, u32[]{:S(2)}, u32[]{:S(2)}) collective-permute-start(bf16[2,64,256]{2,1,0:T(8,128)(2,1)S(1)} %get-tuple-element.35), channel_id=1, source_target_pairs={{0,6},{1,7},{2,0},{3,1},{4,2},{5,3},{6,4},{7,5},{8,14},{9,15},{10,... | collective-permute-start | bytes 196616 | tf_op jit(solution)/shard_map/ppermute | solution.py:158
  42.5 0.0 collective-permute-done.13.refs_2_
  42.5 0.0 collective-permute-start.18
  42.5 0.0 collective-permute-done.14.refs_3_
  42.5 2.0 %collective-permute-start.5 = (bf16[2,64,256]{2,1,0:T(8,128)(2,1)S(1)}, bf16[2,64,256]{2,1,0:T(8,128)(2,1)S(1)}, u32[]{:S(2)}, u32[]{:S(2)}) collective-permute-start(bf16[2,64,256]{2,1,0:T(8,128)(2,1)S(1)} %get-tuple-element.22), channel_id=1, source_target_pairs={{0,1},{1,2},{2,3},{3,4},{4,5},{5,6},{6,7},{7,0},{8,9},{9,10},{10,1... | collective-permute-start | bytes 196616 | tf_op jit(solution)/shard_map/ppermute | solution.py:158
  44.6 0.0 collective-permute-done.15.refs_4_
  44.6 0.0 collective-permute-start.6
  44.6 0.0 collective-permute-done.16.refs_5_
  44.6 1.1 %collective-permute-start.7 = (bf16[2,64,256]{2,1,0:T(8,128)(2,1)S(1)}, bf16[2,64,256]{2,1,0:T(8,128)(2,1)S(1)}, u32[]{:S(2)}, u32[]{:S(2)}) collective-permute-start(bf16[2,64,256]{2,1,0:T(8,128)(2,1)S(1)} %get-tuple-element.24), channel_id=1, source_target_pairs={{0,3},{1,4},{2,5},{3,6},{4,7},{5,0},{6,1},{7,2},{8,11},{9,12},{10,... | collective-permute-start | bytes 196616 | tf_op jit(solution)/shard_map/ppermute | solution.py:158
  45.7 2.8 %collective-permute-start.8 = (bf16[2,64,256]{2,1,0:T(8,128)(2,1)S(1)}, bf16[2,64,256]{2,1,0:T(8,128)(2,1)S(1)}, u32[]{:S(2)}, u32[]{:S(2)}) collective-permute-start(bf16[2,64,256]{2,1,0:T(8,128)(2,1)S(1)} %get-tuple-element.25), channel_id=1, source_target_pairs={{0,4},{1,5},{2,6},{3,7},{4,0},{5,1},{6,2},{7,3},{8,12},{9,13},{10,... | collective-permute-start | bytes 196616 | tf_op jit(solution)/shard_map/ppermute | solution.py:158
  48.5 0.0 collective-permute-done.18.refs_7_
  48.5 0.9 %collective-permute-start.9 = (bf16[2,64,256]{2,1,0:T(8,128)(2,1)S(1)}, bf16[2,64,256]{2,1,0:T(8,128)(2,1)S(1)}, u32[]{:S(2)}, u32[]{:S(2)}) collective-permute-start(bf16[2,64,256]{2,1,0:T(8,128)(2,1)S(1)} %get-tuple-element.26), channel_id=1, source_target_pairs={{0,5},{1,6},{2,7},{3,0},{4,1},{5,2},{6,3},{7,4},{8,13},{9,14},{10,... | collective-permute-start | bytes 196616 | tf_op jit(solution)/shard_map/ppermute | solution.py:158
  49.4 0.9 %collective-permute-done.5.refs_1_ = bf16[2,64,256]{2,1,0:T(8,128)(2,1)S(1)} collective-permute-done((bf16[2,64,256]{2,1,0:T(8,128)(2,1)S(1)}, bf16[2,64,256]{2,1,0:T(8,128)(2,1)S(1)}, u32[]{:S(2)}, u32[]{:S(2)}) %collective-permute-start.5) | collective-permute-done | bytes 65568 | tf_op jit(solution)/shard_map/ppermute | solution.py:158
  50.3 1.9 %collective-permute-start.10 = (bf16[2,64,256]{2,1,0:T(8,128)(2,1)S(1)}, bf16[2,64,256]{2,1,0:T(8,128)(2,1)S(1)}, u32[]{:S(2)}, u32[]{:S(2)}) collective-permute-start(bf16[2,64,256]{2,1,0:T(8,128)(2,1)S(1)} %get-tuple-element.27), channel_id=1, source_target_pairs={{0,6},{1,7},{2,0},{3,1},{4,2},{5,3},{6,4},{7,5},{8,14},{9,15},{10,... | collective-permute-start | bytes 196616 | tf_op jit(solution)/shard_map/ppermute | solution.py:158
  52.3 0.0 collective-permute-done.6.refs_2_
  52.3 1.2 %collective-permute-start.11 = (bf16[2,64,256]{2,1,0:T(8,128)(2,1)S(1)}, bf16[2,64,256]{2,1,0:T(8,128)(2,1)S(1)}, u32[]{:S(2)}, u32[]{:S(2)}) collective-permute-start(bf16[2,64,256]{2,1,0:T(8,128)(2,1)S(1)} %get-tuple-element.28), channel_id=1, source_target_pairs={{0,7},{1,0},{2,1},{3,2},{4,3},{5,4},{6,5},{7,6},{8,15},{9,8},{10,9... | collective-permute-start | bytes 196616 | tf_op jit(solution)/shard_map/ppermute | solution.py:158
  53.5 1.5 %grow_inner.1.refs_8_ = bf16[1,64,128,256]{3,2,1,0:T(8,128)(2,1)} custom-call(bf16[2,64,256]{2,1,0:T(8,128)(2,1)S(1)} %get-tuple-element.29.refs_0_, bf16[2,64,256]{2,1,0:T(8,128)(2,1)S(1)} %collective-permute-done.12.refs_1_, bf16[2,64,256]{2,1,0:T(8,128)(2,1)S(1)} %collective-permute-done.13.refs_2_, ...), custom_call_target="tpu_custom_call" | custom-call | bytes 2097152 | tf_op jit(solution)/shard_map/grow_inner/pallas_call | solution.py:129
  55.1 0.0 collective-permute-done.9.refs_5_
  55.1 0.2 collective-permute-done.10.refs_6_
  55.2 1.3 %collective-permute-done.11.refs_7_ = bf16[2,64,256]{2,1,0:T(8,128)(2,1)S(1)} collective-permute-done((bf16[2,64,256]{2,1,0:T(8,128)(2,1)S(1)}, bf16[2,64,256]{2,1,0:T(8,128)(2,1)S(1)}, u32[]{:S(2)}, u32[]{:S(2)}) %collective-permute-start.11) | collective-permute-done | bytes 65568 | tf_op jit(solution)/shard_map/ppermute | solution.py:158
  56.5 1.6 %grow_edge.1 = bf16[1,64,128,256]{3,2,1,0:T(8,128)(2,1)} custom-call(bf16[2,64,256]{2,1,0:T(8,128)(2,1)S(1)} %get-tuple-element.21.refs_0_, bf16[2,64,256]{2,1,0:T(8,128)(2,1)S(1)} %collective-permute-done.5.refs_1_, bf16[2,64,256]{2,1,0:T(8,128)(2,1)S(1)} %collective-permute-done.6.refs_2_, ...), custom_call_target="tpu_custom_call", output_to_operand_aliasing={{}: (8, {})} | custom-call | bytes 2097152 | tf_op jit(solution)/shard_map/grow_edge/pallas_call | solution.py:129
  (9 shorter events, 0.0 us)
Async XLA Ops:
  0.0 36.5 %copy-start.2 = (bf16[3,3,256,256]{3,2,1,0:T(8,128)(2,1)S(1)}, bf16[3,3,256,256]{3,2,1,0:T(8,128)(2,1)}, u32[]{:S(2)}) copy-start(bf16[3,3,256,256]{3,2,1,0:T(8,128)(2,1)} %sw_ref.3) | copy-start | bytes 3538948
  1.1 18.1 %collective-permute-start = (bf16[2,4,64,256]{3,2,1,0:T(8,128)(2,1)S(1)}, bf16[2,4,64,256]{3,2,1,0:T(8,128)(2,1)S(1)}, u32[]{:S(2)}, u32[]{:S(2)}) collective-permute-start(bf16[2,4,64,256]{3,2,1,0:T(8,128)(2,1)S(1)} %slice.17), channel_id=1, source_target_pairs={{0,8},{8,16},{16,24},{1,9},{9,17},{17,25},{2,10},{10,18},{18,26},{... | collective-permute-start | bytes 786440 | tf_op jit(solution)/shard_map/ppermute | solution.py:147
  4.5 28.2 %collective-permute-start.2 = (bf16[8,1,64,256]{3,2,1,0:T(8,128)(2,1)S(1)}, bf16[8,1,64,256]{3,2,1,0:T(8,128)(2,1)S(1)}, u32[]{:S(2)}, u32[]{:S(2)}) collective-permute-start(bf16[8,1,64,256]{3,2,1,0:T(8,128)(2,1)S(1)} %get-tuple-element.39), channel_id=1, source_target_pairs={{1,0},{2,1},{3,2},{4,3},{5,4},{6,5},{7,6},{9,8},{10,9},{11,10},{12... | collective-permute-start | bytes 786440 | tf_op jit(solution)/shard_map/ppermute | solution.py:147
  5.8 28.2 %collective-permute-start.1 = (bf16[8,1,64,256]{3,2,1,0:T(8,128)(2,1)S(1)}, bf16[8,1,64,256]{3,2,1,0:T(8,128)(2,1)S(1)}, u32[]{:S(2)}, u32[]{:S(2)}) collective-permute-start(bf16[8,1,64,256]{3,2,1,0:T(8,128)(2,1)S(1)} %get-tuple-element.40), channel_id=1, source_target_pairs={{0,1},{1,2},{2,3},{3,4},{4,5},{5,6},{6,7},{8,9},{9,10},{10,11},{11... | collective-permute-start | bytes 786440 | tf_op jit(solution)/shard_map/ppermute | solution.py:147
  11.6 18.5 %collective-permute-start.4 = (bf16[2,1,64,256]{3,2,1,0:T(8,128)(2,1)S(1)}, bf16[2,1,64,256]{3,2,1,0:T(8,128)(2,1)S(1)}, u32[]{:S(2)}, u32[]{:S(2)}) collective-permute-start(bf16[2,1,64,256]{3,2,1,0:T(8,128)(2,1)S(1)} %get-tuple-element.37), channel_id=1, source_target_pairs={{1,8},{2,9},{3,10},{4,11},{5,12},{6,13},{7,14},{9,16},{10,17},{11,... | collective-permute-start | bytes 196616 | tf_op jit(solution)/shard_map/ppermute | solution.py:153
  12.3 19.4 %collective-permute-start.3 = (bf16[2,1,64,256]{3,2,1,0:T(8,128)(2,1)S(1)}, bf16[2,1,64,256]{3,2,1,0:T(8,128)(2,1)S(1)}, u32[]{:S(2)}, u32[]{:S(2)}) collective-permute-start(bf16[2,1,64,256]{3,2,1,0:T(8,128)(2,1)S(1)} %get-tuple-element.38), channel_id=1, source_target_pairs={{0,9},{1,10},{2,11},{3,12},{4,13},{5,14},{6,15},{8,17},{9,18},{10,... | collective-permute-start | bytes 196616 | tf_op jit(solution)/shard_map/ppermute | solution.py:153
  19.2 1.2 %copy-start = (bf16[8,4,64,256]{3,2,1,0:T(8,128)(2,1)S(1)}, bf16[8,4,64,256]{3,2,1,0:T(8,128)(2,1)}, u32[]{:S(2)}) copy-start(bf16[8,4,64,256]{3,2,1,0:T(8,128)(2,1)} %latent_ref.3) | copy-start | bytes 3145732
  20.4 1.3 %copy-start.1 = (bf16[3,3,256,256]{3,2,1,0:T(8,128)(2,1)S(1)}, bf16[3,3,256,256]{3,2,1,0:T(8,128)(2,1)}, u32[]{:S(2)}) copy-start(bf16[3,3,256,256]{3,2,1,0:T(8,128)(2,1)} %sw_ref.3) | copy-start | bytes 3538948
  21.7 1.0 %copy-start.3 = (bf16[3,256,256]{2,1,0:T(8,128)(2,1)S(1)}, bf16[3,256,256]{2,1,0:T(8,128)(2,1)}, u32[]{:S(2)}) copy-start(bf16[3,256,256]{2,1,0:T(8,128)(2,1)} %tw_ref.3) | copy-start | bytes 1179652
  22.7 0.7 %copy-start.4 = (f32[256]{0:T(256)S(1)}, f32[256]{0:T(256)}, u32[]{:S(2)}) copy-start(f32[256]{0:T(256)} %param.7) | copy-start | bytes 3076
  23.4 0.7 %copy-start.5 = (f32[256]{0:T(256)S(1)}, f32[256]{0:T(256)}, u32[]{:S(2)}) copy-start(f32[256]{0:T(256)} %param.9) | copy-start | bytes 3076
  27.1 12.5 %collective-permute-start.12 = (bf16[2,64,256]{2,1,0:T(8,128)(2,1)S(1)}, bf16[2,64,256]{2,1,0:T(8,128)(2,1)S(1)}, u32[]{:S(2)}, u32[]{:S(2)}) collective-permute-start(bf16[2,64,256]{2,1,0:T(8,128)(2,1)S(1)} %get-tuple-element.30), channel_id=1, source_target_pairs={{0,1},{1,2},{2,3},{3,4},{4,5},{5,6},{6,7},{7,0},{8,9},{9,10},{10,1... | collective-permute-start | bytes 196616 | tf_op jit(solution)/shard_map/ppermute | solution.py:158
  30.1 12.5 %collective-permute-start.13 = (bf16[2,64,256]{2,1,0:T(8,128)(2,1)S(1)}, bf16[2,64,256]{2,1,0:T(8,128)(2,1)S(1)}, u32[]{:S(2)}, u32[]{:S(2)}) collective-permute-start(bf16[2,64,256]{2,1,0:T(8,128)(2,1)S(1)} %get-tuple-element.31), channel_id=1, source_target_pairs={{0,2},{1,3},{2,4},{3,5},{4,6},{5,7},{6,0},{7,1},{8,10},{9,11},{10,... | collective-permute-start | bytes 196616 | tf_op jit(solution)/shard_map/ppermute | solution.py:158
  31.6 10.9 %collective-permute-start.14 = (bf16[2,64,256]{2,1,0:T(8,128)(2,1)S(1)}, bf16[2,64,256]{2,1,0:T(8,128)(2,1)S(1)}, u32[]{:S(2)}, u32[]{:S(2)}) collective-permute-start(bf16[2,64,256]{2,1,0:T(8,128)(2,1)S(1)} %get-tuple-element.32), channel_id=1, source_target_pairs={{0,3},{1,4},{2,5},{3,6},{4,7},{5,0},{6,1},{7,2},{8,11},{9,12},{10,... | collective-permute-start | bytes 196616 | tf_op jit(solution)/shard_map/ppermute | solution.py:158
  32.7 11.8 %collective-permute-start.15 = (bf16[2,64,256]{2,1,0:T(8,128)(2,1)S(1)}, bf16[2,64,256]{2,1,0:T(8,128)(2,1)S(1)}, u32[]{:S(2)}, u32[]{:S(2)}) collective-permute-start(bf16[2,64,256]{2,1,0:T(8,128)(2,1)S(1)} %get-tuple-element.33), channel_id=1, source_target_pairs={{0,4},{1,5},{2,6},{3,7},{4,0},{5,1},{6,2},{7,3},{8,12},{9,13},{10,... | collective-permute-start | bytes 196616 | tf_op jit(solution)/shard_map/ppermute | solution.py:158
  34.0 10.6 %collective-permute-start.16 = (bf16[2,64,256]{2,1,0:T(8,128)(2,1)S(1)}, bf16[2,64,256]{2,1,0:T(8,128)(2,1)S(1)}, u32[]{:S(2)}, u32[]{:S(2)}) collective-permute-start(bf16[2,64,256]{2,1,0:T(8,128)(2,1)S(1)} %get-tuple-element.34), channel_id=1, source_target_pairs={{0,5},{1,6},{2,7},{3,0},{4,1},{5,2},{6,3},{7,4},{8,13},{9,14},{10,... | collective-permute-start | bytes 196616 | tf_op jit(solution)/shard_map/ppermute | solution.py:158
  39.6 6.1 %collective-permute-start.17 = (bf16[2,64,256]{2,1,0:T(8,128)(2,1)S(1)}, bf16[2,64,256]{2,1,0:T(8,128)(2,1)S(1)}, u32[]{:S(2)}, u32[]{:S(2)}) collective-permute-start(bf16[2,64,256]{2,1,0:T(8,128)(2,1)S(1)} %get-tuple-element.35), channel_id=1, source_target_pairs={{0,6},{1,7},{2,0},{3,1},{4,2},{5,3},{6,4},{7,5},{8,14},{9,15},{10,... | collective-permute-start | bytes 196616 | tf_op jit(solution)/shard_map/ppermute | solution.py:158
  42.5 5.9 %collective-permute-start.18 = (bf16[2,64,256]{2,1,0:T(8,128)(2,1)S(1)}, bf16[2,64,256]{2,1,0:T(8,128)(2,1)S(1)}, u32[]{:S(2)}, u32[]{:S(2)}) collective-permute-start(bf16[2,64,256]{2,1,0:T(8,128)(2,1)S(1)} %get-tuple-element.36), channel_id=1, source_target_pairs={{0,7},{1,0},{2,1},{3,2},{4,3},{5,4},{6,5},{7,6},{8,15},{9,8},{10,9... | collective-permute-start | bytes 196616 | tf_op jit(solution)/shard_map/ppermute | solution.py:158
  42.5 7.8 %collective-permute-start.5 = (bf16[2,64,256]{2,1,0:T(8,128)(2,1)S(1)}, bf16[2,64,256]{2,1,0:T(8,128)(2,1)S(1)}, u32[]{:S(2)}, u32[]{:S(2)}) collective-permute-start(bf16[2,64,256]{2,1,0:T(8,128)(2,1)S(1)} %get-tuple-element.22), channel_id=1, source_target_pairs={{0,1},{1,2},{2,3},{3,4},{4,5},{5,6},{6,7},{7,0},{8,9},{9,10},{10,1... | collective-permute-start | bytes 196616 | tf_op jit(solution)/shard_map/ppermute | solution.py:158
  44.6 7.7 %collective-permute-start.6 = (bf16[2,64,256]{2,1,0:T(8,128)(2,1)S(1)}, bf16[2,64,256]{2,1,0:T(8,128)(2,1)S(1)}, u32[]{:S(2)}, u32[]{:S(2)}) collective-permute-start(bf16[2,64,256]{2,1,0:T(8,128)(2,1)S(1)} %get-tuple-element.23), channel_id=1, source_target_pairs={{0,2},{1,3},{2,4},{3,5},{4,6},{5,7},{6,0},{7,1},{8,10},{9,11},{10,... | collective-permute-start | bytes 196616 | tf_op jit(solution)/shard_map/ppermute | solution.py:158
  44.6 10.5 %collective-permute-start.7 = (bf16[2,64,256]{2,1,0:T(8,128)(2,1)S(1)}, bf16[2,64,256]{2,1,0:T(8,128)(2,1)S(1)}, u32[]{:S(2)}, u32[]{:S(2)}) collective-permute-start(bf16[2,64,256]{2,1,0:T(8,128)(2,1)S(1)} %get-tuple-element.24), channel_id=1, source_target_pairs={{0,3},{1,4},{2,5},{3,6},{4,7},{5,0},{6,1},{7,2},{8,11},{9,12},{10,... | collective-permute-start | bytes 196616 | tf_op jit(solution)/shard_map/ppermute | solution.py:158
  45.7 9.4 %collective-permute-start.8 = (bf16[2,64,256]{2,1,0:T(8,128)(2,1)S(1)}, bf16[2,64,256]{2,1,0:T(8,128)(2,1)S(1)}, u32[]{:S(2)}, u32[]{:S(2)}) collective-permute-start(bf16[2,64,256]{2,1,0:T(8,128)(2,1)S(1)} %get-tuple-element.25), channel_id=1, source_target_pairs={{0,4},{1,5},{2,6},{3,7},{4,0},{5,1},{6,2},{7,3},{8,12},{9,13},{10,... | collective-permute-start | bytes 196616 | tf_op jit(solution)/shard_map/ppermute | solution.py:158
  48.5 6.6 %collective-permute-start.9 = (bf16[2,64,256]{2,1,0:T(8,128)(2,1)S(1)}, bf16[2,64,256]{2,1,0:T(8,128)(2,1)S(1)}, u32[]{:S(2)}, u32[]{:S(2)}) collective-permute-start(bf16[2,64,256]{2,1,0:T(8,128)(2,1)S(1)} %get-tuple-element.26), channel_id=1, source_target_pairs={{0,5},{1,6},{2,7},{3,0},{4,1},{5,2},{6,3},{7,4},{8,13},{9,14},{10,... | collective-permute-start | bytes 196616 | tf_op jit(solution)/shard_map/ppermute | solution.py:158
  50.3 4.9 %collective-permute-start.10 = (bf16[2,64,256]{2,1,0:T(8,128)(2,1)S(1)}, bf16[2,64,256]{2,1,0:T(8,128)(2,1)S(1)}, u32[]{:S(2)}, u32[]{:S(2)}) collective-permute-start(bf16[2,64,256]{2,1,0:T(8,128)(2,1)S(1)} %get-tuple-element.27), channel_id=1, source_target_pairs={{0,6},{1,7},{2,0},{3,1},{4,2},{5,3},{6,4},{7,5},{8,14},{9,15},{10,... | collective-permute-start | bytes 196616 | tf_op jit(solution)/shard_map/ppermute | solution.py:158
  52.3 4.3 %collective-permute-start.11 = (bf16[2,64,256]{2,1,0:T(8,128)(2,1)S(1)}, bf16[2,64,256]{2,1,0:T(8,128)(2,1)S(1)}, u32[]{:S(2)}, u32[]{:S(2)}) collective-permute-start(bf16[2,64,256]{2,1,0:T(8,128)(2,1)S(1)} %get-tuple-element.28), channel_id=1, source_target_pairs={{0,7},{1,0},{2,1},{3,2},{4,3},{5,4},{6,5},{7,6},{8,15},{9,8},{10,9... | collective-permute-start | bytes 196616 | tf_op jit(solution)/shard_map/ppermute | solution.py:158

commit v2 on v0

v2 whole, which is shorter than its diff:
```python
import jax
import jax.numpy as jnp
from jax import lax
from jax.experimental import pallas as pl
from jax.experimental.pallas import tpu as pltpu
from jax.sharding import PartitionSpec as P

VMEM = pl.BlockSpec(memory_space=pltpu.VMEM)
HBM = pl.BlockSpec(memory_space=pltpu.HBM)
BF16 = jnp.bfloat16
MIB = 1 << 20
PARAMS = pltpu.CompilerParams(vmem_limit_bytes=24 * MIB)


def bf16(*shape):
    return jax.ShapeDtypeStruct(shape, BF16)


def exchanges(n):
    far = sorted(range(n // 2, n), key=lambda k: (k & 1, k))
    cut = 3 * n // 8
    return far[:cut], far[cut:] + sorted(range(1, n // 2), key=lambda k: -k)


def copy_all(pairs, sems):
    copies = [pltpu.make_async_copy(a, b, sems.at[i]) for i, (a, b) in enumerate(pairs)]
    for copy in copies:
        copy.start()
    for copy in copies:
        copy.wait()


def border_kernel(latent, near, far, last, sems):
    frames, rows = latent.shape[:2]
    odd = lax.rem(lax.axis_index("space"), 2)
    near_row, far_row = (rows - 1) * (1 - odd), (rows - 1) * odd
    pairs = [(latent.at[:, near_row], near), (latent.at[:, far_row], far), (latent.at[pl.ds(frames - 2, 2)], last)]
    copy_all(pairs, sems)


def load_kernel(*refs):
    m = len(refs) // 2
    copy_all(list(zip(refs[:m], refs[m : 2 * m])), refs[-1])


def activate(taps, order, weight_ref, bias):
    frames, cols, chans = taps[0].shape
    wide = jnp.concatenate([t.reshape(frames * cols, chans) for t in taps], axis=1)

    def tap(b):
        w = jnp.concatenate([weight_ref[a, b] for a in order], axis=0)
        return jnp.dot(wide, w, preferred_element_type=jnp.float32).reshape(frames, cols, chans)

    col = lax.broadcasted_iota(jnp.int32, (1, cols, chans), 1)
    left = jnp.where(col == 0, 0.0, pltpu.roll(tap(0), 1, axis=1))
    right = jnp.where(col == cols - 1, 0.0, pltpu.roll(tap(2), cols - 1, axis=1))
    half = 0.5 * (tap(1) + left + right + bias)
    return (half + half * jnp.tanh(half)).astype(BF16)


def mix(before, hidden, own, weight_ref, bias):
    frames, cols, chans = own.shape
    before = jnp.where(lax.axis_index("tm") > 0, before, jnp.zeros_like(before))
    joined = jnp.concatenate([before, hidden], axis=0)
    wide = jnp.concatenate([joined[k : k + frames].reshape(frames * cols, chans) for k in range(3)], axis=1)
    total = jnp.dot(wide, weight_ref[...].reshape(3 * chans, chans), preferred_element_type=jnp.float32)
    return (own.astype(jnp.float32) + total.reshape(frames, cols, chans) + bias).astype(BF16)


def inner_kernel(early, latent, prev, sw, sb, tw, tb, mixed, *outs):
    rows = latent.shape[1]
    me = lax.axis_index("space")

    def row(r):
        return jnp.concatenate([prev[:, r], latent[:, r]], axis=0)

    for r in range(1, rows - 1):
        hidden = activate([row(r - 1), row(r), row(r + 1)], (0, 1, 2), sw, sb[...])
        mixed[:, r - 1] = mix(hidden[:2], hidden[2:], latent[:, r], tw, tb[...])
    for k, out in zip(early, outs):
        out[...] = mixed[lax.bitwise_xor(me, k)]


def sides(rows):
    odd = lax.rem(lax.axis_index("space"), 2)
    for top in (odd, 1 - odd):
        yield (rows - 1) * (1 - top), 1 + (rows - 3) * (1 - top), 1 - top, (2 - 2 * top, 1, 2 * top)


def outside(i, halo):
    if i == 0:
        return halo
    me = lax.axis_index("space")
    inside = jnp.logical_and(me > 0, me < lax.axis_size("space") - 1)
    return jnp.where(inside, halo, jnp.zeros_like(halo))


def edge_kernel(latent, near, far, sw, sb, hidden):
    for i, (halo, (r, beyond, _, order)) in enumerate(zip((near, far), sides(latent.shape[1]))):
        hidden[i] = activate([outside(i, halo[...]), latent[:, r], latent[:, beyond]], order, sw, sb[...])


def join_kernel(early, whole, latent, prev, corners, hidden, inner, sw, sb, tw, tb, *rest):
    outs, mixed = rest[:-1], rest[-1]
    rows = latent.shape[1]
    me = lax.axis_index("space")
    for i, (r, beyond, place, order) in enumerate(sides(rows)):
        before = activate([outside(i, corners[i]), prev[:, r], prev[:, beyond]], order, sw, sb[...])
        mixed[:, place] = mix(before, hidden[i], latent[:, r], tw, tb[...])
    for k, out in zip(early, outs):
        out[...] = mixed[lax.bitwise_xor(me, k)]
    for k, out in zip(whole, outs[len(early) :]):
        frame = lax.bitwise_xor(me, k)
        out[0] = mixed[frame, 0]
        out[pl.ds(1, rows - 2)] = inner[frame]
        out[rows - 1] = mixed[frame, 1]


def grow_kernel(plan, pieces, out, grown, sems):
    tile = out.shape[1] // lax.axis_size("space")
    cols = out.shape[2] // 2
    me = lax.axis_index("space")
    at = lax.broadcasted_iota(jnp.int32, (2 * cols, cols), 0)
    of = lax.broadcasted_iota(jnp.int32, (2 * cols, cols), 1)
    twice = jnp.where(at // 2 == of, 1.0, 0.0).astype(BF16)
    copies, used = [], 0
    for (k, runs), piece in zip(plan, pieces):
        base, src = used, lax.bitwise_xor(me, k)
        for i in range(piece.shape[0]):
            wide = jnp.dot(twice, piece[i], preferred_element_type=jnp.float32).astype(BF16)
            grown[used] = wide
            grown[used + 1] = wide
            used += 2
        for first, rows in runs:
            copy = pltpu.make_async_copy(
                grown.at[pl.ds(base, 2 * rows)], out.at[0, pl.ds(src * tile + 2 * first, 2 * rows)], sems.at[len(copies)]
            )
            copy.start()
            copies.append(copy)
            base += 2 * rows
    for copy in copies:
        copy.wait()


def grow(plan, pieces, out, height, name):
    cols, chans = pieces[0].shape[1:]
    count = sum(p.shape[0] for p in pieces)
    extra = [] if out is None else [out]
    m = len(pieces)
    return pl.pallas_call(
        lambda *refs: grow_kernel(plan, refs[:m], *refs[m + len(extra) :]),
        out_shape=bf16(1, 2 * height, 2 * cols, chans),
        in_specs=[VMEM] * m + [HBM] * len(extra),
        out_specs=HBM,
        input_output_aliases={m: 0} if extra else {},
        scratch_shapes=[
            pltpu.VMEM((2 * count, 2 * cols, chans), BF16),
            pltpu.SemaphoreType.DMA((sum(len(runs) for _, runs in plan),)),
        ],
        compiler_params=PARAMS,
        cost_estimate=pl.CostEstimate(flops=0, transcendentals=0, bytes_accessed=8 * count * cols * chans),
        name=name,
    )(*pieces, *extra)


def cost(rows, taps, chans):
    return pl.CostEstimate(flops=2 * taps * rows * chans * chans, transcendentals=rows * chans, bytes_accessed=2 * MIB)


def swap(block, k):
    return lax.ppermute(block, "space", [(i, i ^ k) for i in range(lax.axis_size("space"))])


def ahead(block):
    n = lax.axis_size("tm")
    return lax.ppermute(block, "tm", [(t, (t + 1) % n) for t in range(n)])


def beside(block):
    n = lax.axis_size("space")
    route = [(s, (s + 1 if s % 2 else s - 1) % n) for s in range(n)]
    return lax.ppermute(block, "space", route)


def body(latent, spatial_weight, spatial_bias, temporal_weight, temporal_bias):
    frames, rows, cols, chans = latent.shape
    n = lax.axis_size("space")
    if n & (n - 1) or frames != n:
        raise ValueError("shape")
    early, whole = exchanges(n)

    args = [latent, spatial_weight, spatial_bias.reshape(1, chans), temporal_weight, temporal_bias.reshape(1, chans)]
    args = [pltpu.with_memory_space_constraint(a, pltpu.HBM) for a in args]
    near, far, last = pl.pallas_call(
        border_kernel,
        out_shape=[bf16(frames, cols, chans), bf16(frames, cols, chans), bf16(2, rows, cols, chans)],
        in_specs=[HBM],
        out_specs=[VMEM] * 3,
        scratch_shapes=[pltpu.SemaphoreType.DMA((3,))],
        compiler_params=PARAMS,
        name="border",
    )(args[0])
    near = swap(near, 1)
    far = beside(far)
    prev = ahead(last)
    latent, *params = pl.pallas_call(
        load_kernel,
        out_shape=[jax.ShapeDtypeStruct(a.shape, a.dtype) for a in args],
        in_specs=[HBM] * 5,
        out_specs=[VMEM] * 5,
        scratch_shapes=[pltpu.SemaphoreType.DMA((5,))],
        compiler_params=PARAMS,
        cost_estimate=pl.CostEstimate(flops=0, transcendentals=0, bytes_accessed=5 * MIB),
        name="load",
    )(*args)

    inner, *first = pl.pallas_call(
        lambda *refs: inner_kernel(early, *refs),
        out_shape=[bf16(frames, rows - 2, cols, chans)] + [bf16(rows - 2, cols, chans)] * len(early),
        in_specs=[VMEM] * 6,
        out_specs=[VMEM] * (1 + len(early)),
        compiler_params=PARAMS,
        cost_estimate=cost((frames + 2) * (rows - 2) * cols, 12, chans),
        name="inner",
    )(latent, prev, *params)
    first = [swap(piece, k) for k, piece in zip(early, first)]

    near, far, inner = lax.optimization_barrier((near, far, inner))
    corners = ahead(jnp.stack([near[frames - 2 :], far[frames - 2 :]]))
    hidden = pl.pallas_call(
        edge_kernel,
        out_shape=bf16(2, frames, cols, chans),
        in_specs=[VMEM] * 5,
        out_specs=VMEM,
        compiler_params=PARAMS,
        cost_estimate=cost(frames * 2 * cols, 9, chans),
        name="edge",
    )(latent, near, far, *params[:2])
    second = pl.pallas_call(
        lambda *refs: join_kernel(early, whole + [0], *refs),
        out_shape=[bf16(2, cols, chans)] * len(early) + [bf16(rows, cols, chans)] * (len(whole) + 1),
        in_specs=[VMEM] * 9,
        out_specs=[VMEM] * n,
        scratch_shapes=[pltpu.VMEM((frames, 2, cols, chans), BF16)],
        compiler_params=PARAMS,
        cost_estimate=cost(frames * 2 * cols, 6, chans),
        name="join",
    )(latent, prev, corners, hidden, inner, *params)
    own = second[-1]
    steps = early + whole
    sent = whole[: n // 2 - len(early)] + early + whole[n // 2 - len(early) :]
    second = {k: swap(second[steps.index(k)], k) for k in sent}

    out = grow([(k, [(1, rows - 2)]) for k in early] + [(0, [(0, rows)])], first + [own], None, rows * n, "grow_first")
    plan = [(k, [(0, 1), (rows - 1, 1)] if k in early else [(0, rows)]) for k in sent]
    return grow(plan, [second[k] for k in sent], out, rows * n, "grow_rest")


def solution(mesh):
    in_specs = (P("tm", "space", None, None), P(), P(), P(), P())
    out_specs = P(("tm", "space"), None, None, None)
    return jax.shard_map(body, mesh=mesh, in_specs=in_specs, out_specs=out_specs, check_vma=False)
```

time: 77.9 us -> 48.2 us (0.62); the launches traced: 76.4 us -> 48.1 us
  blocking collectives: 32.8 us -> 0 us
  starting transfers between devices: 7.59 us -> 27.2 us
  local copies, waits for them, and re-layouts: 16.8 us -> 0.01 us
  Pallas kernels: 0 us -> 11.7 us
  matrix products: 5.67 us -> 0 us
  other arithmetic: 2.43 us -> 0.02 us
  waiting for transfers between devices: 11 us -> 9.07 us
    all_to_all x1 -> x0, blocking collectives: 32.8 us -> none  [body(): lax.all_to_all(local_mixed, 'space', split_axis=0, concat_axis=1, tiled=T...]
    ppermute x3 -> x14, starting transfers between devices: 7.59 us -> 27.2 us  [the longest x11 22.2 us: swap(): lax.ppermute(block, 'space', [(i, i ^ k) for i in range(lax.axis_size('sp...]
    broadcast_in_dim x2 -> x0, local copies, waits for them, and re-layouts: 13.2 us -> none  [body(): jnp.broadcast_to(mixed[:, :, None, :, None, :], (count, height, 2, width,...]
    pallas_call x0 -> x7, Pallas kernels: none -> 11.7 us  [the longest x2 3.12 us: grow(): pl.pallas_call(lambda *refs: grow_kernel(plan, refs[:m], *refs[m + len(ex...]
    dot_general x12 -> x0, matrix products: 5.67 us -> none  [the longest x9 4.28 us: body(): jnp.dot(tile, spatial_weight[a, b], preferred_element_type=jnp.float32)]
    concatenate x3 -> x0, other arithmetic: 2.43 us -> none  [the longest x2 2.3 us: padded(): jnp.concatenate([lax.ppermute(tail, axis, [(i, (i + 1) % count) for i in...]
    slice x3 -> x0, local copies, waits for them, and re-layouts: 2.32 us -> none  [the longest x1 1.24 us: body(): bordered[:, a:a + rows, b:b + cols, :].reshape(frames * rows * cols, chans)]
    ppermute x3 -> x14, waiting for transfers between devices: 11 us -> 9.07 us  [the longest x11 9.06 us: swap(): lax.ppermute(block, 'space', [(i, i ^ k) for i in range(lax.axis_size('sp...]
  transfers between devices with their start and end apart: 3 -> 14, of which waited for: 2 -> 3; matrix products, arithmetic and copies ran while one was open for 0% -> 0% of each run, Pallas kernels for 0% -> 18%
where the time goes in v2:
time: 48.2 us; the launch traced here: 48.1 us
  starting transfers between devices  27.2 us (56%)
  Pallas kernels  11.7 us (24%)
  waiting for transfers between devices  9.07 us (19%)
    ppermute x11, starting transfers between devices, swap(): lax.ppermute(block, 'space', [(i, i ^ k) for i in range(lax.axis_size('sp...  22.2 us
    ppermute x11, waiting for transfers between devices, swap(): lax.ppermute(block, 'space', [(i, i ^ k) for i in range(lax.axis_size('sp...  9.06 us
    ppermute x1, starting transfers between devices, beside(): return lax.ppermute(block, 'space', route)  3.57 us
    pallas_call x2, Pallas kernels, grow(): pl.pallas_call(lambda *refs: grow_kernel(plan, refs[:m], *refs[m + len(ex...  3.12 us
    pallas_call x1, Pallas kernels, body(): pl.pallas_call(lambda *refs: inner_kernel(early, *refs), out_shape=[bf16(...  3.02 us
    pallas_call x1, Pallas kernels, body(): pl.pallas_call(load_kernel, out_shape=[jax.ShapeDtypeStruct(a.shape, a.dt...  1.73 us
    pallas_call x1, Pallas kernels, body(): pl.pallas_call(edge_kernel, out_shape=bf16(2, frames, cols, chans), in_sp...  1.54 us
    ppermute x2, starting transfers between devices, ahead(): return lax.ppermute(block, 'tm', [(t, (t + 1) % n) for t in range(n)])  1.37 us
  transfers between devices with their start and end apart: 14, of which 3 were waited for; matrix products, arithmetic and copies ran while one was open for 0% of the time, Pallas kernels for 18%

profile of v2, /device:TPU:0, one launch (start us, length us, event | category | flops | bytes accessed | tf_op | source)
XLA Modules:
  0.0 48.1 jit_solution(17493234032676159201)
XLA Ops:
  0.0 1.1 %border.1 = (bf16[8,64,256]{2,1,0:T(8,128)(2,1)S(1)}, bf16[8,64,256]{2,1,0:T(8,128)(2,1)S(1)}, bf16[2,4,64,256]{3,2,1,0:T(8,128)(2,1)S(1)}) custom-call(bf16[8,4,64,256]{3,2,1,0:T(8,128)(2,1)} %latent.1), custom_call_target="tpu_custom_call" | custom-call | tf_op jit(solution)/shard_map/border/pallas_call | solution.py:194
  1.1 0.5 %collective-permute-start = (bf16[2,4,64,256]{3,2,1,0:T(8,128)(2,1)S(1)}, bf16[2,4,64,256]{3,2,1,0:T(8,128)(2,1)S(1)}, u32[]{:S(2)}, u32[]{:S(2)}) collective-permute-start(bf16[2,4,64,256]{3,2,1,0:T(8,128)(2,1)S(1)} %get-tuple-element.29), channel_id=1, source_target_pairs={{0,8},{8,16},{16,24},{24,0},{1,9},{9,17},{17,25},{25,1},{2,10},{10... | collective-permute-start | bytes 786440 | tf_op jit(solution)/shard_map/ppermute | solution.py:176
  1.6 2.6 %collective-permute-start.1 = (bf16[8,64,256]{2,1,0:T(8,128)(2,1)S(1)}, bf16[8,64,256]{2,1,0:T(8,128)(2,1)S(1)}, u32[]{:S(2)}, u32[]{:S(2)}) collective-permute-start(bf16[8,64,256]{2,1,0:T(8,128)(2,1)S(1)} %get-tuple-element.30), channel_id=1, source_target_pairs={{0,1},{1,0},{2,3},{3,2},{4,5},{5,4},{6,7},{7,6},{8,9},{9,8},{10,11... | collective-permute-start | bytes 786440 | tf_op jit(solution)/shard_map/ppermute | solution.py:171
  4.2 3.6 %collective-permute-start.2 = (bf16[8,64,256]{2,1,0:T(8,128)(2,1)S(1)}, bf16[8,64,256]{2,1,0:T(8,128)(2,1)S(1)}, u32[]{:S(2)}, u32[]{:S(2)}) collective-permute-start(bf16[8,64,256]{2,1,0:T(8,128)(2,1)S(1)} %get-tuple-element.31), channel_id=1, source_target_pairs={{0,7},{1,2},{2,1},{3,4},{4,3},{5,6},{6,5},{7,0},{8,15},{9,10},{10,... | collective-permute-start | bytes 786440 | tf_op jit(solution)/shard_map/ppermute | solution.py:182
  7.8 1.7 %load.1 = (bf16[8,4,64,256]{3,2,1,0:T(8,128)(2,1)S(1)}, bf16[3,3,256,256]{3,2,1,0:T(8,128)(2,1)S(1)}, f32[1,256]{1,0:T(1,128)S(1)}, bf16[3,256,256]{2,1,0:T(8,128)(2,1)S(1)}, f32[1,256]{1,0:T(1,128)S(1)}) custom-call(bf16[8,4,64,256]{3,2,1,0:T(8,128)(2,1)} %latent.1, bf16[3,3,256,256]{3,2,1,0:T(8,128)(2,1)} %refs_1_.1, f32[1,256]{1,0:T(1,128)} %bitcast.6, ...), custom_call_target="tpu_custom_call" | custom-call | bytes 5242880 | tf_op jit(solution)/shard_map/load/pallas_call | solution.py:206
  9.5 0.0 collective-permute-done.refs_1_
  9.5 3.0 %inner.1 = (bf16[8,2,64,256]{3,2,1,0:T(8,128)(2,1)S(1)}, bf16[2,64,256]{2,1,0:T(8,128)(2,1)S(1)}, bf16[2,64,256]{2,1,0:T(8,128)(2,1)S(1)}, bf16[2,64,256]{2,1,0:T(8,128)(2,1)S(1)}) custom-call(bf16[8,4,64,256]{3,2,1,0:T(8,128)(2,1)S(1)} %get-tuple-element.28.refs_0_.latent, bf16[2,4,64,256]{3,2,1,0:T(8,128)(2,1)S(1)} %collective-permute-done.refs_1_, ...), custom_call_target="tpu_custom_call" | custom-call | flops 2013265920 | bytes 2097152 | tf_op jit(solution)/shard_map/inner/pallas_call | solution.py:217
  12.6 3.4 %collective-permute-done.1.near = bf16[8,64,256]{2,1,0:T(8,128)(2,1)S(1)} collective-permute-done((bf16[8,64,256]{2,1,0:T(8,128)(2,1)S(1)}, bf16[8,64,256]{2,1,0:T(8,128)(2,1)S(1)}, u32[]{:S(2)}, u32[]{:S(2)}) %collective-permute-start.1) | collective-permute-done | bytes 262176 | tf_op jit(solution)/shard_map/ppermute | solution.py:171
  16.0 0.0 collective-permute-done.2.far
  16.0 0.9 %collective-permute-start.3 = (bf16[2,2,64,256]{3,2,1,0:T(8,128)(2,1)S(1)}, bf16[2,2,64,256]{3,2,1,0:T(8,128)(2,1)S(1)}, u32[]{:S(2)}, u32[]{:S(2)}) collective-permute-start(bf16[2,2,64,256]{3,2,1,0:T(8,128)(2,1)S(1)} %pad_maximum_fusion), channel_id=1, source_target_pairs={{0,8},{8,16},{16,24},{24,0},{1,9},{9,17},{17,25},{25,1},{2,10},{10... | collective-permute-start | bytes 393224 | tf_op jit(solution)/shard_map/ppermute | solution.py:176
  16.9 3.1 %collective-permute-start.11 = (bf16[2,64,256]{2,1,0:T(8,128)(2,1)S(1)}, bf16[2,64,256]{2,1,0:T(8,128)(2,1)S(1)}, u32[]{:S(2)}, u32[]{:S(2)}) collective-permute-start(bf16[2,64,256]{2,1,0:T(8,128)(2,1)S(1)} %get-tuple-element.47), channel_id=1, source_target_pairs={{0,4},{1,5},{2,6},{3,7},{4,0},{5,1},{6,2},{7,3},{8,12},{9,13},{10,... | collective-permute-start | bytes 196616 | tf_op jit(solution)/shard_map/ppermute | solution.py:171
  20.0 1.3 %collective-permute-start.12 = (bf16[2,64,256]{2,1,0:T(8,128)(2,1)S(1)}, bf16[2,64,256]{2,1,0:T(8,128)(2,1)S(1)}, u32[]{:S(2)}, u32[]{:S(2)}) collective-permute-start(bf16[2,64,256]{2,1,0:T(8,128)(2,1)S(1)} %get-tuple-element.48), channel_id=1, source_target_pairs={{0,6},{1,7},{2,4},{3,5},{4,2},{5,3},{6,0},{7,1},{8,14},{9,15},{10,... | collective-permute-start | bytes 196616 | tf_op jit(solution)/shard_map/ppermute | solution.py:171
  21.4 2.6 %collective-permute-start.13 = (bf16[2,64,256]{2,1,0:T(8,128)(2,1)S(1)}, bf16[2,64,256]{2,1,0:T(8,128)(2,1)S(1)}, u32[]{:S(2)}, u32[]{:S(2)}) collective-permute-start(bf16[2,64,256]{2,1,0:T(8,128)(2,1)S(1)} %get-tuple-element.49), channel_id=1, source_target_pairs={{0,5},{1,4},{2,7},{3,6},{4,1},{5,0},{6,3},{7,2},{8,13},{9,12},{10,... | collective-permute-start | bytes 196616 | tf_op jit(solution)/shard_map/ppermute | solution.py:171
  24.0 1.5 %edge.1.refs_3_ = bf16[2,8,64,256]{3,2,1,0:T(8,128)(2,1)S(1)} custom-call(bf16[8,4,64,256]{3,2,1,0:T(8,128)(2,1)S(1)} %get-tuple-element.28.refs_0_.latent, bf16[8,64,256]{2,1,0:T(8,128)(2,1)S(1)} %collective-permute-done.1.near, bf16[8,64,256]{2,1,0:T(8,128)(2,1)S(1)} %collective-permute-done.2.far, ...), custom_call_target="tpu_custom_call" | custom-call | flops 1207959552 | bytes 2097152 | tf_op jit(solution)/shard_map/edge/pallas_call | solution.py:230
  25.5 0.0 collective-permute-done.3.refs_2_
  25.5 1.2 %join.1 = (bf16[2,64,256]{2,1,0:T(8,128)(2,1)S(1)}, bf16[2,64,256]{2,1,0:T(8,128)(2,1)S(1)}, bf16[2,64,256]{2,1,0:T(8,128)(2,1)S(1)}, bf16[4,64,256]{2,1,0:T(8,1...) custom-call(bf16[8,4,64,256]{3,2,1,0:T(8,128)(2,1)S(1)} %get-tuple-e, ...), custom_call_target="tpu_custom_call" | custom-call | flops 805306368 | bytes 2097152 | tf_op jit(solution)/shard_map/join/pallas_call | solution.py:239
  26.7 1.3 %collective-permute-start.5 = (bf16[2,64,256]{2,1,0:T(8,128)(2,1)S(1)}, bf16[2,64,256]{2,1,0:T(8,128)(2,1)S(1)}, u32[]{:S(2)}, u32[]{:S(2)}) collective-permute-start(bf16[2,64,256]{2,1,0:T(8,128)(2,1)S(1)} %get-tuple-element.41), channel_id=1, source_target_pairs={{0,4},{1,5},{2,6},{3,7},{4,0},{5,1},{6,2},{7,3},{8,12},{9,13},{10,... | collective-permute-start | bytes 196616 | tf_op jit(solution)/shard_map/ppermute | solution.py:171
  28.0 2.5 %collective-permute-start.6 = (bf16[2,64,256]{2,1,0:T(8,128)(2,1)S(1)}, bf16[2,64,256]{2,1,0:T(8,128)(2,1)S(1)}, u32[]{:S(2)}, u32[]{:S(2)}) collective-permute-start(bf16[2,64,256]{2,1,0:T(8,128)(2,1)S(1)} %get-tuple-element.42), channel_id=1, source_target_pairs={{0,6},{1,7},{2,4},{3,5},{4,2},{5,3},{6,0},{7,1},{8,14},{9,15},{10,... | collective-permute-start | bytes 196616 | tf_op jit(solution)/shard_map/ppermute | solution.py:171
  30.5 0.0 collective-permute-done.11.refs_0_
  30.5 1.4 %collective-permute-start.4 = (bf16[4,64,256]{2,1,0:T(8,128)(2,1)S(1)}, bf16[4,64,256]{2,1,0:T(8,128)(2,1)S(1)}, u32[]{:S(2)}, u32[]{:S(2)}) collective-permute-start(bf16[4,64,256]{2,1,0:T(8,128)(2,1)S(1)} %get-tuple-element.40), channel_id=1, source_target_pairs={{0,7},{1,6},{2,5},{3,4},{4,3},{5,2},{6,1},{7,0},{8,15},{9,14},{10,... | collective-permute-start | bytes 393224 | tf_op jit(solution)/shard_map/ppermute | solution.py:171
  31.9 0.0 collective-permute-done.12.refs_1_
  31.9 0.0 collective-permute-start.8
  31.9 0.0 collective-permute-done.13.refs_2_
  31.9 2.9 %collective-permute-start.9 = (bf16[4,64,256]{2,1,0:T(8,128)(2,1)S(1)}, bf16[4,64,256]{2,1,0:T(8,128)(2,1)S(1)}, u32[]{:S(2)}, u32[]{:S(2)}) collective-permute-start(bf16[4,64,256]{2,1,0:T(8,128)(2,1)S(1)} %get-tuple-element.45), channel_id=1, source_target_pairs={{0,2},{1,3},{2,0},{3,1},{4,6},{5,7},{6,4},{7,5},{8,10},{9,11},{10,... | collective-permute-start | bytes 393224 | tf_op jit(solution)/shard_map/ppermute | solution.py:171
  34.8 3.0 %collective-permute-done.5.refs_1_ = bf16[2,64,256]{2,1,0:T(8,128)(2,1)S(1)} collective-permute-done((bf16[2,64,256]{2,1,0:T(8,128)(2,1)S(1)}, bf16[2,64,256]{2,1,0:T(8,128)(2,1)S(1)}, u32[]{:S(2)}, u32[]{:S(2)}) %collective-permute-start.5) | collective-permute-done | bytes 65568 | tf_op jit(solution)/shard_map/ppermute | solution.py:171
  37.7 0.0 collective-permute-start.10
  37.7 0.0 collective-permute-done.6.refs_2_
  37.8 4.5 %collective-permute-start.7 = (bf16[2,64,256]{2,1,0:T(8,128)(2,1)S(1)}, bf16[2,64,256]{2,1,0:T(8,128)(2,1)S(1)}, u32[]{:S(2)}, u32[]{:S(2)}) collective-permute-start(bf16[2,64,256]{2,1,0:T(8,128)(2,1)S(1)} %get-tuple-element.43), channel_id=1, source_target_pairs={{0,5},{1,4},{2,7},{3,6},{4,1},{5,0},{6,3},{7,2},{8,13},{9,12},{10,... | collective-permute-start | bytes 196616 | tf_op jit(solution)/shard_map/ppermute | solution.py:171
  42.3 1.3 %grow_first.1.refs_7_ = bf16[1,64,128,256]{3,2,1,0:T(8,128)(2,1)} custom-call(bf16[2,64,256]{2,1,0:T(8,128)(2,1)S(1)} %collective-permute-done.11.refs_0_, bf16[2,64,256]{2,1,0:T(8,128)(2,1)S(1)} %collective-permute-done.12.refs_1_, bf16[2,64,256]{2,1,0:T(8,128)(2,1)S(1)} %collective-permute-done.13.refs_2_, bf16[4,64,256]{2,1,0:T(8,128)(2,1)S(1)} %get-tuple-element.50.refs_3_), custom_call_target="tpu_custom_call" | custom-call | bytes 1310720 | tf_op jit(solution)/shard_map/grow_first/pallas_call | solution.py:150
  43.5 2.6 %collective-permute-done.7.refs_3_ = bf16[2,64,256]{2,1,0:T(8,128)(2,1)S(1)} collective-permute-done((bf16[2,64,256]{2,1,0:T(8,128)(2,1)S(1)}, bf16[2,64,256]{2,1,0:T(8,128)(2,1)S(1)}, u32[]{:S(2)}, u32[]{:S(2)}) %collective-permute-start.7) | collective-permute-done | bytes 65568 | tf_op jit(solution)/shard_map/ppermute | solution.py:171
  46.2 0.0 collective-permute-done.4.refs_0_
  46.2 0.0 collective-permute-done.8.refs_4_
  46.2 0.0 collective-permute-done.9.refs_5_
  46.2 0.0 collective-permute-done.10.refs_6_
  46.2 1.9 %grow_rest.1 = bf16[1,64,128,256]{3,2,1,0:T(8,128)(2,1)} custom-call(bf16[4,64,256]{2,1,0:T(8,128)(2,1)S(1)} %collective-permute-done.4.refs_0_, bf16[2,64,256]{2,1,0:T(8,128)(2,1)S(1)} %collective-permute-done.5.refs_1_, bf16[2,64,256]{2,1,0:T(8,128)(2,1)S(1)} %collective-permute-done.6.refs_2_, ...), custom_call_target="tpu_custom_call", output_to_operand_aliasing={{}: (7, {})} | custom-call | bytes 2883584 | tf_op jit(solution)/shard_map/grow_rest/pallas_call | solution.py:150
  (2 shorter events, 0.0 us)
Async XLA Ops:
  1.1 8.4 %collective-permute-start = (bf16[2,4,64,256]{3,2,1,0:T(8,128)(2,1)S(1)}, bf16[2,4,64,256]{3,2,1,0:T(8,128)(2,1)S(1)}, u32[]{:S(2)}, u32[]{:S(2)}) collective-permute-start(bf16[2,4,64,256]{3,2,1,0:T(8,128)(2,1)S(1)} %get-tuple-element.29), channel_id=1, source_target_pairs={{0,8},{8,16},{16,24},{24,0},{1,9},{9,17},{17,25},{25,1},{2,10},{10... | collective-permute-start | bytes 786440 | tf_op jit(solution)/shard_map/ppermute | solution.py:176
  1.6 14.4 %collective-permute-start.1 = (bf16[8,64,256]{2,1,0:T(8,128)(2,1)S(1)}, bf16[8,64,256]{2,1,0:T(8,128)(2,1)S(1)}, u32[]{:S(2)}, u32[]{:S(2)}) collective-permute-start(bf16[8,64,256]{2,1,0:T(8,128)(2,1)S(1)} %get-tuple-element.30), channel_id=1, source_target_pairs={{0,1},{1,0},{2,3},{3,2},{4,5},{5,4},{6,7},{7,6},{8,9},{9,8},{10,11... | collective-permute-start | bytes 786440 | tf_op jit(solution)/shard_map/ppermute | solution.py:171
  4.2 11.8 %collective-permute-start.2 = (bf16[8,64,256]{2,1,0:T(8,128)(2,1)S(1)}, bf16[8,64,256]{2,1,0:T(8,128)(2,1)S(1)}, u32[]{:S(2)}, u32[]{:S(2)}) collective-permute-start(bf16[8,64,256]{2,1,0:T(8,128)(2,1)S(1)} %get-tuple-element.31), channel_id=1, source_target_pairs={{0,7},{1,2},{2,1},{3,4},{4,3},{5,6},{6,5},{7,0},{8,15},{9,10},{10,... | collective-permute-start | bytes 786440 | tf_op jit(solution)/shard_map/ppermute | solution.py:182
  16.0 9.5 %collective-permute-start.3 = (bf16[2,2,64,256]{3,2,1,0:T(8,128)(2,1)S(1)}, bf16[2,2,64,256]{3,2,1,0:T(8,128)(2,1)S(1)}, u32[]{:S(2)}, u32[]{:S(2)}) collective-permute-start(bf16[2,2,64,256]{3,2,1,0:T(8,128)(2,1)S(1)} %pad_maximum_fusion), channel_id=1, source_target_pairs={{0,8},{8,16},{16,24},{24,0},{1,9},{9,17},{17,25},{25,1},{2,10},{10... | collective-permute-start | bytes 393224 | tf_op jit(solution)/shard_map/ppermute | solution.py:176
  16.9 13.6 %collective-permute-start.11 = (bf16[2,64,256]{2,1,0:T(8,128)(2,1)S(1)}, bf16[2,64,256]{2,1,0:T(8,128)(2,1)S(1)}, u32[]{:S(2)}, u32[]{:S(2)}) collective-permute-start(bf16[2,64,256]{2,1,0:T(8,128)(2,1)S(1)} %get-tuple-element.47), channel_id=1, source_target_pairs={{0,4},{1,5},{2,6},{3,7},{4,0},{5,1},{6,2},{7,3},{8,12},{9,13},{10,... | collective-permute-start | bytes 196616 | tf_op jit(solution)/shard_map/ppermute | solution.py:171
  20.0 11.9 %collective-permute-start.12 = (bf16[2,64,256]{2,1,0:T(8,128)(2,1)S(1)}, bf16[2,64,256]{2,1,0:T(8,128)(2,1)S(1)}, u32[]{:S(2)}, u32[]{:S(2)}) collective-permute-start(bf16[2,64,256]{2,1,0:T(8,128)(2,1)S(1)} %get-tuple-element.48), channel_id=1, source_target_pairs={{0,6},{1,7},{2,4},{3,5},{4,2},{5,3},{6,0},{7,1},{8,14},{9,15},{10,... | collective-permute-start | bytes 196616 | tf_op jit(solution)/shard_map/ppermute | solution.py:171
  21.4 10.5 %collective-permute-start.13 = (bf16[2,64,256]{2,1,0:T(8,128)(2,1)S(1)}, bf16[2,64,256]{2,1,0:T(8,128)(2,1)S(1)}, u32[]{:S(2)}, u32[]{:S(2)}) collective-permute-start(bf16[2,64,256]{2,1,0:T(8,128)(2,1)S(1)} %get-tuple-element.49), channel_id=1, source_target_pairs={{0,5},{1,4},{2,7},{3,6},{4,1},{5,0},{6,3},{7,2},{8,13},{9,12},{10,... | collective-permute-start | bytes 196616 | tf_op jit(solution)/shard_map/ppermute | solution.py:171
  26.7 11.0 %collective-permute-start.5 = (bf16[2,64,256]{2,1,0:T(8,128)(2,1)S(1)}, bf16[2,64,256]{2,1,0:T(8,128)(2,1)S(1)}, u32[]{:S(2)}, u32[]{:S(2)}) collective-permute-start(bf16[2,64,256]{2,1,0:T(8,128)(2,1)S(1)} %get-tuple-element.41), channel_id=1, source_target_pairs={{0,4},{1,5},{2,6},{3,7},{4,0},{5,1},{6,2},{7,3},{8,12},{9,13},{10,... | collective-permute-start | bytes 196616 | tf_op jit(solution)/shard_map/ppermute | solution.py:171
  28.0 9.7 %collective-permute-start.6 = (bf16[2,64,256]{2,1,0:T(8,128)(2,1)S(1)}, bf16[2,64,256]{2,1,0:T(8,128)(2,1)S(1)}, u32[]{:S(2)}, u32[]{:S(2)}) collective-permute-start(bf16[2,64,256]{2,1,0:T(8,128)(2,1)S(1)} %get-tuple-element.42), channel_id=1, source_target_pairs={{0,6},{1,7},{2,4},{3,5},{4,2},{5,3},{6,0},{7,1},{8,14},{9,15},{10,... | collective-permute-start | bytes 196616 | tf_op jit(solution)/shard_map/ppermute | solution.py:171
  30.5 15.7 %collective-permute-start.4 = (bf16[4,64,256]{2,1,0:T(8,128)(2,1)S(1)}, bf16[4,64,256]{2,1,0:T(8,128)(2,1)S(1)}, u32[]{:S(2)}, u32[]{:S(2)}) collective-permute-start(bf16[4,64,256]{2,1,0:T(8,128)(2,1)S(1)} %get-tuple-element.40), channel_id=1, source_target_pairs={{0,7},{1,6},{2,5},{3,4},{4,3},{5,2},{6,1},{7,0},{8,15},{9,14},{10,... | collective-permute-start | bytes 393224 | tf_op jit(solution)/shard_map/ppermute | solution.py:171
  31.9 14.3 %collective-permute-start.8 = (bf16[4,64,256]{2,1,0:T(8,128)(2,1)S(1)}, bf16[4,64,256]{2,1,0:T(8,128)(2,1)S(1)}, u32[]{:S(2)}, u32[]{:S(2)}) collective-permute-start(bf16[4,64,256]{2,1,0:T(8,128)(2,1)S(1)} %get-tuple-element.44), channel_id=1, source_target_pairs={{0,3},{1,2},{2,1},{3,0},{4,7},{5,6},{6,5},{7,4},{8,11},{9,10},{10,... | collective-permute-start | bytes 393224 | tf_op jit(solution)/shard_map/ppermute | solution.py:171
  31.9 14.3 %collective-permute-start.9 = (bf16[4,64,256]{2,1,0:T(8,128)(2,1)S(1)}, bf16[4,64,256]{2,1,0:T(8,128)(2,1)S(1)}, u32[]{:S(2)}, u32[]{:S(2)}) collective-permute-start(bf16[4,64,256]{2,1,0:T(8,128)(2,1)S(1)} %get-tuple-element.45), channel_id=1, source_target_pairs={{0,2},{1,3},{2,0},{3,1},{4,6},{5,7},{6,4},{7,5},{8,10},{9,11},{10,... | collective-permute-start | bytes 393224 | tf_op jit(solution)/shard_map/ppermute | solution.py:171
  37.7 8.4 %collective-permute-start.10 = (bf16[4,64,256]{2,1,0:T(8,128)(2,1)S(1)}, bf16[4,64,256]{2,1,0:T(8,128)(2,1)S(1)}, u32[]{:S(2)}, u32[]{:S(2)}) collective-permute-start(bf16[4,64,256]{2,1,0:T(8,128)(2,1)S(1)} %get-tuple-element.46), channel_id=1, source_target_pairs={{0,1},{1,0},{2,3},{3,2},{4,5},{5,4},{6,7},{7,6},{8,9},{9,8},{10,11... | collective-permute-start | bytes 393224 | tf_op jit(solution)/shard_map/ppermute | solution.py:171
  37.8 8.4 %collective-permute-start.7 = (bf16[2,64,256]{2,1,0:T(8,128)(2,1)S(1)}, bf16[2,64,256]{2,1,0:T(8,128)(2,1)S(1)}, u32[]{:S(2)}, u32[]{:S(2)}) collective-permute-start(bf16[2,64,256]{2,1,0:T(8,128)(2,1)S(1)} %get-tuple-element.43), channel_id=1, source_target_pairs={{0,5},{1,4},{2,7},{3,6},{4,1},{5,0},{6,3},{7,2},{8,13},{9,12},{10,... | collective-permute-start | bytes 196616 | tf_op jit(solution)/shard_map/ppermute | solution.py:171

commit v3 on v2

--- a/solution.py
+++ b/solution.py
@@ -7,6 +7,7 @@
 
 VMEM = pl.BlockSpec(memory_space=pltpu.VMEM)
 HBM = pl.BlockSpec(memory_space=pltpu.HBM)
+ANY = pl.BlockSpec(memory_space=pl.ANY)
 BF16 = jnp.bfloat16
 MIB = 1 << 20
 PARAMS = pltpu.CompilerParams(vmem_limit_bytes=24 * MIB)
@@ -17,9 +18,8 @@
 
 
 def exchanges(n):
-    far = sorted(range(n // 2, n), key=lambda k: (k & 1, k))
-    cut = 3 * n // 8
-    return far[:cut], far[cut:] + sorted(range(1, n // 2), key=lambda k: -k)
+    half = n // 2
+    return list(range(1, half)) + sorted(range(half, n), key=lambda k: (k & 1, k))
 
 
 def copy_all(pairs, sems):
@@ -67,18 +67,15 @@
     return (own.astype(jnp.float32) + total.reshape(frames, cols, chans) + bias).astype(BF16)
 
 
-def inner_kernel(early, latent, prev, sw, sb, tw, tb, mixed, *outs):
-    rows = latent.shape[1]
-    me = lax.axis_index("space")
-
-    def row(r):
-        return jnp.concatenate([prev[:, r], latent[:, r]], axis=0)
-
-    for r in range(1, rows - 1):
-        hidden = activate([row(r - 1), row(r), row(r + 1)], (0, 1, 2), sw, sb[...])
-        mixed[:, r - 1] = mix(hidden[:2], hidden[2:], latent[:, r], tw, tb[...])
-    for k, out in zip(early, outs):
-        out[...] = mixed[lax.bitwise_xor(me, k)]
+def inner_kernel(latent, sw, sb, hidden):
+    for r in range(1, latent.shape[1] - 1):
+        hidden[r - 1] = activate([latent[:, r + i] for i in (-1, 0, 1)], (0, 1, 2), sw, sb[...])
+
+
+def inner_mix_kernel(latent, prev, hidden, sw, sb, tw, tb, out):
+    for r in range(1, latent.shape[1] - 1):
+        before = activate([prev[:, r + i] for i in (-1, 0, 1)], (0, 1, 2), sw, sb[...])
+        out[:, r - 1] = mix(before, hidden[r - 1], latent[:, r], tw, tb[...])
 
 
 def sides(rows):
@@ -100,20 +97,21 @@
         hidden[i] = activate([outside(i, halo[...]), latent[:, r], latent[:, beyond]], order, sw, sb[...])
 
 
-def join_kernel(early, whole, latent, prev, corners, hidden, inner, sw, sb, tw, tb, *rest):
-    outs, mixed = rest[:-1], rest[-1]
+def join_kernel(steps, latent, prev, corners, hidden, sw, sb, tw_hbm, tb, *rest):
+    outs, mixed, tw, sem = rest[:-3], *rest[-3:]
+    copy = pltpu.make_async_copy(tw_hbm, tw, sem)
+    copy.start()
     rows = latent.shape[1]
     me = lax.axis_index("space")
-    for i, (r, beyond, place, order) in enumerate(sides(rows)):
-        before = activate([outside(i, corners[i]), prev[:, r], prev[:, beyond]], order, sw, sb[...])
-        mixed[:, place] = mix(before, hidden[i], latent[:, r], tw, tb[...])
-    for k, out in zip(early, outs):
+    before = [
+        activate([outside(i, corners[i]), prev[:, r], prev[:, beyond]], order, sw, sb[...])
+        for i, (r, beyond, _, order) in enumerate(sides(rows))
+    ]
+    copy.wait()
+    for i, (r, _, place, _) in enumerate(sides(rows)):
+        mixed[:, place] = mix(before[i], hidden[i], latent[:, r], tw, tb[...])
+    for k, out in zip(steps, outs):
         out[...] = mixed[lax.bitwise_xor(me, k)]
-    for k, out in zip(whole, outs[len(early) :]):
-        frame = lax.bitwise_xor(me, k)
-        out[0] = mixed[frame, 0]
-        out[pl.ds(1, rows - 2)] = inner[frame]
-        out[rows - 1] = mixed[frame, 1]
 
 
 def grow_kernel(plan, pieces, out, grown, sems):
@@ -123,21 +121,24 @@
     at = lax.broadcasted_iota(jnp.int32, (2 * cols, cols), 0)
     of = lax.broadcasted_iota(jnp.int32, (2 * cols, cols), 1)
     twice = jnp.where(at // 2 == of, 1.0, 0.0).astype(BF16)
+    rows = [(piece, i) for piece in pieces for i in range(piece.shape[0])]
     copies, used = [], 0
-    for (k, runs), piece in zip(plan, pieces):
-        base, src = used, lax.bitwise_xor(me, k)
-        for i in range(piece.shape[0]):
-            wide = jnp.dot(twice, piece[i], preferred_element_type=jnp.float32).astype(BF16)
-            grown[used] = wide
-            grown[used + 1] = wide
-            used += 2
-        for first, rows in runs:
+    for src, k, runs in plan:
+        src = lax.bitwise_xor(me, k) if src is None else src
+        for first, count in runs:
+            for i in range(count):
+                piece, r = rows[used + i]
+                wide = jnp.dot(twice, piece[r], preferred_element_type=jnp.float32).astype(BF16)
+                grown[2 * (used + i)] = wide
+                grown[2 * (used + i) + 1] = wide
             copy = pltpu.make_async_copy(
-                grown.at[pl.ds(base, 2 * rows)], out.at[0, pl.ds(src * tile + 2 * first, 2 * rows)], sems.at[len(copies)]
+                grown.at[pl.ds(2 * used, 2 * count)],
+                out.at[0, pl.ds(src * tile + 2 * first, 2 * count)],
+                sems.at[len(copies)],
             )
             copy.start()
             copies.append(copy)
-            base += 2 * rows
+            used += count
     for copy in copies:
         copy.wait()
 
@@ -155,7 +156,7 @@
         input_output_aliases={m: 0} if extra else {},
         scratch_shapes=[
             pltpu.VMEM((2 * count, 2 * cols, chans), BF16),
-            pltpu.SemaphoreType.DMA((sum(len(runs) for _, runs in plan),)),
+            pltpu.SemaphoreType.DMA((sum(len(runs) for _, _, runs in plan),)),
         ],
         compiler_params=PARAMS,
         cost_estimate=pl.CostEstimate(flops=0, transcendentals=0, bytes_accessed=8 * count * cols * chans),
@@ -187,7 +188,7 @@
     n = lax.axis_size("space")
     if n & (n - 1) or frames != n:
         raise ValueError("shape")
-    early, whole = exchanges(n)
+    steps = exchanges(n)
 
     args = [latent, spatial_weight, spatial_bias.reshape(1, chans), temporal_weight, temporal_bias.reshape(1, chans)]
     args = [pltpu.with_memory_space_constraint(a, pltpu.HBM) for a in args]
@@ -214,18 +215,28 @@
         name="load",
     )(*args)
 
-    inner, *first = pl.pallas_call(
-        lambda *refs: inner_kernel(early, *refs),
-        out_shape=[bf16(frames, rows - 2, cols, chans)] + [bf16(rows - 2, cols, chans)] * len(early),
-        in_specs=[VMEM] * 6,
-        out_specs=[VMEM] * (1 + len(early)),
-        compiler_params=PARAMS,
-        cost_estimate=cost((frames + 2) * (rows - 2) * cols, 12, chans),
+    hidden = pl.pallas_call(
+        inner_kernel,
+        out_shape=bf16(rows - 2, frames, cols, chans),
+        in_specs=[VMEM] * 3,
+        out_specs=VMEM,
+        compiler_params=PARAMS,
+        cost_estimate=cost(frames * (rows - 2) * cols, 9, chans),
         name="inner",
-    )(latent, prev, *params)
-    first = [swap(piece, k) for k, piece in zip(early, first)]
-
-    near, far, inner = lax.optimization_barrier((near, far, inner))
+    )(latent, *params[:2])
+    inner = pl.pallas_call(
+        inner_mix_kernel,
+        out_shape=bf16(frames, rows - 2, cols, chans),
+        in_specs=[VMEM] * 7,
+        out_specs=VMEM,
+        compiler_params=PARAMS,
+        cost_estimate=cost(frames * (rows - 2) * cols, 6, chans),
+        name="inner_mix",
+    )(latent, prev, hidden, *params)
+    inner_own = inner
+    inner = lax.all_to_all(inner, "space", split_axis=0, concat_axis=1, tiled=True)[0]
+
+    near, far, token = lax.optimization_barrier((near, far, inner_own))
     corners = ahead(jnp.stack([near[frames - 2 :], far[frames - 2 :]]))
     hidden = pl.pallas_call(
         edge_kernel,
@@ -236,24 +247,26 @@
         cost_estimate=cost(frames * 2 * cols, 9, chans),
         name="edge",
     )(latent, near, far, *params[:2])
-    second = pl.pallas_call(
-        lambda *refs: join_kernel(early, whole + [0], *refs),
-        out_shape=[bf16(2, cols, chans)] * len(early) + [bf16(rows, cols, chans)] * (len(whole) + 1),
-        in_specs=[VMEM] * 9,
+    edges = pl.pallas_call(
+        lambda *refs: join_kernel([0] + steps, *refs),
+        out_shape=[bf16(2, cols, chans)] * n,
+        in_specs=[VMEM] * 6 + [HBM, VMEM],
         out_specs=[VMEM] * n,
-        scratch_shapes=[pltpu.VMEM((frames, 2, cols, chans), BF16)],
+        scratch_shapes=[
+            pltpu.VMEM((frames, 2, cols, chans), BF16),
+            pltpu.VMEM(temporal_weight.shape, BF16),
+            pltpu.SemaphoreType.DMA,
+        ],
         compiler_params=PARAMS,
         cost_estimate=cost(frames * 2 * cols, 6, chans),
         name="join",
-    )(latent, prev, corners, hidden, inner, *params)
-    own = second[-1]
-    steps = early + whole
-    sent = whole[: n // 2 - len(early)] + early + whole[n // 2 - len(early) :]
-    second = {k: swap(second[steps.index(k)], k) for k in sent}
-
-    out = grow([(k, [(1, rows - 2)]) for k in early] + [(0, [(0, rows)])], first + [own], None, rows * n, "grow_first")
-    plan = [(k, [(0, 1), (rows - 1, 1)] if k in early else [(0, rows)]) for k in sent]
-    return grow(plan, [second[k] for k in sent], out, rows * n, "grow_rest")
+    )(latent, prev, corners, hidden, *params[:2], args[3], params[3])
+    edges = [edges[0]] + [swap(edge, k) for k, edge in zip(steps, edges[1:])]
+
+    out = grow([(s, None, [(1, rows - 2)]) for s in range(n)], [pltpu.with_memory_space_constraint(inner, pltpu.HBM)], None, rows * n, "grow_inner")
+    ends = [(0, 1), (rows - 1, 1)]
+    out = grow([(None, k, ends) for k in [0] + steps[:n // 2]], edges[: n // 2 + 1], out, rows * n, "grow_first")
+    return grow([(None, k, ends) for k in steps[n // 2:]], edges[n // 2 + 1 :], out, rows * n, "grow_last")
 
 
 def solution(mesh):

time: 48.2 us -> 45.1 us (0.936)
  starting transfers between devices: 27.2 us -> 23 us
  Pallas kernels: 11.7 us -> 14.7 us
  waiting for transfers between devices: 9.07 us -> 6.88 us
    ppermute x11 -> x8, starting transfers between devices: 22.2 us -> 13.7 us  [swap(): lax.ppermute(block, 'space', [(i, i ^ k) for i in range(lax.axis_size('sp...]
    all_to_all x0 -> x1, starting transfers between devices: none -> 4.15 us  [body(): lax.all_to_all(inner, 'space', split_axis=0, concat_axis=1, tiled=True)[0]]
    ppermute x11 -> x8, waiting for transfers between devices: 9.06 us -> 4.93 us  [swap(): lax.ppermute(block, 'space', [(i, i ^ k) for i in range(lax.axis_size('sp...]
    ppermute x2, waiting for transfers between devices: 0.01 us -> 1.89 us  [ahead(): return lax.ppermute(block, 'tm', [(t, (t + 1) % n) for t in range(n)])]
    pallas_call x2 -> x3, Pallas kernels: 3.12 us -> 4.97 us  [grow(): pl.pallas_call(lambda *refs: grow_kernel(plan, refs[:m], *refs[m + len(ex...]
    pallas_call x2 -> x3, Pallas kernels: 4.18 us -> 5.4 us  [the longest x1 1.99 us: body(): pl.pallas_call(lambda *refs: join_kernel([0] + steps, *refs), out_shape=[...]
  transfers between devices with their start and end apart: 14 -> 12, of which waited for: 3 -> 4; matrix products, arithmetic and copies ran while one was open for 0% -> 0% of each run, Pallas kernels for 18% -> 28%
where the time goes in v3:
time: 45.1 us; the launch traced here: 44.8 us
  starting transfers between devices  23 us (51%)
  Pallas kernels  14.7 us (33%)
  waiting for transfers between devices  6.88 us (15%)
    ppermute x8, starting transfers between devices, swap(): lax.ppermute(block, 'space', [(i, i ^ k) for i in range(lax.axis_size('sp...  13.7 us
    pallas_call x3, Pallas kernels, grow(): pl.pallas_call(lambda *refs: grow_kernel(plan, refs[:m], *refs[m + len(ex...  4.97 us
    ppermute x8, waiting for transfers between devices, swap(): lax.ppermute(block, 'space', [(i, i ^ k) for i in range(lax.axis_size('sp...  4.93 us
    all_to_all x1, starting transfers between devices, body(): lax.all_to_all(inner, 'space', split_axis=0, concat_axis=1, tiled=True)[0]  4.15 us
    ppermute x1, starting transfers between devices, beside(): return lax.ppermute(block, 'space', route)  3.57 us
    pallas_call x1, Pallas kernels, body(): pl.pallas_call(lambda *refs: join_kernel([0] + steps, *refs), out_shape=[...  1.99 us
    pallas_call x1, Pallas kernels, body(): pl.pallas_call(inner_mix_kernel, out_shape=bf16(frames, rows - 2, cols, c...  1.91 us
    ppermute x2, waiting for transfers between devices, ahead(): return lax.ppermute(block, 'tm', [(t, (t + 1) % n) for t in range(n)])  1.89 us
  transfers between devices with their start and end apart: 12, of which 4 were waited for; matrix products, arithmetic and copies ran while one was open for 0% of the time, Pallas kernels for 28%

profile of v3, /device:TPU:0, one launch (start us, length us, event | category | flops | bytes accessed | tf_op | source)
XLA Modules:
  0.0 44.8 jit_solution(2048945486493620708)
XLA Ops:
  0.0 1.1 %border.1 = (bf16[8,64,256]{2,1,0:T(8,128)(2,1)S(1)}, bf16[8,64,256]{2,1,0:T(8,128)(2,1)S(1)}, bf16[2,4,64,256]{3,2,1,0:T(8,128)(2,1)S(1)}) custom-call(bf16[8,4,64,256]{3,2,1,0:T(8,128)(2,1)} %latent.1), custom_call_target="tpu_custom_call" | custom-call | tf_op jit(solution)/shard_map/border/pallas_call | solution.py:195
  1.1 0.5 %collective-permute-start = (bf16[2,4,64,256]{3,2,1,0:T(8,128)(2,1)S(1)}, bf16[2,4,64,256]{3,2,1,0:T(8,128)(2,1)S(1)}, u32[]{:S(2)}, u32[]{:S(2)}) collective-permute-start(bf16[2,4,64,256]{3,2,1,0:T(8,128)(2,1)S(1)} %get-tuple-element.24), channel_id=1, source_target_pairs={{0,8},{8,16},{16,24},{24,0},{1,9},{9,17},{17,25},{25,1},{2,10},{10... | collective-permute-start | bytes 786440 | tf_op jit(solution)/shard_map/ppermute | solution.py:177
  1.6 2.6 %collective-permute-start.1 = (bf16[8,64,256]{2,1,0:T(8,128)(2,1)S(1)}, bf16[8,64,256]{2,1,0:T(8,128)(2,1)S(1)}, u32[]{:S(2)}, u32[]{:S(2)}) collective-permute-start(bf16[8,64,256]{2,1,0:T(8,128)(2,1)S(1)} %get-tuple-element.25), channel_id=1, source_target_pairs={{0,1},{1,0},{2,3},{3,2},{4,5},{5,4},{6,7},{7,6},{8,9},{9,8},{10,11... | collective-permute-start | bytes 786440 | tf_op jit(solution)/shard_map/ppermute | solution.py:172
  4.2 3.6 %collective-permute-start.2 = (bf16[8,64,256]{2,1,0:T(8,128)(2,1)S(1)}, bf16[8,64,256]{2,1,0:T(8,128)(2,1)S(1)}, u32[]{:S(2)}, u32[]{:S(2)}) collective-permute-start(bf16[8,64,256]{2,1,0:T(8,128)(2,1)S(1)} %get-tuple-element.26), channel_id=1, source_target_pairs={{0,7},{1,2},{2,1},{3,4},{4,3},{5,6},{6,5},{7,0},{8,15},{9,10},{10,... | collective-permute-start | bytes 786440 | tf_op jit(solution)/shard_map/ppermute | solution.py:183
  7.8 1.7 %load.1 = (bf16[8,4,64,256]{3,2,1,0:T(8,128)(2,1)S(1)}, bf16[3,3,256,256]{3,2,1,0:T(8,128)(2,1)S(1)}, f32[1,256]{1,0:T(1,128)S(1)}, bf16[3,256,256]{2,1,0:T(8,128)(2,1)S(1)}, f32[1,256]{1,0:T(1,128)S(1)}) custom-call(bf16[8,4,64,256]{3,2,1,0:T(8,128)(2,1)} %latent.1, bf16[3,3,256,256]{3,2,1,0:T(8,128)(2,1)} %refs_1_.1, f32[1,256]{1,0:T(1,128)} %bitcast.7, ...), custom_call_target="tpu_custom_call" | custom-call | bytes 5242880 | tf_op jit(solution)/shard_map/load/pallas_call | solution.py:207
  9.5 1.5 %inner.1.hidden = bf16[2,8,64,256]{3,2,1,0:T(8,128)(2,1)S(1)} custom-call(bf16[8,4,64,256]{3,2,1,0:T(8,128)(2,1)S(1)} %get-tuple-element.23.latent.refs_0_, bf16[3,3,256,256]{3,2,1,0:T(8,128)(2,1)S(1)} %get-tuple-element.27.sw.refs_4_, f32[1,256]{1,0:T(1,128)S(1)} %get-tuple-element.28.sb.refs_5_), custom_call_target="tpu_custom_call" | custom-call | flops 1207959552 | bytes 2097152 | tf_op jit(solution)/shard_map/inner/pallas_call | solution.py:218
  11.0 0.0 collective-permute-done.prev.refs_1_
  11.0 1.9 %inner_mix.1 = bf16[8,2,64,256]{3,2,1,0:T(8,128)(2,1)} custom-call(bf16[8,4,64,256]{3,2,1,0:T(8,128)(2,1)S(1)} %get-tuple-element.23.latent.refs_0_, bf16[2,4,64,256]{3,2,1,0:T(8,128)(2,1)S(1)} %collective-permute-done.prev.refs_1_, bf16[2,8,64,256]{3,2,1,0:T(8,128)(2,1)S(1)} %inner.1.hidden, bf16[3,3,256,256]{3,2,1,0:T(8,128)(2,1)S(1)} %get-tuple-element.27.sw.refs_4_, ...), custom_call_target="tpu_custom_call" | custom-call | flops 805306368 | bytes 2097152 | tf_op jit(solution)/shard_map/inner_mix/pallas_call | solution.py:227
  13.0 4.1 %all-to-all-start = ((bf16[8,2,64,256]{3,2,1,0:T(8,128)(2,1)}), bf16[8,2,64,256]{3,2,1,0:T(8,128)(2,1)}, u32[]{:S(2)}, u32[]{:S(2)}) async-start(bf16[8,2,64,256]{3,2,1,0:T(8,128)(2,1)} %inner_mix.1), calls=%async_computation | async-start | bytes 1048576 | tf_op jit(solution)/shard_map/all_to_all | solution.py:237
  17.1 0.0 collective-permute-done.1.near
  17.1 0.0 collective-permute-done.2.far
  17.2 1.0 %collective-permute-start.3 = (bf16[2,2,64,256]{3,2,1,0:T(8,128)(2,1)S(1)}, bf16[2,2,64,256]{3,2,1,0:T(8,128)(2,1)S(1)}, u32[]{:S(2)}, u32[]{:S(2)}) collective-permute-start(bf16[2,2,64,256]{3,2,1,0:T(8,128)(2,1)S(1)} %pad_maximum_fusion), channel_id=1, source_target_pairs={{0,8},{8,16},{16,24},{24,0},{1,9},{9,17},{17,25},{25,1},{2,10},{10... | collective-permute-start | bytes 393224 | tf_op jit(solution)/shard_map/ppermute | solution.py:177
  18.2 1.5 %edge.1.refs_3_ = bf16[2,8,64,256]{3,2,1,0:T(8,128)(2,1)S(1)} custom-call(bf16[8,4,64,256]{3,2,1,0:T(8,128)(2,1)S(1)} %get-tuple-element.23.latent.refs_0_, bf16[8,64,256]{2,1,0:T(8,128)(2,1)S(1)} %collective-permute-done.1.near, bf16[8,64,256]{2,1,0:T(8,128)(2,1)S(1)} %collective-permute-done.2.far, ...), custom_call_target="tpu_custom_call" | custom-call | flops 1207959552 | bytes 2097152 | tf_op jit(solution)/shard_map/edge/pallas_call | solution.py:241
  19.7 1.9 %collective-permute-done.3.refs_2_ = bf16[2,2,64,256]{3,2,1,0:T(8,128)(2,1)S(1)} collective-permute-done((bf16[2,2,64,256]{3,2,1,0:T(8,128)(2,1)S(1)}, bf16[2,2,64,256]{3,2,1,0:T(8,128)(2,1)S(1)}, u32[]{:S(2)}, u32[]{:S(2)}) %collective-permute-start.3) | collective-permute-done | bytes 131104 | tf_op jit(solution)/shard_map/ppermute | solution.py:177
  21.6 2.0 %join.1 = (bf16[2,64,256]{2,1,0:T(8,128)(2,1)S(1)}, bf16[2,64,256]{2,1,0:T(8,128)(2,1)S(1)}, bf16[2,64,256]{2,1,0:T(8,128)(2,1)S(1)}, bf16[2,64,256]{2,1,0:T(8,1...) custom-call(bf16[8,4,64,256]{3,2,1,0:T(8,128)(2,1)S(1)} %get-tuple-e, ...), custom_call_target="tpu_custom_call" | custom-call | flops 805306368 | bytes 2097152 | tf_op jit(solution)/shard_map/join/pallas_call | solution.py:250
  23.6 1.9 %collective-permute-start.7 = (bf16[2,64,256]{2,1,0:T(8,128)(2,1)S(1)}, bf16[2,64,256]{2,1,0:T(8,128)(2,1)S(1)}, u32[]{:S(2)}, u32[]{:S(2)}) collective-permute-start(bf16[2,64,256]{2,1,0:T(8,128)(2,1)S(1)} %get-tuple-element.37), channel_id=1, source_target_pairs={{0,1},{1,0},{2,3},{3,2},{4,5},{5,4},{6,7},{7,6},{8,9},{9,8},{10,11... | collective-permute-start | bytes 196616 | tf_op jit(solution)/shard_map/ppermute | solution.py:172
  25.6 1.5 %collective-permute-start.8 = (bf16[2,64,256]{2,1,0:T(8,128)(2,1)S(1)}, bf16[2,64,256]{2,1,0:T(8,128)(2,1)S(1)}, u32[]{:S(2)}, u32[]{:S(2)}) collective-permute-start(bf16[2,64,256]{2,1,0:T(8,128)(2,1)S(1)} %get-tuple-element.38), channel_id=1, source_target_pairs={{0,2},{1,3},{2,0},{3,1},{4,6},{5,7},{6,4},{7,5},{8,10},{9,11},{10,... | collective-permute-start | bytes 196616 | tf_op jit(solution)/shard_map/ppermute | solution.py:172
  27.0 2.4 %collective-permute-start.4 = (bf16[2,64,256]{2,1,0:T(8,128)(2,1)S(1)}, bf16[2,64,256]{2,1,0:T(8,128)(2,1)S(1)}, u32[]{:S(2)}, u32[]{:S(2)}) collective-permute-start(bf16[2,64,256]{2,1,0:T(8,128)(2,1)S(1)} %get-tuple-element.33), channel_id=1, source_target_pairs={{0,6},{1,7},{2,4},{3,5},{4,2},{5,3},{6,0},{7,1},{8,14},{9,15},{10,... | collective-permute-start | bytes 196616 | tf_op jit(solution)/shard_map/ppermute | solution.py:172
  29.4 0.6 %collective-permute-start.9 = (bf16[2,64,256]{2,1,0:T(8,128)(2,1)S(1)}, bf16[2,64,256]{2,1,0:T(8,128)(2,1)S(1)}, u32[]{:S(2)}, u32[]{:S(2)}) collective-permute-start(bf16[2,64,256]{2,1,0:T(8,128)(2,1)S(1)} %get-tuple-element.39), channel_id=1, source_target_pairs={{0,3},{1,2},{2,1},{3,0},{4,7},{5,6},{6,5},{7,4},{8,11},{9,10},{10,... | collective-permute-start | bytes 196616 | tf_op jit(solution)/shard_map/ppermute | solution.py:172
  30.0 1.4 %collective-permute-start.10 = (bf16[2,64,256]{2,1,0:T(8,128)(2,1)S(1)}, bf16[2,64,256]{2,1,0:T(8,128)(2,1)S(1)}, u32[]{:S(2)}, u32[]{:S(2)}) collective-permute-start(bf16[2,64,256]{2,1,0:T(8,128)(2,1)S(1)} %get-tuple-element.40), channel_id=1, source_target_pairs={{0,4},{1,5},{2,6},{3,7},{4,0},{5,1},{6,2},{7,3},{8,12},{9,13},{10,... | collective-permute-start | bytes 196616 | tf_op jit(solution)/shard_map/ppermute | solution.py:172
  31.4 0.0 collective-permute-done.7.refs_1_
  31.4 2.4 %collective-permute-start.5 = (bf16[2,64,256]{2,1,0:T(8,128)(2,1)S(1)}, bf16[2,64,256]{2,1,0:T(8,128)(2,1)S(1)}, u32[]{:S(2)}, u32[]{:S(2)}) collective-permute-start(bf16[2,64,256]{2,1,0:T(8,128)(2,1)S(1)} %get-tuple-element.34), channel_id=1, source_target_pairs={{0,5},{1,4},{2,7},{3,6},{4,1},{5,0},{6,3},{7,2},{8,13},{9,12},{10,... | collective-permute-start | bytes 196616 | tf_op jit(solution)/shard_map/ppermute | solution.py:172
  33.8 0.0 collective-permute-done.8.refs_2_
  33.8 1.0 %collective-permute-start.6 = (bf16[2,64,256]{2,1,0:T(8,128)(2,1)S(1)}, bf16[2,64,256]{2,1,0:T(8,128)(2,1)S(1)}, u32[]{:S(2)}, u32[]{:S(2)}) collective-permute-start(bf16[2,64,256]{2,1,0:T(8,128)(2,1)S(1)} %get-tuple-element.35), channel_id=1, source_target_pairs={{0,7},{1,6},{2,5},{3,4},{4,3},{5,2},{6,1},{7,0},{8,15},{9,14},{10,... | collective-permute-start | bytes 196616 | tf_op jit(solution)/shard_map/ppermute | solution.py:172
  34.8 0.1 all-to-all-done
  34.8 2.6 %grow_inner.1.refs_5_ = bf16[1,64,128,256]{3,2,1,0:T(8,128)(2,1)} custom-call(bf16[16,64,256]{2,1,0:T(8,128)(2,1)} %bitcast.4.refs_0_), custom_call_target="tpu_custom_call" | custom-call | bytes 2097152 | tf_op jit(solution)/shard_map/grow_inner/pallas_call | solution.py:151
  37.4 0.0 collective-permute-done.9.refs_3_
  37.4 4.2 %collective-permute-done.10.refs_4_ = bf16[2,64,256]{2,1,0:T(8,128)(2,1)S(1)} collective-permute-done((bf16[2,64,256]{2,1,0:T(8,128)(2,1)S(1)}, bf16[2,64,256]{2,1,0:T(8,128)(2,1)S(1)}, u32[]{:S(2)}, u32[]{:S(2)}) %collective-permute-start.10) | collective-permute-done | bytes 65568 | tf_op jit(solution)/shard_map/ppermute | solution.py:172
  41.7 1.3 %grow_first.1.refs_3_ = bf16[1,64,128,256]{3,2,1,0:T(8,128)(2,1)} custom-call(bf16[2,64,256]{2,1,0:T(8,128)(2,1)S(1)} %get-tuple-element.36.refs_0_, bf16[2,64,256]{2,1,0:T(8,128)(2,1)S(1)} %collective-permute-done.7.refs_1_, bf16[2,64,256]{2,1,0:T(8,128)(2,1)S(1)} %collective-permute-done.8.refs_2_, ...), custom_call_target="tpu_custom_call", output_to_operand_aliasing={{}: (5, {})} | custom-call | bytes 1310720 | tf_op jit(solution)/shard_map/grow_first/pallas_call | solution.py:151
  43.0 0.0 collective-permute-done.4.refs_0_
  43.0 0.7 %collective-permute-done.5.refs_1_ = bf16[2,64,256]{2,1,0:T(8,128)(2,1)S(1)} collective-permute-done((bf16[2,64,256]{2,1,0:T(8,128)(2,1)S(1)}, bf16[2,64,256]{2,1,0:T(8,128)(2,1)S(1)}, u32[]{:S(2)}, u32[]{:S(2)}) %collective-permute-start.5) | collective-permute-done | bytes 65568 | tf_op jit(solution)/shard_map/ppermute | solution.py:172
  43.7 0.0 collective-permute-done.6.refs_2_
  43.7 1.1 %grow_last.1 = bf16[1,64,128,256]{3,2,1,0:T(8,128)(2,1)} custom-call(bf16[2,64,256]{2,1,0:T(8,128)(2,1)S(1)} %collective-permute-done.4.refs_0_, bf16[2,64,256]{2,1,0:T(8,128)(2,1)S(1)} %collective-permute-done.5.refs_1_, bf16[2,64,256]{2,1,0:T(8,128)(2,1)S(1)} %collective-permute-done.6.refs_2_, ...), custom_call_target="tpu_custom_call", output_to_operand_aliasing={{}: (3, {})} | custom-call | bytes 786432 | tf_op jit(solution)/shard_map/grow_last/pallas_call | solution.py:151
  (2 shorter events, 0.0 us)
Async XLA Ops:
  1.1 9.9 %collective-permute-start = (bf16[2,4,64,256]{3,2,1,0:T(8,128)(2,1)S(1)}, bf16[2,4,64,256]{3,2,1,0:T(8,128)(2,1)S(1)}, u32[]{:S(2)}, u32[]{:S(2)}) collective-permute-start(bf16[2,4,64,256]{3,2,1,0:T(8,128)(2,1)S(1)} %get-tuple-element.24), channel_id=1, source_target_pairs={{0,8},{8,16},{16,24},{24,0},{1,9},{9,17},{17,25},{25,1},{2,10},{10... | collective-permute-start | bytes 786440 | tf_op jit(solution)/shard_map/ppermute | solution.py:177
  1.6 15.5 %collective-permute-start.1 = (bf16[8,64,256]{2,1,0:T(8,128)(2,1)S(1)}, bf16[8,64,256]{2,1,0:T(8,128)(2,1)S(1)}, u32[]{:S(2)}, u32[]{:S(2)}) collective-permute-start(bf16[8,64,256]{2,1,0:T(8,128)(2,1)S(1)} %get-tuple-element.25), channel_id=1, source_target_pairs={{0,1},{1,0},{2,3},{3,2},{4,5},{5,4},{6,7},{7,6},{8,9},{9,8},{10,11... | collective-permute-start | bytes 786440 | tf_op jit(solution)/shard_map/ppermute | solution.py:172
  4.2 12.9 %collective-permute-start.2 = (bf16[8,64,256]{2,1,0:T(8,128)(2,1)S(1)}, bf16[8,64,256]{2,1,0:T(8,128)(2,1)S(1)}, u32[]{:S(2)}, u32[]{:S(2)}) collective-permute-start(bf16[8,64,256]{2,1,0:T(8,128)(2,1)S(1)} %get-tuple-element.26), channel_id=1, source_target_pairs={{0,7},{1,2},{2,1},{3,4},{4,3},{5,6},{6,5},{7,0},{8,15},{9,10},{10,... | collective-permute-start | bytes 786440 | tf_op jit(solution)/shard_map/ppermute | solution.py:183
  13.0 21.9 %all-to-all-start = ((bf16[8,2,64,256]{3,2,1,0:T(8,128)(2,1)}), bf16[8,2,64,256]{3,2,1,0:T(8,128)(2,1)}, u32[]{:S(2)}, u32[]{:S(2)}) async-start(bf16[8,2,64,256]{3,2,1,0:T(8,128)(2,1)} %inner_mix.1), calls=%async_computation | async-start | bytes 1048576 | tf_op jit(solution)/shard_map/all_to_all | solution.py:237
  17.2 4.4 %collective-permute-start.3 = (bf16[2,2,64,256]{3,2,1,0:T(8,128)(2,1)S(1)}, bf16[2,2,64,256]{3,2,1,0:T(8,128)(2,1)S(1)}, u32[]{:S(2)}, u32[]{:S(2)}) collective-permute-start(bf16[2,2,64,256]{3,2,1,0:T(8,128)(2,1)S(1)} %pad_maximum_fusion), channel_id=1, source_target_pairs={{0,8},{8,16},{16,24},{24,0},{1,9},{9,17},{17,25},{25,1},{2,10},{10... | collective-permute-start | bytes 393224 | tf_op jit(solution)/shard_map/ppermute | solution.py:177
  23.6 7.8 %collective-permute-start.7 = (bf16[2,64,256]{2,1,0:T(8,128)(2,1)S(1)}, bf16[2,64,256]{2,1,0:T(8,128)(2,1)S(1)}, u32[]{:S(2)}, u32[]{:S(2)}) collective-permute-start(bf16[2,64,256]{2,1,0:T(8,128)(2,1)S(1)} %get-tuple-element.37), channel_id=1, source_target_pairs={{0,1},{1,0},{2,3},{3,2},{4,5},{5,4},{6,7},{7,6},{8,9},{9,8},{10,11... | collective-permute-start | bytes 196616 | tf_op jit(solution)/shard_map/ppermute | solution.py:172
  25.6 8.3 %collective-permute-start.8 = (bf16[2,64,256]{2,1,0:T(8,128)(2,1)S(1)}, bf16[2,64,256]{2,1,0:T(8,128)(2,1)S(1)}, u32[]{:S(2)}, u32[]{:S(2)}) collective-permute-start(bf16[2,64,256]{2,1,0:T(8,128)(2,1)S(1)} %get-tuple-element.38), channel_id=1, source_target_pairs={{0,2},{1,3},{2,0},{3,1},{4,6},{5,7},{6,4},{7,5},{8,10},{9,11},{10,... | collective-permute-start | bytes 196616 | tf_op jit(solution)/shard_map/ppermute | solution.py:172
  27.0 15.9 %collective-permute-start.4 = (bf16[2,64,256]{2,1,0:T(8,128)(2,1)S(1)}, bf16[2,64,256]{2,1,0:T(8,128)(2,1)S(1)}, u32[]{:S(2)}, u32[]{:S(2)}) collective-permute-start(bf16[2,64,256]{2,1,0:T(8,128)(2,1)S(1)} %get-tuple-element.33), channel_id=1, source_target_pairs={{0,6},{1,7},{2,4},{3,5},{4,2},{5,3},{6,0},{7,1},{8,14},{9,15},{10,... | collective-permute-start | bytes 196616 | tf_op jit(solution)/shard_map/ppermute | solution.py:172
  29.4 8.0 %collective-permute-start.9 = (bf16[2,64,256]{2,1,0:T(8,128)(2,1)S(1)}, bf16[2,64,256]{2,1,0:T(8,128)(2,1)S(1)}, u32[]{:S(2)}, u32[]{:S(2)}) collective-permute-start(bf16[2,64,256]{2,1,0:T(8,128)(2,1)S(1)} %get-tuple-element.39), channel_id=1, source_target_pairs={{0,3},{1,2},{2,1},{3,0},{4,7},{5,6},{6,5},{7,4},{8,11},{9,10},{10,... | collective-permute-start | bytes 196616 | tf_op jit(solution)/shard_map/ppermute | solution.py:172
  30.0 11.7 %collective-permute-start.10 = (bf16[2,64,256]{2,1,0:T(8,128)(2,1)S(1)}, bf16[2,64,256]{2,1,0:T(8,128)(2,1)S(1)}, u32[]{:S(2)}, u32[]{:S(2)}) collective-permute-start(bf16[2,64,256]{2,1,0:T(8,128)(2,1)S(1)} %get-tuple-element.40), channel_id=1, source_target_pairs={{0,4},{1,5},{2,6},{3,7},{4,0},{5,1},{6,2},{7,3},{8,12},{9,13},{10,... | collective-permute-start | bytes 196616 | tf_op jit(solution)/shard_map/ppermute | solution.py:172
  31.4 12.3 %collective-permute-start.5 = (bf16[2,64,256]{2,1,0:T(8,128)(2,1)S(1)}, bf16[2,64,256]{2,1,0:T(8,128)(2,1)S(1)}, u32[]{:S(2)}, u32[]{:S(2)}) collective-permute-start(bf16[2,64,256]{2,1,0:T(8,128)(2,1)S(1)} %get-tuple-element.34), channel_id=1, source_target_pairs={{0,5},{1,4},{2,7},{3,6},{4,1},{5,0},{6,3},{7,2},{8,13},{9,12},{10,... | collective-permute-start | bytes 196616 | tf_op jit(solution)/shard_map/ppermute | solution.py:172
  33.8 9.9 %collective-permute-start.6 = (bf16[2,64,256]{2,1,0:T(8,128)(2,1)S(1)}, bf16[2,64,256]{2,1,0:T(8,128)(2,1)S(1)}, u32[]{:S(2)}, u32[]{:S(2)}) collective-permute-start(bf16[2,64,256]{2,1,0:T(8,128)(2,1)S(1)} %get-tuple-element.35), channel_id=1, source_target_pairs={{0,7},{1,6},{2,5},{3,4},{4,3},{5,2},{6,1},{7,0},{8,15},{9,14},{10,... | collective-permute-start | bytes 196616 | tf_op jit(solution)/shard_map/ppermute | solution.py:172

commit v4 on v3

--- a/solution.py
+++ b/solution.py
@@ -19,7 +19,7 @@
 
 def exchanges(n):
     half = n // 2
-    return list(range(1, half)) + sorted(range(half, n), key=lambda k: (k & 1, k))
+    return list(range(2, half)) + sorted(range(half, n), key=lambda k: (k & 1, k)) + [1]
 
 
 def copy_all(pairs, sems):
@@ -92,22 +92,22 @@
     return jnp.where(inside, halo, jnp.zeros_like(halo))
 
 
-def edge_kernel(latent, near, far, sw, sb, hidden):
+def edge_kernel(latent, near, far, sw, sb, tw, hidden, tw_v, sem):
+    copy = pltpu.make_async_copy(tw, tw_v, sem)
+    copy.start()
     for i, (halo, (r, beyond, _, order)) in enumerate(zip((near, far), sides(latent.shape[1]))):
         hidden[i] = activate([outside(i, halo[...]), latent[:, r], latent[:, beyond]], order, sw, sb[...])
-
-
-def join_kernel(steps, latent, prev, corners, hidden, sw, sb, tw_hbm, tb, *rest):
-    outs, mixed, tw, sem = rest[:-3], *rest[-3:]
-    copy = pltpu.make_async_copy(tw_hbm, tw, sem)
-    copy.start()
+    copy.wait()
+
+
+def join_kernel(steps, latent, prev, corners, hidden, sw, sb, tw, tb, *rest):
+    outs, mixed = rest[:-1], rest[-1]
     rows = latent.shape[1]
     me = lax.axis_index("space")
     before = [
         activate([outside(i, corners[i]), prev[:, r], prev[:, beyond]], order, sw, sb[...])
         for i, (r, beyond, _, order) in enumerate(sides(rows))
     ]
-    copy.wait()
     for i, (r, _, place, _) in enumerate(sides(rows)):
         mixed[:, place] = mix(before[i], hidden[i], latent[:, r], tw, tb[...])
     for k, out in zip(steps, outs):
@@ -178,9 +178,13 @@
 
 
 def beside(block):
-    n = lax.axis_size("space")
-    route = [(s, (s + 1 if s % 2 else s - 1) % n) for s in range(n)]
-    return lax.ppermute(block, "space", route)
+    ts, n = lax.axis_size("tm"), lax.axis_size("space")
+    route = []
+    for t in range(ts):
+        for s in range(n):
+            to = (t ^ 1 if t ^ 1 < ts else t, s) if s in (0, n - 1) else (t, s + 1 if s % 2 else s - 1)
+            route.append((t * n + s, to[0] * n + to[1]))
+    return lax.ppermute(block, ("tm", "space"), route)
 
 
 def body(latent, spatial_weight, spatial_bias, temporal_weight, temporal_bias):
@@ -238,29 +242,26 @@
 
     near, far, token = lax.optimization_barrier((near, far, inner_own))
     corners = ahead(jnp.stack([near[frames - 2 :], far[frames - 2 :]]))
-    hidden = pl.pallas_call(
+    hidden, tw = pl.pallas_call(
         edge_kernel,
-        out_shape=bf16(2, frames, cols, chans),
-        in_specs=[VMEM] * 5,
-        out_specs=VMEM,
+        out_shape=[bf16(2, frames, cols, chans), bf16(*temporal_weight.shape)],
+        in_specs=[VMEM] * 5 + [HBM],
+        out_specs=[VMEM] * 2,
+        scratch_shapes=[pltpu.SemaphoreType.DMA],
         compiler_params=PARAMS,
         cost_estimate=cost(frames * 2 * cols, 9, chans),
         name="edge",
-    )(latent, near, far, *params[:2])
+    )(latent, near, far, *params[:2], args[3])
     edges = pl.pallas_call(
         lambda *refs: join_kernel([0] + steps, *refs),
         out_shape=[bf16(2, cols, chans)] * n,
-        in_specs=[VMEM] * 6 + [HBM, VMEM],
+        in_specs=[VMEM] * 8,
         out_specs=[VMEM] * n,
-        scratch_shapes=[
-            pltpu.VMEM((frames, 2, cols, chans), BF16),
-            pltpu.VMEM(temporal_weight.shape, BF16),
-            pltpu.SemaphoreType.DMA,
-        ],
+        scratch_shapes=[pltpu.VMEM((frames, 2, cols, chans), BF16)],
         compiler_params=PARAMS,
         cost_estimate=cost(frames * 2 * cols, 6, chans),
         name="join",
-    )(latent, prev, corners, hidden, *params[:2], args[3], params[3])
+    )(latent, prev, corners, hidden, *params[:2], tw, params[3])
     edges = [edges[0]] + [swap(edge, k) for k, edge in zip(steps, edges[1:])]
 
     out = grow([(s, None, [(1, rows - 2)]) for s in range(n)], [pltpu.with_memory_space_constraint(inner, pltpu.HBM)], None, rows * n, "grow_inner")

time: 45.1 us -> 43.2 us (0.958)
  waiting for transfers between devices: 6.88 us -> 5.32 us
  Pallas kernels: 14.7 us -> 13.9 us
  starting transfers between devices: 23 us -> 23.5 us
    ppermute x1, starting transfers between devices: 3.57 us -> 1.28 us  [beside(): return lax.ppermute(block, ('tm', 'space'), route)]
    ppermute x8, starting transfers between devices: 13.7 us -> 15.7 us  [swap(): lax.ppermute(block, 'space', [(i, i ^ k) for i in range(lax.axis_size('sp...]
    ppermute x8, waiting for transfers between devices: 4.93 us -> 3 us  [swap(): lax.ppermute(block, 'space', [(i, i ^ k) for i in range(lax.axis_size('sp...]
    all_to_all x1, starting transfers between devices: 4.15 us -> 5.49 us  [body(): lax.all_to_all(inner, 'space', split_axis=0, concat_axis=1, tiled=True)[0]]
    pallas_call x1, Pallas kernels: 1.99 us -> 1.04 us  [body(): pl.pallas_call(lambda *refs: join_kernel([0] + steps, *refs), out_shape=[...]
    ppermute x2, starting transfers between devices: 1.55 us -> 1.03 us  [ahead(): return lax.ppermute(block, 'tm', [(t, (t + 1) % n) for t in range(n)])]
  transfers between devices with their start and end apart: 12 -> 12, of which waited for: 4 -> 2; matrix products, arithmetic and copies ran while one was open for 0% -> 0% of each run, Pallas kernels for 28% -> 27%
where the time goes in v4:
time: 43.2 us; the launch traced here: 42.9 us
  starting transfers between devices  23.5 us (54%)
  Pallas kernels  13.9 us (32%)
  waiting for transfers between devices  5.32 us (12%)
    ppermute x8, starting transfers between devices, swap(): lax.ppermute(block, 'space', [(i, i ^ k) for i in range(lax.axis_size('sp...  15.7 us
    all_to_all x1, starting transfers between devices, body(): lax.all_to_all(inner, 'space', split_axis=0, concat_axis=1, tiled=True)[0]  5.49 us
    pallas_call x3, Pallas kernels, grow(): pl.pallas_call(lambda *refs: grow_kernel(plan, refs[:m], *refs[m + len(ex...  4.97 us
    ppermute x8, waiting for transfers between devices, swap(): lax.ppermute(block, 'space', [(i, i ^ k) for i in range(lax.axis_size('sp...  3 us
    ppermute x2, waiting for transfers between devices, ahead(): return lax.ppermute(block, 'tm', [(t, (t + 1) % n) for t in range(n)])  2.32 us
    pallas_call x1, Pallas kernels, body(): pl.pallas_call(inner_mix_kernel, out_shape=bf16(frames, rows - 2, cols, c...  1.91 us
    pallas_call x1, Pallas kernels, body(): pl.pallas_call(load_kernel, out_shape=[jax.ShapeDtypeStruct(a.shape, a.dt...  1.73 us
    pallas_call x1, Pallas kernels, body(): pl.pallas_call(edge_kernel, out_shape=[bf16(2, frames, cols, chans), bf16...  1.59 us
  transfers between devices with their start and end apart: 12, of which 2 were waited for; matrix products, arithmetic and copies ran while one was open for 0% of the time, Pallas kernels for 27%

profile of v4, /device:TPU:0, one launch (start us, length us, event | category | flops | bytes accessed | tf_op | source)
XLA Modules:
  0.0 42.9 jit_solution(9749597838403121364)
XLA Ops:
  0.0 1.1 %border.1 = (bf16[8,64,256]{2,1,0:T(8,128)(2,1)S(1)}, bf16[8,64,256]{2,1,0:T(8,128)(2,1)S(1)}, bf16[2,4,64,256]{3,2,1,0:T(8,128)(2,1)S(1)}) custom-call(bf16[8,4,64,256]{3,2,1,0:T(8,128)(2,1)} %latent.1), custom_call_target="tpu_custom_call" | custom-call | tf_op jit(solution)/shard_map/border/pallas_call | solution.py:199
  1.1 0.5 %collective-permute-start = (bf16[2,4,64,256]{3,2,1,0:T(8,128)(2,1)S(1)}, bf16[2,4,64,256]{3,2,1,0:T(8,128)(2,1)S(1)}, u32[]{:S(2)}, u32[]{:S(2)}) collective-permute-start(bf16[2,4,64,256]{3,2,1,0:T(8,128)(2,1)S(1)} %get-tuple-element.26), channel_id=1, source_target_pairs={{0,8},{8,16},{16,24},{24,0},{1,9},{9,17},{17,25},{25,1},{2,10},{10... | collective-permute-start | bytes 786440 | tf_op jit(solution)/shard_map/ppermute | solution.py:177
  1.6 2.6 %collective-permute-start.1 = (bf16[8,64,256]{2,1,0:T(8,128)(2,1)S(1)}, bf16[8,64,256]{2,1,0:T(8,128)(2,1)S(1)}, u32[]{:S(2)}, u32[]{:S(2)}) collective-permute-start(bf16[8,64,256]{2,1,0:T(8,128)(2,1)S(1)} %get-tuple-element.27), channel_id=1, source_target_pairs={{0,1},{1,0},{2,3},{3,2},{4,5},{5,4},{6,7},{7,6},{8,9},{9,8},{10,11... | collective-permute-start | bytes 786440 | tf_op jit(solution)/shard_map/ppermute | solution.py:172
  4.2 1.3 %collective-permute-start.2 = (bf16[8,64,256]{2,1,0:T(8,128)(2,1)S(1)}, bf16[8,64,256]{2,1,0:T(8,128)(2,1)S(1)}, u32[]{:S(2)}, u32[]{:S(2)}) collective-permute-start(bf16[8,64,256]{2,1,0:T(8,128)(2,1)S(1)} %get-tuple-element.28), channel_id=1, source_target_pairs={{0,8},{1,2},{2,1},{3,4},{4,3},{5,6},{6,5},{7,15},{8,0},{9,10},{10,... | collective-permute-start | bytes 786440 | tf_op jit(solution)/shard_map/ppermute | solution.py:187
  5.5 1.7 %load.1 = (bf16[8,4,64,256]{3,2,1,0:T(8,128)(2,1)S(1)}, bf16[3,3,256,256]{3,2,1,0:T(8,128)(2,1)S(1)}, f32[1,256]{1,0:T(1,128)S(1)}, bf16[3,256,256]{2,1,0:T(8,128)(2,1)S(1)}, f32[1,256]{1,0:T(1,128)S(1)}) custom-call(bf16[8,4,64,256]{3,2,1,0:T(8,128)(2,1)} %latent.1, bf16[3,3,256,256]{3,2,1,0:T(8,128)(2,1)} %refs_1_.1, f32[1,256]{1,0:T(1,128)} %bitcast.7, ...), custom_call_target="tpu_custom_call" | custom-call | bytes 5242880 | tf_op jit(solution)/shard_map/load/pallas_call | solution.py:211
  7.2 1.5 %inner.1.hidden = bf16[2,8,64,256]{3,2,1,0:T(8,128)(2,1)S(1)} custom-call(bf16[8,4,64,256]{3,2,1,0:T(8,128)(2,1)S(1)} %get-tuple-element.25.latent.refs_0_, bf16[3,3,256,256]{3,2,1,0:T(8,128)(2,1)S(1)} %get-tuple-element.29.sw.refs_4_, f32[1,256]{1,0:T(1,128)S(1)} %get-tuple-element.30.sb.refs_5_), custom_call_target="tpu_custom_call" | custom-call | flops 1207959552 | bytes 2097152 | tf_op jit(solution)/shard_map/inner/pallas_call | solution.py:222
  8.7 0.0 collective-permute-done.prev.refs_1_
  8.7 1.9 %inner_mix.1 = bf16[8,2,64,256]{3,2,1,0:T(8,128)(2,1)} custom-call(bf16[8,4,64,256]{3,2,1,0:T(8,128)(2,1)S(1)} %get-tuple-element.25.latent.refs_0_, bf16[2,4,64,256]{3,2,1,0:T(8,128)(2,1)S(1)} %collective-permute-done.prev.refs_1_, bf16[2,8,64,256]{3,2,1,0:T(8,128)(2,1)S(1)} %inner.1.hidden, bf16[3,3,256,256]{3,2,1,0:T(8,128)(2,1)S(1)} %get-tuple-element.29.sw.refs_4_, ...), custom_call_target="tpu_custom_call" | custom-call | flops 805306368 | bytes 2097152 | tf_op jit(solution)/shard_map/inner_mix/pallas_call | solution.py:231
  10.7 5.5 %all-to-all-start = ((bf16[8,2,64,256]{3,2,1,0:T(8,128)(2,1)}), bf16[8,2,64,256]{3,2,1,0:T(8,128)(2,1)}, u32[]{:S(2)}, u32[]{:S(2)}) async-start(bf16[8,2,64,256]{3,2,1,0:T(8,128)(2,1)} %inner_mix.1), calls=%async_computation | async-start | bytes 1048576 | tf_op jit(solution)/shard_map/all_to_all | solution.py:241
  16.2 0.0 collective-permute-done.1.near
  16.2 0.0 collective-permute-done.2.far
  16.2 0.5 %collective-permute-start.3 = (bf16[2,2,64,256]{3,2,1,0:T(8,128)(2,1)S(1)}, bf16[2,2,64,256]{3,2,1,0:T(8,128)(2,1)S(1)}, u32[]{:S(2)}, u32[]{:S(2)}) collective-permute-start(bf16[2,2,64,256]{3,2,1,0:T(8,128)(2,1)S(1)} %pad_maximum_fusion), channel_id=1, source_target_pairs={{0,8},{8,16},{16,24},{24,0},{1,9},{9,17},{17,25},{25,1},{2,10},{10... | collective-permute-start | bytes 393224 | tf_op jit(solution)/shard_map/ppermute | solution.py:177
  16.7 1.6 %edge.1 = (bf16[2,8,64,256]{3,2,1,0:T(8,128)(2,1)S(1)}, bf16[3,256,256]{2,1,0:T(8,128)(2,1)S(1)}) custom-call(bf16[8,4,64,256]{3,2,1,0:T(8,128)(2,1)S(1)} %get-tuple-element.25.latent.refs_0_, bf16[8,64,256]{2,1,0:T(8,128)(2,1)S(1)} %collective-permute-done.1.near, bf16[8,64,256]{2,1,0:T(8,128)(2,1)S(1)} %collective-permute-done.2.far, ...), custom_call_target="tpu_custom_call" | custom-call | flops 1207959552 | bytes 2097152 | tf_op jit(solution)/shard_map/edge/pallas_call | solution.py:245
  18.3 2.3 %collective-permute-done.3.refs_2_ = bf16[2,2,64,256]{3,2,1,0:T(8,128)(2,1)S(1)} collective-permute-done((bf16[2,2,64,256]{3,2,1,0:T(8,128)(2,1)S(1)}, bf16[2,2,64,256]{3,2,1,0:T(8,128)(2,1)S(1)}, u32[]{:S(2)}, u32[]{:S(2)}) %collective-permute-start.3) | collective-permute-done | bytes 131104 | tf_op jit(solution)/shard_map/ppermute | solution.py:177
  20.7 1.0 %join.1 = (bf16[2,64,256]{2,1,0:T(8,128)(2,1)S(1)}, bf16[2,64,256]{2,1,0:T(8,128)(2,1)S(1)}, bf16[2,64,256]{2,1,0:T(8,128)(2,1)S(1)}, bf16[2,64,256]{2,1,0:T(8,1...) custom-call(bf16[8,4,64,256]{3,2,1,0:T(8,128)(2,1)S(1)} %get-tuple-e, ...), custom_call_target="tpu_custom_call" | custom-call | flops 805306368 | bytes 2097152 | tf_op jit(solution)/shard_map/join/pallas_call | solution.py:255
  21.7 2.5 %collective-permute-start.7 = (bf16[2,64,256]{2,1,0:T(8,128)(2,1)S(1)}, bf16[2,64,256]{2,1,0:T(8,128)(2,1)S(1)}, u32[]{:S(2)}, u32[]{:S(2)}) collective-permute-start(bf16[2,64,256]{2,1,0:T(8,128)(2,1)S(1)} %get-tuple-element.41), channel_id=1, source_target_pairs={{0,2},{1,3},{2,0},{3,1},{4,6},{5,7},{6,4},{7,5},{8,10},{9,11},{10,... | collective-permute-start | bytes 196616 | tf_op jit(solution)/shard_map/ppermute | solution.py:172
  24.2 1.4 %collective-permute-start.8 = (bf16[2,64,256]{2,1,0:T(8,128)(2,1)S(1)}, bf16[2,64,256]{2,1,0:T(8,128)(2,1)S(1)}, u32[]{:S(2)}, u32[]{:S(2)}) collective-permute-start(bf16[2,64,256]{2,1,0:T(8,128)(2,1)S(1)} %get-tuple-element.42), channel_id=1, source_target_pairs={{0,3},{1,2},{2,1},{3,0},{4,7},{5,6},{6,5},{7,4},{8,11},{9,10},{10,... | collective-permute-start | bytes 196616 | tf_op jit(solution)/shard_map/ppermute | solution.py:172
  25.6 2.6 %collective-permute-start.4 = (bf16[2,64,256]{2,1,0:T(8,128)(2,1)S(1)}, bf16[2,64,256]{2,1,0:T(8,128)(2,1)S(1)}, u32[]{:S(2)}, u32[]{:S(2)}) collective-permute-start(bf16[2,64,256]{2,1,0:T(8,128)(2,1)S(1)} %get-tuple-element.37), channel_id=1, source_target_pairs={{0,5},{1,4},{2,7},{3,6},{4,1},{5,0},{6,3},{7,2},{8,13},{9,12},{10,... | collective-permute-start | bytes 196616 | tf_op jit(solution)/shard_map/ppermute | solution.py:172
  28.1 0.0 collective-permute-start.9
  28.1 3.9 %collective-permute-start.10 = (bf16[2,64,256]{2,1,0:T(8,128)(2,1)S(1)}, bf16[2,64,256]{2,1,0:T(8,128)(2,1)S(1)}, u32[]{:S(2)}, u32[]{:S(2)}) collective-permute-start(bf16[2,64,256]{2,1,0:T(8,128)(2,1)S(1)} %get-tuple-element.44), channel_id=1, source_target_pairs={{0,6},{1,7},{2,4},{3,5},{4,2},{5,3},{6,0},{7,1},{8,14},{9,15},{10,... | collective-permute-start | bytes 196616 | tf_op jit(solution)/shard_map/ppermute | solution.py:172
  32.0 0.0 collective-permute-done.7.refs_1_
  32.1 1.1 %collective-permute-start.5 = (bf16[2,64,256]{2,1,0:T(8,128)(2,1)S(1)}, bf16[2,64,256]{2,1,0:T(8,128)(2,1)S(1)}, u32[]{:S(2)}, u32[]{:S(2)}) collective-permute-start(bf16[2,64,256]{2,1,0:T(8,128)(2,1)S(1)} %get-tuple-element.38), channel_id=1, source_target_pairs={{0,7},{1,6},{2,5},{3,4},{4,3},{5,2},{6,1},{7,0},{8,15},{9,14},{10,... | collective-permute-start | bytes 196616 | tf_op jit(solution)/shard_map/ppermute | solution.py:172
  33.2 0.0 collective-permute-done.8.refs_2_
  33.2 1.7 %collective-permute-start.6 = (bf16[2,64,256]{2,1,0:T(8,128)(2,1)S(1)}, bf16[2,64,256]{2,1,0:T(8,128)(2,1)S(1)}, u32[]{:S(2)}, u32[]{:S(2)}) collective-permute-start(bf16[2,64,256]{2,1,0:T(8,128)(2,1)S(1)} %get-tuple-element.39), channel_id=1, source_target_pairs={{0,1},{1,0},{2,3},{3,2},{4,5},{5,4},{6,7},{7,6},{8,9},{9,8},{10,11... | collective-permute-start | bytes 196616 | tf_op jit(solution)/shard_map/ppermute | solution.py:172
  34.9 0.0 all-to-all-done
  34.9 2.6 %grow_inner.1.refs_5_ = bf16[1,64,128,256]{3,2,1,0:T(8,128)(2,1)} custom-call(bf16[16,64,256]{2,1,0:T(8,128)(2,1)} %bitcast.4.refs_0_), custom_call_target="tpu_custom_call" | custom-call | bytes 2097152 | tf_op jit(solution)/shard_map/grow_inner/pallas_call | solution.py:151
  37.5 3.0 %collective-permute-done.9.refs_3_ = bf16[2,64,256]{2,1,0:T(8,128)(2,1)S(1)} collective-permute-done((bf16[2,64,256]{2,1,0:T(8,128)(2,1)S(1)}, bf16[2,64,256]{2,1,0:T(8,128)(2,1)S(1)}, u32[]{:S(2)}, u32[]{:S(2)}) %collective-permute-start.9) | collective-permute-done | bytes 65568 | tf_op jit(solution)/shard_map/ppermute | solution.py:172
  40.4 0.0 collective-permute-done.10.refs_4_
  40.4 1.3 %grow_first.1.refs_3_ = bf16[1,64,128,256]{3,2,1,0:T(8,128)(2,1)} custom-call(bf16[2,64,256]{2,1,0:T(8,128)(2,1)S(1)} %get-tuple-element.40.refs_0_, bf16[2,64,256]{2,1,0:T(8,128)(2,1)S(1)} %collective-permute-done.7.refs_1_, bf16[2,64,256]{2,1,0:T(8,128)(2,1)S(1)} %collective-permute-done.8.refs_2_, ...), custom_call_target="tpu_custom_call", output_to_operand_aliasing={{}: (5, {})} | custom-call | bytes 1310720 | tf_op jit(solution)/shard_map/grow_first/pallas_call | solution.py:151
  41.7 0.0 collective-permute-done.4.refs_0_
  41.8 0.0 collective-permute-done.5.refs_1_
  41.8 0.0 collective-permute-done.6.refs_2_
  41.8 1.1 %grow_last.1 = bf16[1,64,128,256]{3,2,1,0:T(8,128)(2,1)} custom-call(bf16[2,64,256]{2,1,0:T(8,128)(2,1)S(1)} %collective-permute-done.4.refs_0_, bf16[2,64,256]{2,1,0:T(8,128)(2,1)S(1)} %collective-permute-done.5.refs_1_, bf16[2,64,256]{2,1,0:T(8,128)(2,1)S(1)} %collective-permute-done.6.refs_2_, ...), custom_call_target="tpu_custom_call", output_to_operand_aliasing={{}: (3, {})} | custom-call | bytes 786432 | tf_op jit(solution)/shard_map/grow_last/pallas_call | solution.py:151
  (2 shorter events, 0.0 us)
Async XLA Ops:
  1.1 7.6 %collective-permute-start = (bf16[2,4,64,256]{3,2,1,0:T(8,128)(2,1)S(1)}, bf16[2,4,64,256]{3,2,1,0:T(8,128)(2,1)S(1)}, u32[]{:S(2)}, u32[]{:S(2)}) collective-permute-start(bf16[2,4,64,256]{3,2,1,0:T(8,128)(2,1)S(1)} %get-tuple-element.26), channel_id=1, source_target_pairs={{0,8},{8,16},{16,24},{24,0},{1,9},{9,17},{17,25},{25,1},{2,10},{10... | collective-permute-start | bytes 786440 | tf_op jit(solution)/shard_map/ppermute | solution.py:177
  1.6 14.5 %collective-permute-start.1 = (bf16[8,64,256]{2,1,0:T(8,128)(2,1)S(1)}, bf16[8,64,256]{2,1,0:T(8,128)(2,1)S(1)}, u32[]{:S(2)}, u32[]{:S(2)}) collective-permute-start(bf16[8,64,256]{2,1,0:T(8,128)(2,1)S(1)} %get-tuple-element.27), channel_id=1, source_target_pairs={{0,1},{1,0},{2,3},{3,2},{4,5},{5,4},{6,7},{7,6},{8,9},{9,8},{10,11... | collective-permute-start | bytes 786440 | tf_op jit(solution)/shard_map/ppermute | solution.py:172
  4.2 11.9 %collective-permute-start.2 = (bf16[8,64,256]{2,1,0:T(8,128)(2,1)S(1)}, bf16[8,64,256]{2,1,0:T(8,128)(2,1)S(1)}, u32[]{:S(2)}, u32[]{:S(2)}) collective-permute-start(bf16[8,64,256]{2,1,0:T(8,128)(2,1)S(1)} %get-tuple-element.28), channel_id=1, source_target_pairs={{0,8},{1,2},{2,1},{3,4},{4,3},{5,6},{6,5},{7,15},{8,0},{9,10},{10,... | collective-permute-start | bytes 786440 | tf_op jit(solution)/shard_map/ppermute | solution.py:187
  10.7 24.2 %all-to-all-start = ((bf16[8,2,64,256]{3,2,1,0:T(8,128)(2,1)}), bf16[8,2,64,256]{3,2,1,0:T(8,128)(2,1)}, u32[]{:S(2)}, u32[]{:S(2)}) async-start(bf16[8,2,64,256]{3,2,1,0:T(8,128)(2,1)} %inner_mix.1), calls=%async_computation | async-start | bytes 1048576 | tf_op jit(solution)/shard_map/all_to_all | solution.py:241
  16.2 4.4 %collective-permute-start.3 = (bf16[2,2,64,256]{3,2,1,0:T(8,128)(2,1)S(1)}, bf16[2,2,64,256]{3,2,1,0:T(8,128)(2,1)S(1)}, u32[]{:S(2)}, u32[]{:S(2)}) collective-permute-start(bf16[2,2,64,256]{3,2,1,0:T(8,128)(2,1)S(1)} %pad_maximum_fusion), channel_id=1, source_target_pairs={{0,8},{8,16},{16,24},{24,0},{1,9},{9,17},{17,25},{25,1},{2,10},{10... | collective-permute-start | bytes 393224 | tf_op jit(solution)/shard_map/ppermute | solution.py:177
  21.7 10.3 %collective-permute-start.7 = (bf16[2,64,256]{2,1,0:T(8,128)(2,1)S(1)}, bf16[2,64,256]{2,1,0:T(8,128)(2,1)S(1)}, u32[]{:S(2)}, u32[]{:S(2)}) collective-permute-start(bf16[2,64,256]{2,1,0:T(8,128)(2,1)S(1)} %get-tuple-element.41), channel_id=1, source_target_pairs={{0,2},{1,3},{2,0},{3,1},{4,6},{5,7},{6,4},{7,5},{8,10},{9,11},{10,... | collective-permute-start | bytes 196616 | tf_op jit(solution)/shard_map/ppermute | solution.py:172
  24.2 9.0 %collective-permute-start.8 = (bf16[2,64,256]{2,1,0:T(8,128)(2,1)S(1)}, bf16[2,64,256]{2,1,0:T(8,128)(2,1)S(1)}, u32[]{:S(2)}, u32[]{:S(2)}) collective-permute-start(bf16[2,64,256]{2,1,0:T(8,128)(2,1)S(1)} %get-tuple-element.42), channel_id=1, source_target_pairs={{0,3},{1,2},{2,1},{3,0},{4,7},{5,6},{6,5},{7,4},{8,11},{9,10},{10,... | collective-permute-start | bytes 196616 | tf_op jit(solution)/shard_map/ppermute | solution.py:172
  25.6 16.2 %collective-permute-start.4 = (bf16[2,64,256]{2,1,0:T(8,128)(2,1)S(1)}, bf16[2,64,256]{2,1,0:T(8,128)(2,1)S(1)}, u32[]{:S(2)}, u32[]{:S(2)}) collective-permute-start(bf16[2,64,256]{2,1,0:T(8,128)(2,1)S(1)} %get-tuple-element.37), channel_id=1, source_target_pairs={{0,5},{1,4},{2,7},{3,6},{4,1},{5,0},{6,3},{7,2},{8,13},{9,12},{10,... | collective-permute-start | bytes 196616 | tf_op jit(solution)/shard_map/ppermute | solution.py:172
  28.1 12.3 %collective-permute-start.9 = (bf16[2,64,256]{2,1,0:T(8,128)(2,1)S(1)}, bf16[2,64,256]{2,1,0:T(8,128)(2,1)S(1)}, u32[]{:S(2)}, u32[]{:S(2)}) collective-permute-start(bf16[2,64,256]{2,1,0:T(8,128)(2,1)S(1)} %get-tuple-element.43), channel_id=1, source_target_pairs={{0,4},{1,5},{2,6},{3,7},{4,0},{5,1},{6,2},{7,3},{8,12},{9,13},{10,... | collective-permute-start | bytes 196616 | tf_op jit(solution)/shard_map/ppermute | solution.py:172
  28.1 12.3 %collective-permute-start.10 = (bf16[2,64,256]{2,1,0:T(8,128)(2,1)S(1)}, bf16[2,64,256]{2,1,0:T(8,128)(2,1)S(1)}, u32[]{:S(2)}, u32[]{:S(2)}) collective-permute-start(bf16[2,64,256]{2,1,0:T(8,128)(2,1)S(1)} %get-tuple-element.44), channel_id=1, source_target_pairs={{0,6},{1,7},{2,4},{3,5},{4,2},{5,3},{6,0},{7,1},{8,14},{9,15},{10,... | collective-permute-start | bytes 196616 | tf_op jit(solution)/shard_map/ppermute | solution.py:172
  32.1 9.7 %collective-permute-start.5 = (bf16[2,64,256]{2,1,0:T(8,128)(2,1)S(1)}, bf16[2,64,256]{2,1,0:T(8,128)(2,1)S(1)}, u32[]{:S(2)}, u32[]{:S(2)}) collective-permute-start(bf16[2,64,256]{2,1,0:T(8,128)(2,1)S(1)} %get-tuple-element.38), channel_id=1, source_target_pairs={{0,7},{1,6},{2,5},{3,4},{4,3},{5,2},{6,1},{7,0},{8,15},{9,14},{10,... | collective-permute-start | bytes 196616 | tf_op jit(solution)/shard_map/ppermute | solution.py:172
  33.2 8.6 %collective-permute-start.6 = (bf16[2,64,256]{2,1,0:T(8,128)(2,1)S(1)}, bf16[2,64,256]{2,1,0:T(8,128)(2,1)S(1)}, u32[]{:S(2)}, u32[]{:S(2)}) collective-permute-start(bf16[2,64,256]{2,1,0:T(8,128)(2,1)S(1)} %get-tuple-element.39), channel_id=1, source_target_pairs={{0,1},{1,0},{2,3},{3,2},{4,5},{5,4},{6,7},{7,6},{8,9},{9,8},{10,11... | collective-permute-start | bytes 196616 | tf_op jit(solution)/shard_map/ppermute | solution.py:172

commit v5 on v4

--- a/solution.py
+++ b/solution.py
@@ -19,7 +19,7 @@
 
 def exchanges(n):
     half = n // 2
-    return list(range(2, half)) + sorted(range(half, n), key=lambda k: (k & 1, k)) + [1]
+    return list(range(2, half)) + [k ^ 1 for k in range(half, n)] + [1]
 
 
 def copy_all(pairs, sems):
@@ -266,8 +266,9 @@
 
     out = grow([(s, None, [(1, rows - 2)]) for s in range(n)], [pltpu.with_memory_space_constraint(inner, pltpu.HBM)], None, rows * n, "grow_inner")
     ends = [(0, 1), (rows - 1, 1)]
-    out = grow([(None, k, ends) for k in [0] + steps[:n // 2]], edges[: n // 2 + 1], out, rows * n, "grow_first")
-    return grow([(None, k, ends) for k in steps[n // 2:]], edges[n // 2 + 1 :], out, rows * n, "grow_last")
+    cut = 2
+    out = grow([(None, k, ends) for k in [0] + steps[:cut]], edges[: cut + 1], out, rows * n, "grow_first")
+    return grow([(None, k, ends) for k in steps[cut:]], edges[cut + 1 :], out, rows * n, "grow_last")
 
 
 def solution(mesh):

time: 43.2 us -> 42.1 us (0.975)
  starting transfers between devices: 23.5 us -> 22.2 us
    ppermute x8, starting transfers between devices: 15.7 us -> 14.4 us  [swap(): lax.ppermute(block, 'space', [(i, i ^ k) for i in range(lax.axis_size('sp...]
  transfers between devices with their start and end apart: 12 -> 12, of which waited for: 2 -> 3; matrix products, arithmetic and copies ran while one was open for 0% -> 0% of each run, Pallas kernels for 27% -> 27%
where the time goes in v5:
time: 42.1 us; the launch traced here: 41.7 us
  starting transfers between devices  22.2 us (53%)
  Pallas kernels  13.9 us (33%)
  waiting for transfers between devices  5.49 us (13%)
    ppermute x8, starting transfers between devices, swap(): lax.ppermute(block, 'space', [(i, i ^ k) for i in range(lax.axis_size('sp...  14.4 us
    all_to_all x1, starting transfers between devices, body(): lax.all_to_all(inner, 'space', split_axis=0, concat_axis=1, tiled=True)[0]  5.49 us
    pallas_call x3, Pallas kernels, grow(): pl.pallas_call(lambda *refs: grow_kernel(plan, refs[:m], *refs[m + len(ex...  4.98 us
    ppermute x8, waiting for transfers between devices, swap(): lax.ppermute(block, 'space', [(i, i ^ k) for i in range(lax.axis_size('sp...  3.17 us
    ppermute x2, waiting for transfers between devices, ahead(): return lax.ppermute(block, 'tm', [(t, (t + 1) % n) for t in range(n)])  2.32 us
    pallas_call x1, Pallas kernels, body(): pl.pallas_call(inner_mix_kernel, out_shape=bf16(frames, rows - 2, cols, c...  1.91 us
    pallas_call x1, Pallas kernels, body(): pl.pallas_call(load_kernel, out_shape=[jax.ShapeDtypeStruct(a.shape, a.dt...  1.73 us
    pallas_call x1, Pallas kernels, body(): pl.pallas_call(edge_kernel, out_shape=[bf16(2, frames, cols, chans), bf16...  1.59 us
  transfers between devices with their start and end apart: 12, of which 3 were waited for; matrix products, arithmetic and copies ran while one was open for 0% of the time, Pallas kernels for 27%

profile of v5, /device:TPU:0, one launch (start us, length us, event | category | flops | bytes accessed | tf_op | source)
XLA Modules:
  0.0 41.7 jit_solution(1796124731563459785)
XLA Ops:
  0.0 1.1 %border.1 = (bf16[8,64,256]{2,1,0:T(8,128)(2,1)S(1)}, bf16[8,64,256]{2,1,0:T(8,128)(2,1)S(1)}, bf16[2,4,64,256]{3,2,1,0:T(8,128)(2,1)S(1)}) custom-call(bf16[8,4,64,256]{3,2,1,0:T(8,128)(2,1)} %latent.1), custom_call_target="tpu_custom_call" | custom-call | tf_op jit(solution)/shard_map/border/pallas_call | solution.py:199
  1.1 0.5 %collective-permute-start = (bf16[2,4,64,256]{3,2,1,0:T(8,128)(2,1)S(1)}, bf16[2,4,64,256]{3,2,1,0:T(8,128)(2,1)S(1)}, u32[]{:S(2)}, u32[]{:S(2)}) collective-permute-start(bf16[2,4,64,256]{3,2,1,0:T(8,128)(2,1)S(1)} %get-tuple-element.26), channel_id=1, source_target_pairs={{0,8},{8,16},{16,24},{24,0},{1,9},{9,17},{17,25},{25,1},{2,10},{10... | collective-permute-start | bytes 786440 | tf_op jit(solution)/shard_map/ppermute | solution.py:177
  1.6 2.6 %collective-permute-start.1 = (bf16[8,64,256]{2,1,0:T(8,128)(2,1)S(1)}, bf16[8,64,256]{2,1,0:T(8,128)(2,1)S(1)}, u32[]{:S(2)}, u32[]{:S(2)}) collective-permute-start(bf16[8,64,256]{2,1,0:T(8,128)(2,1)S(1)} %get-tuple-element.27), channel_id=1, source_target_pairs={{0,1},{1,0},{2,3},{3,2},{4,5},{5,4},{6,7},{7,6},{8,9},{9,8},{10,11... | collective-permute-start | bytes 786440 | tf_op jit(solution)/shard_map/ppermute | solution.py:172
  4.2 1.3 %collective-permute-start.2 = (bf16[8,64,256]{2,1,0:T(8,128)(2,1)S(1)}, bf16[8,64,256]{2,1,0:T(8,128)(2,1)S(1)}, u32[]{:S(2)}, u32[]{:S(2)}) collective-permute-start(bf16[8,64,256]{2,1,0:T(8,128)(2,1)S(1)} %get-tuple-element.28), channel_id=1, source_target_pairs={{0,8},{1,2},{2,1},{3,4},{4,3},{5,6},{6,5},{7,15},{8,0},{9,10},{10,... | collective-permute-start | bytes 786440 | tf_op jit(solution)/shard_map/ppermute | solution.py:187
  5.5 1.7 %load.1 = (bf16[8,4,64,256]{3,2,1,0:T(8,128)(2,1)S(1)}, bf16[3,3,256,256]{3,2,1,0:T(8,128)(2,1)S(1)}, f32[1,256]{1,0:T(1,128)S(1)}, bf16[3,256,256]{2,1,0:T(8,128)(2,1)S(1)}, f32[1,256]{1,0:T(1,128)S(1)}) custom-call(bf16[8,4,64,256]{3,2,1,0:T(8,128)(2,1)} %latent.1, bf16[3,3,256,256]{3,2,1,0:T(8,128)(2,1)} %refs_1_.1, f32[1,256]{1,0:T(1,128)} %bitcast.7, ...), custom_call_target="tpu_custom_call" | custom-call | bytes 5242880 | tf_op jit(solution)/shard_map/load/pallas_call | solution.py:211
  7.2 1.5 %inner.1.hidden = bf16[2,8,64,256]{3,2,1,0:T(8,128)(2,1)S(1)} custom-call(bf16[8,4,64,256]{3,2,1,0:T(8,128)(2,1)S(1)} %get-tuple-element.25.latent.refs_0_, bf16[3,3,256,256]{3,2,1,0:T(8,128)(2,1)S(1)} %get-tuple-element.29.sw.refs_4_, f32[1,256]{1,0:T(1,128)S(1)} %get-tuple-element.30.sb.refs_5_), custom_call_target="tpu_custom_call" | custom-call | flops 1207959552 | bytes 2097152 | tf_op jit(solution)/shard_map/inner/pallas_call | solution.py:222
  8.7 0.0 collective-permute-done.prev.refs_1_
  8.7 1.9 %inner_mix.1 = bf16[8,2,64,256]{3,2,1,0:T(8,128)(2,1)} custom-call(bf16[8,4,64,256]{3,2,1,0:T(8,128)(2,1)S(1)} %get-tuple-element.25.latent.refs_0_, bf16[2,4,64,256]{3,2,1,0:T(8,128)(2,1)S(1)} %collective-permute-done.prev.refs_1_, bf16[2,8,64,256]{3,2,1,0:T(8,128)(2,1)S(1)} %inner.1.hidden, bf16[3,3,256,256]{3,2,1,0:T(8,128)(2,1)S(1)} %get-tuple-element.29.sw.refs_4_, ...), custom_call_target="tpu_custom_call" | custom-call | flops 805306368 | bytes 2097152 | tf_op jit(solution)/shard_map/inner_mix/pallas_call | solution.py:231
  10.7 5.5 %all-to-all-start = ((bf16[8,2,64,256]{3,2,1,0:T(8,128)(2,1)}), bf16[8,2,64,256]{3,2,1,0:T(8,128)(2,1)}, u32[]{:S(2)}, u32[]{:S(2)}) async-start(bf16[8,2,64,256]{3,2,1,0:T(8,128)(2,1)} %inner_mix.1), calls=%async_computation | async-start | bytes 1048576 | tf_op jit(solution)/shard_map/all_to_all | solution.py:241
  16.2 0.0 collective-permute-done.1.near
  16.2 0.0 collective-permute-done.2.far
  16.2 0.5 %collective-permute-start.3 = (bf16[2,2,64,256]{3,2,1,0:T(8,128)(2,1)S(1)}, bf16[2,2,64,256]{3,2,1,0:T(8,128)(2,1)S(1)}, u32[]{:S(2)}, u32[]{:S(2)}) collective-permute-start(bf16[2,2,64,256]{3,2,1,0:T(8,128)(2,1)S(1)} %pad_maximum_fusion), channel_id=1, source_target_pairs={{0,8},{8,16},{16,24},{24,0},{1,9},{9,17},{17,25},{25,1},{2,10},{10... | collective-permute-start | bytes 393224 | tf_op jit(solution)/shard_map/ppermute | solution.py:177
  16.7 1.6 %edge.1 = (bf16[2,8,64,256]{3,2,1,0:T(8,128)(2,1)S(1)}, bf16[3,256,256]{2,1,0:T(8,128)(2,1)S(1)}) custom-call(bf16[8,4,64,256]{3,2,1,0:T(8,128)(2,1)S(1)} %get-tuple-element.25.latent.refs_0_, bf16[8,64,256]{2,1,0:T(8,128)(2,1)S(1)} %collective-permute-done.1.near, bf16[8,64,256]{2,1,0:T(8,128)(2,1)S(1)} %collective-permute-done.2.far, ...), custom_call_target="tpu_custom_call" | custom-call | flops 1207959552 | bytes 2097152 | tf_op jit(solution)/shard_map/edge/pallas_call | solution.py:245
  18.3 2.3 %collective-permute-done.3.refs_2_ = bf16[2,2,64,256]{3,2,1,0:T(8,128)(2,1)S(1)} collective-permute-done((bf16[2,2,64,256]{3,2,1,0:T(8,128)(2,1)S(1)}, bf16[2,2,64,256]{3,2,1,0:T(8,128)(2,1)S(1)}, u32[]{:S(2)}, u32[]{:S(2)}) %collective-permute-start.3) | collective-permute-done | bytes 131104 | tf_op jit(solution)/shard_map/ppermute | solution.py:177
  20.7 1.0 %join.1 = (bf16[2,64,256]{2,1,0:T(8,128)(2,1)S(1)}, bf16[2,64,256]{2,1,0:T(8,128)(2,1)S(1)}, bf16[2,64,256]{2,1,0:T(8,128)(2,1)S(1)}, bf16[2,64,256]{2,1,0:T(8,1...) custom-call(bf16[8,4,64,256]{3,2,1,0:T(8,128)(2,1)S(1)} %get-tuple-e, ...), custom_call_target="tpu_custom_call" | custom-call | flops 805306368 | bytes 2097152 | tf_op jit(solution)/shard_map/join/pallas_call | solution.py:255
  21.7 2.5 %collective-permute-start.9 = (bf16[2,64,256]{2,1,0:T(8,128)(2,1)S(1)}, bf16[2,64,256]{2,1,0:T(8,128)(2,1)S(1)}, u32[]{:S(2)}, u32[]{:S(2)}) collective-permute-start(bf16[2,64,256]{2,1,0:T(8,128)(2,1)S(1)} %get-tuple-element.43), channel_id=1, source_target_pairs={{0,2},{1,3},{2,0},{3,1},{4,6},{5,7},{6,4},{7,5},{8,10},{9,11},{10,... | collective-permute-start | bytes 196616 | tf_op jit(solution)/shard_map/ppermute | solution.py:172
  24.2 1.4 %collective-permute-start.10 = (bf16[2,64,256]{2,1,0:T(8,128)(2,1)S(1)}, bf16[2,64,256]{2,1,0:T(8,128)(2,1)S(1)}, u32[]{:S(2)}, u32[]{:S(2)}) collective-permute-start(bf16[2,64,256]{2,1,0:T(8,128)(2,1)S(1)} %get-tuple-element.44), channel_id=1, source_target_pairs={{0,3},{1,2},{2,1},{3,0},{4,7},{5,6},{6,5},{7,4},{8,11},{9,10},{10,... | collective-permute-start | bytes 196616 | tf_op jit(solution)/shard_map/ppermute | solution.py:172
  25.6 2.6 %collective-permute-start.4 = (bf16[2,64,256]{2,1,0:T(8,128)(2,1)S(1)}, bf16[2,64,256]{2,1,0:T(8,128)(2,1)S(1)}, u32[]{:S(2)}, u32[]{:S(2)}) collective-permute-start(bf16[2,64,256]{2,1,0:T(8,128)(2,1)S(1)} %get-tuple-element.37), channel_id=1, source_target_pairs={{0,5},{1,4},{2,7},{3,6},{4,1},{5,0},{6,3},{7,2},{8,13},{9,12},{10,... | collective-permute-start | bytes 196616 | tf_op jit(solution)/shard_map/ppermute | solution.py:172
  28.1 0.0 collective-permute-start.5
  28.1 4.2 %collective-permute-start.6 = (bf16[2,64,256]{2,1,0:T(8,128)(2,1)S(1)}, bf16[2,64,256]{2,1,0:T(8,128)(2,1)S(1)}, u32[]{:S(2)}, u32[]{:S(2)}) collective-permute-start(bf16[2,64,256]{2,1,0:T(8,128)(2,1)S(1)} %get-tuple-element.39), channel_id=1, source_target_pairs={{0,7},{1,6},{2,5},{3,4},{4,3},{5,2},{6,1},{7,0},{8,15},{9,14},{10,... | collective-permute-start | bytes 196616 | tf_op jit(solution)/shard_map/ppermute | solution.py:172
  32.3 0.0 collective-permute-done.9.refs_1_
  32.3 1.1 %collective-permute-start.7 = (bf16[2,64,256]{2,1,0:T(8,128)(2,1)S(1)}, bf16[2,64,256]{2,1,0:T(8,128)(2,1)S(1)}, u32[]{:S(2)}, u32[]{:S(2)}) collective-permute-start(bf16[2,64,256]{2,1,0:T(8,128)(2,1)S(1)} %get-tuple-element.40), channel_id=1, source_target_pairs={{0,6},{1,7},{2,4},{3,5},{4,2},{5,3},{6,0},{7,1},{8,14},{9,15},{10,... | collective-permute-start | bytes 196616 | tf_op jit(solution)/shard_map/ppermute | solution.py:172
  33.4 0.0 collective-permute-done.10.refs_2_
  33.4 0.2 collective-permute-start.8
  33.6 0.0 all-to-all-done
  33.6 2.6 %grow_inner.1.refs_3_ = bf16[1,64,128,256]{3,2,1,0:T(8,128)(2,1)} custom-call(bf16[16,64,256]{2,1,0:T(8,128)(2,1)} %bitcast.4.refs_0_), custom_call_target="tpu_custom_call" | custom-call | bytes 2097152 | tf_op jit(solution)/shard_map/grow_inner/pallas_call | solution.py:151
  36.2 1.1 %grow_first.1.refs_5_ = bf16[1,64,128,256]{3,2,1,0:T(8,128)(2,1)} custom-call(bf16[2,64,256]{2,1,0:T(8,128)(2,1)S(1)} %get-tuple-element.42.refs_0_, bf16[2,64,256]{2,1,0:T(8,128)(2,1)S(1)} %collective-permute-done.9.refs_1_, bf16[2,64,256]{2,1,0:T(8,128)(2,1)S(1)} %collective-permute-done.10.refs_2_, ...), custom_call_target="tpu_custom_call", output_to_operand_aliasing={{}: (3, {})} | custom-call | bytes 786432 | tf_op jit(solution)/shard_map/grow_first/pallas_call | solution.py:151
  37.3 2.6 %collective-permute-done.4.refs_0_ = bf16[2,64,256]{2,1,0:T(8,128)(2,1)S(1)} collective-permute-done((bf16[2,64,256]{2,1,0:T(8,128)(2,1)S(1)}, bf16[2,64,256]{2,1,0:T(8,128)(2,1)S(1)}, u32[]{:S(2)}, u32[]{:S(2)}) %collective-permute-start.4) | collective-permute-done | bytes 65568 | tf_op jit(solution)/shard_map/ppermute | solution.py:172
  39.9 0.5 %collective-permute-done.5.refs_1_ = bf16[2,64,256]{2,1,0:T(8,128)(2,1)S(1)} collective-permute-done((bf16[2,64,256]{2,1,0:T(8,128)(2,1)S(1)}, bf16[2,64,256]{2,1,0:T(8,128)(2,1)S(1)}, u32[]{:S(2)}, u32[]{:S(2)}) %collective-permute-start.5) | collective-permute-done | bytes 65568 | tf_op jit(solution)/shard_map/ppermute | solution.py:172
  40.4 0.0 collective-permute-done.6.refs_2_
  40.4 0.0 collective-permute-done.7.refs_3_
  40.4 0.0 collective-permute-done.8.refs_4_
  40.4 1.3 %grow_last.1 = bf16[1,64,128,256]{3,2,1,0:T(8,128)(2,1)} custom-call(bf16[2,64,256]{2,1,0:T(8,128)(2,1)S(1)} %collective-permute-done.4.refs_0_, bf16[2,64,256]{2,1,0:T(8,128)(2,1)S(1)} %collective-permute-done.5.refs_1_, bf16[2,64,256]{2,1,0:T(8,128)(2,1)S(1)} %collective-permute-done.6.refs_2_, ...), custom_call_target="tpu_custom_call", output_to_operand_aliasing={{}: (5, {})} | custom-call | bytes 1310720 | tf_op jit(solution)/shard_map/grow_last/pallas_call | solution.py:151
  (2 shorter events, 0.0 us)
Async XLA Ops:
  1.1 7.6 %collective-permute-start = (bf16[2,4,64,256]{3,2,1,0:T(8,128)(2,1)S(1)}, bf16[2,4,64,256]{3,2,1,0:T(8,128)(2,1)S(1)}, u32[]{:S(2)}, u32[]{:S(2)}) collective-permute-start(bf16[2,4,64,256]{3,2,1,0:T(8,128)(2,1)S(1)} %get-tuple-element.26), channel_id=1, source_target_pairs={{0,8},{8,16},{16,24},{24,0},{1,9},{9,17},{17,25},{25,1},{2,10},{10... | collective-permute-start | bytes 786440 | tf_op jit(solution)/shard_map/ppermute | solution.py:177
  1.6 14.5 %collective-permute-start.1 = (bf16[8,64,256]{2,1,0:T(8,128)(2,1)S(1)}, bf16[8,64,256]{2,1,0:T(8,128)(2,1)S(1)}, u32[]{:S(2)}, u32[]{:S(2)}) collective-permute-start(bf16[8,64,256]{2,1,0:T(8,128)(2,1)S(1)} %get-tuple-element.27), channel_id=1, source_target_pairs={{0,1},{1,0},{2,3},{3,2},{4,5},{5,4},{6,7},{7,6},{8,9},{9,8},{10,11... | collective-permute-start | bytes 786440 | tf_op jit(solution)/shard_map/ppermute | solution.py:172
  4.2 11.9 %collective-permute-start.2 = (bf16[8,64,256]{2,1,0:T(8,128)(2,1)S(1)}, bf16[8,64,256]{2,1,0:T(8,128)(2,1)S(1)}, u32[]{:S(2)}, u32[]{:S(2)}) collective-permute-start(bf16[8,64,256]{2,1,0:T(8,128)(2,1)S(1)} %get-tuple-element.28), channel_id=1, source_target_pairs={{0,8},{1,2},{2,1},{3,4},{4,3},{5,6},{6,5},{7,15},{8,0},{9,10},{10,... | collective-permute-start | bytes 786440 | tf_op jit(solution)/shard_map/ppermute | solution.py:187
  10.7 22.9 %all-to-all-start = ((bf16[8,2,64,256]{3,2,1,0:T(8,128)(2,1)}), bf16[8,2,64,256]{3,2,1,0:T(8,128)(2,1)}, u32[]{:S(2)}, u32[]{:S(2)}) async-start(bf16[8,2,64,256]{3,2,1,0:T(8,128)(2,1)} %inner_mix.1), calls=%async_computation | async-start | bytes 1048576 | tf_op jit(solution)/shard_map/all_to_all | solution.py:241
  16.2 4.4 %collective-permute-start.3 = (bf16[2,2,64,256]{3,2,1,0:T(8,128)(2,1)S(1)}, bf16[2,2,64,256]{3,2,1,0:T(8,128)(2,1)S(1)}, u32[]{:S(2)}, u32[]{:S(2)}) collective-permute-start(bf16[2,2,64,256]{3,2,1,0:T(8,128)(2,1)S(1)} %pad_maximum_fusion), channel_id=1, source_target_pairs={{0,8},{8,16},{16,24},{24,0},{1,9},{9,17},{17,25},{25,1},{2,10},{10... | collective-permute-start | bytes 393224 | tf_op jit(solution)/shard_map/ppermute | solution.py:177
  21.7 10.6 %collective-permute-start.9 = (bf16[2,64,256]{2,1,0:T(8,128)(2,1)S(1)}, bf16[2,64,256]{2,1,0:T(8,128)(2,1)S(1)}, u32[]{:S(2)}, u32[]{:S(2)}) collective-permute-start(bf16[2,64,256]{2,1,0:T(8,128)(2,1)S(1)} %get-tuple-element.43), channel_id=1, source_target_pairs={{0,2},{1,3},{2,0},{3,1},{4,6},{5,7},{6,4},{7,5},{8,10},{9,11},{10,... | collective-permute-start | bytes 196616 | tf_op jit(solution)/shard_map/ppermute | solution.py:172
  24.2 9.2 %collective-permute-start.10 = (bf16[2,64,256]{2,1,0:T(8,128)(2,1)S(1)}, bf16[2,64,256]{2,1,0:T(8,128)(2,1)S(1)}, u32[]{:S(2)}, u32[]{:S(2)}) collective-permute-start(bf16[2,64,256]{2,1,0:T(8,128)(2,1)S(1)} %get-tuple-element.44), channel_id=1, source_target_pairs={{0,3},{1,2},{2,1},{3,0},{4,7},{5,6},{6,5},{7,4},{8,11},{9,10},{10,... | collective-permute-start | bytes 196616 | tf_op jit(solution)/shard_map/ppermute | solution.py:172
  25.6 14.4 %collective-permute-start.4 = (bf16[2,64,256]{2,1,0:T(8,128)(2,1)S(1)}, bf16[2,64,256]{2,1,0:T(8,128)(2,1)S(1)}, u32[]{:S(2)}, u32[]{:S(2)}) collective-permute-start(bf16[2,64,256]{2,1,0:T(8,128)(2,1)S(1)} %get-tuple-element.37), channel_id=1, source_target_pairs={{0,5},{1,4},{2,7},{3,6},{4,1},{5,0},{6,3},{7,2},{8,13},{9,12},{10,... | collective-permute-start | bytes 196616 | tf_op jit(solution)/shard_map/ppermute | solution.py:172
  28.1 12.3 %collective-permute-start.5 = (bf16[2,64,256]{2,1,0:T(8,128)(2,1)S(1)}, bf16[2,64,256]{2,1,0:T(8,128)(2,1)S(1)}, u32[]{:S(2)}, u32[]{:S(2)}) collective-permute-start(bf16[2,64,256]{2,1,0:T(8,128)(2,1)S(1)} %get-tuple-element.38), channel_id=1, source_target_pairs={{0,4},{1,5},{2,6},{3,7},{4,0},{5,1},{6,2},{7,3},{8,12},{9,13},{10,... | collective-permute-start | bytes 196616 | tf_op jit(solution)/shard_map/ppermute | solution.py:172
  28.1 12.3 %collective-permute-start.6 = (bf16[2,64,256]{2,1,0:T(8,128)(2,1)S(1)}, bf16[2,64,256]{2,1,0:T(8,128)(2,1)S(1)}, u32[]{:S(2)}, u32[]{:S(2)}) collective-permute-start(bf16[2,64,256]{2,1,0:T(8,128)(2,1)S(1)} %get-tuple-element.39), channel_id=1, source_target_pairs={{0,7},{1,6},{2,5},{3,4},{4,3},{5,2},{6,1},{7,0},{8,15},{9,14},{10,... | collective-permute-start | bytes 196616 | tf_op jit(solution)/shard_map/ppermute | solution.py:172
  32.3 8.1 %collective-permute-start.7 = (bf16[2,64,256]{2,1,0:T(8,128)(2,1)S(1)}, bf16[2,64,256]{2,1,0:T(8,128)(2,1)S(1)}, u32[]{:S(2)}, u32[]{:S(2)}) collective-permute-start(bf16[2,64,256]{2,1,0:T(8,128)(2,1)S(1)} %get-tuple-element.40), channel_id=1, source_target_pairs={{0,6},{1,7},{2,4},{3,5},{4,2},{5,3},{6,0},{7,1},{8,14},{9,15},{10,... | collective-permute-start | bytes 196616 | tf_op jit(solution)/shard_map/ppermute | solution.py:172
  33.4 7.0 %collective-permute-start.8 = (bf16[2,64,256]{2,1,0:T(8,128)(2,1)S(1)}, bf16[2,64,256]{2,1,0:T(8,128)(2,1)S(1)}, u32[]{:S(2)}, u32[]{:S(2)}) collective-permute-start(bf16[2,64,256]{2,1,0:T(8,128)(2,1)S(1)} %get-tuple-element.41), channel_id=1, source_target_pairs={{0,1},{1,0},{2,3},{3,2},{4,5},{5,4},{6,7},{7,6},{8,9},{9,8},{10,11... | collective-permute-start | bytes 196616 | tf_op jit(solution)/shard_map/ppermute | solution.py:172

commit v6 on v5

--- a/solution.py
+++ b/solution.py
@@ -36,11 +36,6 @@
     near_row, far_row = (rows - 1) * (1 - odd), (rows - 1) * odd
     pairs = [(latent.at[:, near_row], near), (latent.at[:, far_row], far), (latent.at[pl.ds(frames - 2, 2)], last)]
     copy_all(pairs, sems)
-
-
-def load_kernel(*refs):
-    m = len(refs) // 2
-    copy_all(list(zip(refs[:m], refs[m : 2 * m])), refs[-1])
 
 
 def activate(taps, order, weight_ref, bias):
@@ -67,9 +62,18 @@
     return (own.astype(jnp.float32) + total.reshape(frames, cols, chans) + bias).astype(BF16)
 
 
-def inner_kernel(latent, sw, sb, hidden):
+def inner_kernel(*refs):
+    args, (hidden, *loaded), sems = refs[:5], refs[5:11], refs[11]
+    copies = [pltpu.make_async_copy(a, b, sems.at[i]) for i, (a, b) in enumerate(zip(args, loaded))]
+    for copy in copies:
+        copy.start()
+    latent, sw, sb = loaded[:3]
+    for copy in copies[:3]:
+        copy.wait()
     for r in range(1, latent.shape[1] - 1):
         hidden[r - 1] = activate([latent[:, r + i] for i in (-1, 0, 1)], (0, 1, 2), sw, sb[...])
+    for copy in copies[3:]:
+        copy.wait()
 
 
 def inner_mix_kernel(latent, prev, hidden, sw, sb, tw, tb, out):
@@ -208,26 +212,16 @@
     near = swap(near, 1)
     far = beside(far)
     prev = ahead(last)
-    latent, *params = pl.pallas_call(
-        load_kernel,
-        out_shape=[jax.ShapeDtypeStruct(a.shape, a.dtype) for a in args],
+    hidden, latent, *params = pl.pallas_call(
+        inner_kernel,
+        out_shape=[bf16(rows - 2, frames, cols, chans)] + [jax.ShapeDtypeStruct(a.shape, a.dtype) for a in args],
         in_specs=[HBM] * 5,
-        out_specs=[VMEM] * 5,
+        out_specs=[VMEM] * 6,
         scratch_shapes=[pltpu.SemaphoreType.DMA((5,))],
-        compiler_params=PARAMS,
-        cost_estimate=pl.CostEstimate(flops=0, transcendentals=0, bytes_accessed=5 * MIB),
-        name="load",
-    )(*args)
-
-    hidden = pl.pallas_call(
-        inner_kernel,
-        out_shape=bf16(rows - 2, frames, cols, chans),
-        in_specs=[VMEM] * 3,
-        out_specs=VMEM,
         compiler_params=PARAMS,
         cost_estimate=cost(frames * (rows - 2) * cols, 9, chans),
         name="inner",
-    )(latent, *params[:2])
+    )(*args)
     inner = pl.pallas_call(
         inner_mix_kernel,
         out_shape=bf16(frames, rows - 2, cols, chans),

time: 42.1 us -> 42.1 us (level)
    pallas_call x2 -> x1, Pallas kernels: 3.24 us -> 3.15 us  [body(): pl.pallas_call(inner_kernel, out_shape=[bf16(rows - 2, frames, cols, chan...]
where the time goes in v6:
time: 42.1 us; the launch traced here: 41.8 us
  starting transfers between devices  22.4 us (53%)
  Pallas kernels  13.8 us (33%)
  waiting for transfers between devices  5.49 us (13%)
    ppermute x8, starting transfers between devices, swap(): lax.ppermute(block, 'space', [(i, i ^ k) for i in range(lax.axis_size('sp...  14.4 us
    all_to_all x1, starting transfers between devices, body(): lax.all_to_all(inner, 'space', split_axis=0, concat_axis=1, tiled=True)[0]  5.59 us
    pallas_call x3, Pallas kernels, grow(): pl.pallas_call(lambda *refs: grow_kernel(plan, refs[:m], *refs[m + len(ex...  4.98 us
    ppermute x8, waiting for transfers between devices, swap(): lax.ppermute(block, 'space', [(i, i ^ k) for i in range(lax.axis_size('sp...  3.17 us
    pallas_call x1, Pallas kernels, body(): pl.pallas_call(inner_kernel, out_shape=[bf16(rows - 2, frames, cols, chan...  3.15 us
    ppermute x2, waiting for transfers between devices, ahead(): return lax.ppermute(block, 'tm', [(t, (t + 1) % n) for t in range(n)])  2.32 us
    pallas_call x1, Pallas kernels, body(): pl.pallas_call(inner_mix_kernel, out_shape=bf16(frames, rows - 2, cols, c...  1.9 us
    pallas_call x1, Pallas kernels, body(): pl.pallas_call(edge_kernel, out_shape=[bf16(2, frames, cols, chans), bf16...  1.59 us
  transfers between devices with their start and end apart: 12, of which 3 were waited for; matrix products, arithmetic and copies ran while one was open for 0% of the time, Pallas kernels for 27%

profile of v6, /device:TPU:0, one launch (start us, length us, event | category | flops | bytes accessed | tf_op | source)
XLA Modules:
  0.0 41.8 jit_solution(10580263236490610334)
XLA Ops:
  0.0 1.1 %border.1 = (bf16[8,64,256]{2,1,0:T(8,128)(2,1)S(1)}, bf16[8,64,256]{2,1,0:T(8,128)(2,1)S(1)}, bf16[2,4,64,256]{3,2,1,0:T(8,128)(2,1)S(1)}) custom-call(bf16[8,4,64,256]{3,2,1,0:T(8,128)(2,1)} %latent.1), custom_call_target="tpu_custom_call" | custom-call | tf_op jit(solution)/shard_map/border/pallas_call | solution.py:203
  1.1 0.5 %collective-permute-start = (bf16[2,4,64,256]{3,2,1,0:T(8,128)(2,1)S(1)}, bf16[2,4,64,256]{3,2,1,0:T(8,128)(2,1)S(1)}, u32[]{:S(2)}, u32[]{:S(2)}) collective-permute-start(bf16[2,4,64,256]{3,2,1,0:T(8,128)(2,1)S(1)} %get-tuple-element.27), channel_id=1, source_target_pairs={{0,8},{8,16},{16,24},{24,0},{1,9},{9,17},{17,25},{25,1},{2,10},{10... | collective-permute-start | bytes 786440 | tf_op jit(solution)/shard_map/ppermute | solution.py:181
  1.6 2.6 %collective-permute-start.1 = (bf16[8,64,256]{2,1,0:T(8,128)(2,1)S(1)}, bf16[8,64,256]{2,1,0:T(8,128)(2,1)S(1)}, u32[]{:S(2)}, u32[]{:S(2)}) collective-permute-start(bf16[8,64,256]{2,1,0:T(8,128)(2,1)S(1)} %get-tuple-element.28), channel_id=1, source_target_pairs={{0,1},{1,0},{2,3},{3,2},{4,5},{5,4},{6,7},{7,6},{8,9},{9,8},{10,11... | collective-permute-start | bytes 786440 | tf_op jit(solution)/shard_map/ppermute | solution.py:176
  4.2 1.3 %collective-permute-start.2 = (bf16[8,64,256]{2,1,0:T(8,128)(2,1)S(1)}, bf16[8,64,256]{2,1,0:T(8,128)(2,1)S(1)}, u32[]{:S(2)}, u32[]{:S(2)}) collective-permute-start(bf16[8,64,256]{2,1,0:T(8,128)(2,1)S(1)} %get-tuple-element.29), channel_id=1, source_target_pairs={{0,8},{1,2},{2,1},{3,4},{4,3},{5,6},{6,5},{7,15},{8,0},{9,10},{10,... | collective-permute-start | bytes 786440 | tf_op jit(solution)/shard_map/ppermute | solution.py:191
  5.5 3.1 %inner.1 = (bf16[2,8,64,256]{3,2,1,0:T(8,128)(2,1)S(1)}, bf16[8,4,64,256]{3,2,1,0:T(8,128)(2,1)S(1)}, bf16[3,3,256,256]{3,2,1,0:T(8,128)(2,1)S(1)}, f32[1,256]{1...) custom-call(bf16[8,4,64,256]{3,2,1,0:T(8,128)(2,1)} %latent.1, bf16[3,3,256,256]{3,2,1,0:T(8,128)(2,1)} %refs_1_.1, ...), custom_call_target="tpu_custom_call" | custom-call | flops 1207959552 | bytes 2097152 | tf_op jit(solution)/shard_map/inner/pallas_call | solution.py:215
  8.6 0.0 collective-permute-done.prev.refs_1_
  8.7 1.9 %inner_mix.1 = bf16[8,2,64,256]{3,2,1,0:T(8,128)(2,1)} custom-call(bf16[8,4,64,256]{3,2,1,0:T(8,128)(2,1)S(1)} %get-tuple-element.26.latent.refs_0_, bf16[2,4,64,256]{3,2,1,0:T(8,128)(2,1)S(1)} %collective-permute-done.prev.refs_1_, bf16[2,8,64,256]{3,2,1,0:T(8,128)(2,1)S(1)} %get-tuple-element.30.hidden, ...), custom_call_target="tpu_custom_call" | custom-call | flops 805306368 | bytes 2097152 | tf_op jit(solution)/shard_map/inner_mix/pallas_call | solution.py:225
  10.6 5.6 %all-to-all-start = ((bf16[8,2,64,256]{3,2,1,0:T(8,128)(2,1)}), bf16[8,2,64,256]{3,2,1,0:T(8,128)(2,1)}, u32[]{:S(2)}, u32[]{:S(2)}) async-start(bf16[8,2,64,256]{3,2,1,0:T(8,128)(2,1)} %inner_mix.1), calls=%async_computation | async-start | bytes 1048576 | tf_op jit(solution)/shard_map/all_to_all | solution.py:235
  16.1 0.0 collective-permute-done.1.near
  16.2 0.0 collective-permute-done.2.far
  16.2 0.5 %collective-permute-start.3 = (bf16[2,2,64,256]{3,2,1,0:T(8,128)(2,1)S(1)}, bf16[2,2,64,256]{3,2,1,0:T(8,128)(2,1)S(1)}, u32[]{:S(2)}, u32[]{:S(2)}) collective-permute-start(bf16[2,2,64,256]{3,2,1,0:T(8,128)(2,1)S(1)} %pad_maximum_fusion), channel_id=1, source_target_pairs={{0,8},{8,16},{16,24},{24,0},{1,9},{9,17},{17,25},{25,1},{2,10},{10... | collective-permute-start | bytes 393224 | tf_op jit(solution)/shard_map/ppermute | solution.py:181
  16.7 1.6 %edge.1 = (bf16[2,8,64,256]{3,2,1,0:T(8,128)(2,1)S(1)}, bf16[3,256,256]{2,1,0:T(8,128)(2,1)S(1)}) custom-call(bf16[8,4,64,256]{3,2,1,0:T(8,128)(2,1)S(1)} %get-tuple-element.26.latent.refs_0_, bf16[8,64,256]{2,1,0:T(8,128)(2,1)S(1)} %collective-permute-done.1.near, bf16[8,64,256]{2,1,0:T(8,128)(2,1)S(1)} %collective-permute-done.2.far, ...), custom_call_target="tpu_custom_call" | custom-call | flops 1207959552 | bytes 2097152 | tf_op jit(solution)/shard_map/edge/pallas_call | solution.py:239
  18.3 2.3 %collective-permute-done.3.refs_2_ = bf16[2,2,64,256]{3,2,1,0:T(8,128)(2,1)S(1)} collective-permute-done((bf16[2,2,64,256]{3,2,1,0:T(8,128)(2,1)S(1)}, bf16[2,2,64,256]{3,2,1,0:T(8,128)(2,1)S(1)}, u32[]{:S(2)}, u32[]{:S(2)}) %collective-permute-start.3) | collective-permute-done | bytes 131104 | tf_op jit(solution)/shard_map/ppermute | solution.py:181
  20.6 1.0 %join.1 = (bf16[2,64,256]{2,1,0:T(8,128)(2,1)S(1)}, bf16[2,64,256]{2,1,0:T(8,128)(2,1)S(1)}, bf16[2,64,256]{2,1,0:T(8,128)(2,1)S(1)}, bf16[2,64,256]{2,1,0:T(8,1...) custom-call(bf16[8,4,64,256]{3,2,1,0:T(8,128)(2,1)S(1)} %get-tuple-e, ...), custom_call_target="tpu_custom_call" | custom-call | flops 805306368 | bytes 2097152 | tf_op jit(solution)/shard_map/join/pallas_call | solution.py:249
  21.7 2.5 %collective-permute-start.9 = (bf16[2,64,256]{2,1,0:T(8,128)(2,1)S(1)}, bf16[2,64,256]{2,1,0:T(8,128)(2,1)S(1)}, u32[]{:S(2)}, u32[]{:S(2)}) collective-permute-start(bf16[2,64,256]{2,1,0:T(8,128)(2,1)S(1)} %get-tuple-element.45), channel_id=1, source_target_pairs={{0,2},{1,3},{2,0},{3,1},{4,6},{5,7},{6,4},{7,5},{8,10},{9,11},{10,... | collective-permute-start | bytes 196616 | tf_op jit(solution)/shard_map/ppermute | solution.py:176
  24.2 1.4 %collective-permute-start.10 = (bf16[2,64,256]{2,1,0:T(8,128)(2,1)S(1)}, bf16[2,64,256]{2,1,0:T(8,128)(2,1)S(1)}, u32[]{:S(2)}, u32[]{:S(2)}) collective-permute-start(bf16[2,64,256]{2,1,0:T(8,128)(2,1)S(1)} %get-tuple-element.46), channel_id=1, source_target_pairs={{0,3},{1,2},{2,1},{3,0},{4,7},{5,6},{6,5},{7,4},{8,11},{9,10},{10,... | collective-permute-start | bytes 196616 | tf_op jit(solution)/shard_map/ppermute | solution.py:176
  25.6 2.6 %collective-permute-start.4 = (bf16[2,64,256]{2,1,0:T(8,128)(2,1)S(1)}, bf16[2,64,256]{2,1,0:T(8,128)(2,1)S(1)}, u32[]{:S(2)}, u32[]{:S(2)}) collective-permute-start(bf16[2,64,256]{2,1,0:T(8,128)(2,1)S(1)} %get-tuple-element.39), channel_id=1, source_target_pairs={{0,5},{1,4},{2,7},{3,6},{4,1},{5,0},{6,3},{7,2},{8,13},{9,12},{10,... | collective-permute-start | bytes 196616 | tf_op jit(solution)/shard_map/ppermute | solution.py:176
  28.1 0.0 collective-permute-start.5
  28.1 4.2 %collective-permute-start.6 = (bf16[2,64,256]{2,1,0:T(8,128)(2,1)S(1)}, bf16[2,64,256]{2,1,0:T(8,128)(2,1)S(1)}, u32[]{:S(2)}, u32[]{:S(2)}) collective-permute-start(bf16[2,64,256]{2,1,0:T(8,128)(2,1)S(1)} %get-tuple-element.41), channel_id=1, source_target_pairs={{0,7},{1,6},{2,5},{3,4},{4,3},{5,2},{6,1},{7,0},{8,15},{9,14},{10,... | collective-permute-start | bytes 196616 | tf_op jit(solution)/shard_map/ppermute | solution.py:176
  32.3 0.0 collective-permute-done.9.refs_1_
  32.3 1.1 %collective-permute-start.7 = (bf16[2,64,256]{2,1,0:T(8,128)(2,1)S(1)}, bf16[2,64,256]{2,1,0:T(8,128)(2,1)S(1)}, u32[]{:S(2)}, u32[]{:S(2)}) collective-permute-start(bf16[2,64,256]{2,1,0:T(8,128)(2,1)S(1)} %get-tuple-element.42), channel_id=1, source_target_pairs={{0,6},{1,7},{2,4},{3,5},{4,2},{5,3},{6,0},{7,1},{8,14},{9,15},{10,... | collective-permute-start | bytes 196616 | tf_op jit(solution)/shard_map/ppermute | solution.py:176
  33.5 0.0 collective-permute-done.10.refs_2_
  33.5 0.1 collective-permute-start.8
  33.6 0.0 all-to-all-done
  33.6 2.6 %grow_inner.1.refs_3_ = bf16[1,64,128,256]{3,2,1,0:T(8,128)(2,1)} custom-call(bf16[16,64,256]{2,1,0:T(8,128)(2,1)} %bitcast.4.refs_0_), custom_call_target="tpu_custom_call" | custom-call | bytes 2097152 | tf_op jit(solution)/shard_map/grow_inner/pallas_call | solution.py:155
  36.2 1.1 %grow_first.1.refs_5_ = bf16[1,64,128,256]{3,2,1,0:T(8,128)(2,1)} custom-call(bf16[2,64,256]{2,1,0:T(8,128)(2,1)S(1)} %get-tuple-element.44.refs_0_, bf16[2,64,256]{2,1,0:T(8,128)(2,1)S(1)} %collective-permute-done.9.refs_1_, bf16[2,64,256]{2,1,0:T(8,128)(2,1)S(1)} %collective-permute-done.10.refs_2_, ...), custom_call_target="tpu_custom_call", output_to_operand_aliasing={{}: (3, {})} | custom-call | bytes 786432 | tf_op jit(solution)/shard_map/grow_first/pallas_call | solution.py:155
  37.3 2.6 %collective-permute-done.4.refs_0_ = bf16[2,64,256]{2,1,0:T(8,128)(2,1)S(1)} collective-permute-done((bf16[2,64,256]{2,1,0:T(8,128)(2,1)S(1)}, bf16[2,64,256]{2,1,0:T(8,128)(2,1)S(1)}, u32[]{:S(2)}, u32[]{:S(2)}) %collective-permute-start.4) | collective-permute-done | bytes 65568 | tf_op jit(solution)/shard_map/ppermute | solution.py:176
  39.9 0.5 %collective-permute-done.5.refs_1_ = bf16[2,64,256]{2,1,0:T(8,128)(2,1)S(1)} collective-permute-done((bf16[2,64,256]{2,1,0:T(8,128)(2,1)S(1)}, bf16[2,64,256]{2,1,0:T(8,128)(2,1)S(1)}, u32[]{:S(2)}, u32[]{:S(2)}) %collective-permute-start.5) | collective-permute-done | bytes 65568 | tf_op jit(solution)/shard_map/ppermute | solution.py:176
  40.4 0.0 collective-permute-done.6.refs_2_
  40.4 0.0 collective-permute-done.7.refs_3_
  40.4 0.0 collective-permute-done.8.refs_4_
  40.4 1.3 %grow_last.1 = bf16[1,64,128,256]{3,2,1,0:T(8,128)(2,1)} custom-call(bf16[2,64,256]{2,1,0:T(8,128)(2,1)S(1)} %collective-permute-done.4.refs_0_, bf16[2,64,256]{2,1,0:T(8,128)(2,1)S(1)} %collective-permute-done.5.refs_1_, bf16[2,64,256]{2,1,0:T(8,128)(2,1)S(1)} %collective-permute-done.6.refs_2_, ...), custom_call_target="tpu_custom_call", output_to_operand_aliasing={{}: (5, {})} | custom-call | bytes 1310720 | tf_op jit(solution)/shard_map/grow_last/pallas_call | solution.py:155
  (2 shorter events, 0.0 us)
Async XLA Ops:
  1.1 7.5 %collective-permute-start = (bf16[2,4,64,256]{3,2,1,0:T(8,128)(2,1)S(1)}, bf16[2,4,64,256]{3,2,1,0:T(8,128)(2,1)S(1)}, u32[]{:S(2)}, u32[]{:S(2)}) collective-permute-start(bf16[2,4,64,256]{3,2,1,0:T(8,128)(2,1)S(1)} %get-tuple-element.27), channel_id=1, source_target_pairs={{0,8},{8,16},{16,24},{24,0},{1,9},{9,17},{17,25},{25,1},{2,10},{10... | collective-permute-start | bytes 786440 | tf_op jit(solution)/shard_map/ppermute | solution.py:181
  1.6 14.5 %collective-permute-start.1 = (bf16[8,64,256]{2,1,0:T(8,128)(2,1)S(1)}, bf16[8,64,256]{2,1,0:T(8,128)(2,1)S(1)}, u32[]{:S(2)}, u32[]{:S(2)}) collective-permute-start(bf16[8,64,256]{2,1,0:T(8,128)(2,1)S(1)} %get-tuple-element.28), channel_id=1, source_target_pairs={{0,1},{1,0},{2,3},{3,2},{4,5},{5,4},{6,7},{7,6},{8,9},{9,8},{10,11... | collective-permute-start | bytes 786440 | tf_op jit(solution)/shard_map/ppermute | solution.py:176
  4.2 11.9 %collective-permute-start.2 = (bf16[8,64,256]{2,1,0:T(8,128)(2,1)S(1)}, bf16[8,64,256]{2,1,0:T(8,128)(2,1)S(1)}, u32[]{:S(2)}, u32[]{:S(2)}) collective-permute-start(bf16[8,64,256]{2,1,0:T(8,128)(2,1)S(1)} %get-tuple-element.29), channel_id=1, source_target_pairs={{0,8},{1,2},{2,1},{3,4},{4,3},{5,6},{6,5},{7,15},{8,0},{9,10},{10,... | collective-permute-start | bytes 786440 | tf_op jit(solution)/shard_map/ppermute | solution.py:191
  10.6 23.0 %all-to-all-start = ((bf16[8,2,64,256]{3,2,1,0:T(8,128)(2,1)}), bf16[8,2,64,256]{3,2,1,0:T(8,128)(2,1)}, u32[]{:S(2)}, u32[]{:S(2)}) async-start(bf16[8,2,64,256]{3,2,1,0:T(8,128)(2,1)} %inner_mix.1), calls=%async_computation | async-start | bytes 1048576 | tf_op jit(solution)/shard_map/all_to_all | solution.py:235
  16.2 4.4 %collective-permute-start.3 = (bf16[2,2,64,256]{3,2,1,0:T(8,128)(2,1)S(1)}, bf16[2,2,64,256]{3,2,1,0:T(8,128)(2,1)S(1)}, u32[]{:S(2)}, u32[]{:S(2)}) collective-permute-start(bf16[2,2,64,256]{3,2,1,0:T(8,128)(2,1)S(1)} %pad_maximum_fusion), channel_id=1, source_target_pairs={{0,8},{8,16},{16,24},{24,0},{1,9},{9,17},{17,25},{25,1},{2,10},{10... | collective-permute-start | bytes 393224 | tf_op jit(solution)/shard_map/ppermute | solution.py:181
  21.7 10.6 %collective-permute-start.9 = (bf16[2,64,256]{2,1,0:T(8,128)(2,1)S(1)}, bf16[2,64,256]{2,1,0:T(8,128)(2,1)S(1)}, u32[]{:S(2)}, u32[]{:S(2)}) collective-permute-start(bf16[2,64,256]{2,1,0:T(8,128)(2,1)S(1)} %get-tuple-element.45), channel_id=1, source_target_pairs={{0,2},{1,3},{2,0},{3,1},{4,6},{5,7},{6,4},{7,5},{8,10},{9,11},{10,... | collective-permute-start | bytes 196616 | tf_op jit(solution)/shard_map/ppermute | solution.py:176
  24.2 9.3 %collective-permute-start.10 = (bf16[2,64,256]{2,1,0:T(8,128)(2,1)S(1)}, bf16[2,64,256]{2,1,0:T(8,128)(2,1)S(1)}, u32[]{:S(2)}, u32[]{:S(2)}) collective-permute-start(bf16[2,64,256]{2,1,0:T(8,128)(2,1)S(1)} %get-tuple-element.46), channel_id=1, source_target_pairs={{0,3},{1,2},{2,1},{3,0},{4,7},{5,6},{6,5},{7,4},{8,11},{9,10},{10,... | collective-permute-start | bytes 196616 | tf_op jit(solution)/shard_map/ppermute | solution.py:176
  25.6 14.4 %collective-permute-start.4 = (bf16[2,64,256]{2,1,0:T(8,128)(2,1)S(1)}, bf16[2,64,256]{2,1,0:T(8,128)(2,1)S(1)}, u32[]{:S(2)}, u32[]{:S(2)}) collective-permute-start(bf16[2,64,256]{2,1,0:T(8,128)(2,1)S(1)} %get-tuple-element.39), channel_id=1, source_target_pairs={{0,5},{1,4},{2,7},{3,6},{4,1},{5,0},{6,3},{7,2},{8,13},{9,12},{10,... | collective-permute-start | bytes 196616 | tf_op jit(solution)/shard_map/ppermute | solution.py:176
  28.1 12.3 %collective-permute-start.5 = (bf16[2,64,256]{2,1,0:T(8,128)(2,1)S(1)}, bf16[2,64,256]{2,1,0:T(8,128)(2,1)S(1)}, u32[]{:S(2)}, u32[]{:S(2)}) collective-permute-start(bf16[2,64,256]{2,1,0:T(8,128)(2,1)S(1)} %get-tuple-element.40), channel_id=1, source_target_pairs={{0,4},{1,5},{2,6},{3,7},{4,0},{5,1},{6,2},{7,3},{8,12},{9,13},{10,... | collective-permute-start | bytes 196616 | tf_op jit(solution)/shard_map/ppermute | solution.py:176
  28.1 12.3 %collective-permute-start.6 = (bf16[2,64,256]{2,1,0:T(8,128)(2,1)S(1)}, bf16[2,64,256]{2,1,0:T(8,128)(2,1)S(1)}, u32[]{:S(2)}, u32[]{:S(2)}) collective-permute-start(bf16[2,64,256]{2,1,0:T(8,128)(2,1)S(1)} %get-tuple-element.41), channel_id=1, source_target_pairs={{0,7},{1,6},{2,5},{3,4},{4,3},{5,2},{6,1},{7,0},{8,15},{9,14},{10,... | collective-permute-start | bytes 196616 | tf_op jit(solution)/shard_map/ppermute | solution.py:176
  32.3 8.1 %collective-permute-start.7 = (bf16[2,64,256]{2,1,0:T(8,128)(2,1)S(1)}, bf16[2,64,256]{2,1,0:T(8,128)(2,1)S(1)}, u32[]{:S(2)}, u32[]{:S(2)}) collective-permute-start(bf16[2,64,256]{2,1,0:T(8,128)(2,1)S(1)} %get-tuple-element.42), channel_id=1, source_target_pairs={{0,6},{1,7},{2,4},{3,5},{4,2},{5,3},{6,0},{7,1},{8,14},{9,15},{10,... | collective-permute-start | bytes 196616 | tf_op jit(solution)/shard_map/ppermute | solution.py:176
  33.5 7.0 %collective-permute-start.8 = (bf16[2,64,256]{2,1,0:T(8,128)(2,1)S(1)}, bf16[2,64,256]{2,1,0:T(8,128)(2,1)S(1)}, u32[]{:S(2)}, u32[]{:S(2)}) collective-permute-start(bf16[2,64,256]{2,1,0:T(8,128)(2,1)S(1)} %get-tuple-element.43), channel_id=1, source_target_pairs={{0,1},{1,0},{2,3},{3,2},{4,5},{5,4},{6,7},{7,6},{8,9},{9,8},{10,11... | collective-permute-start | bytes 196616 | tf_op jit(solution)/shard_map/ppermute | solution.py:176
